TPU v7x, 32 devices: a whole 2x2x4 slice. The times are simulated.
32 devices in a mesh: dp: 8 (over y, x, core), mp: 4 (over z).
Axes of the slice: x: 2, y: 2, z: 4, core: 2. Of those that a mesh axis runs over, the one named last changes fastest.
Arguments:
- caption_tokens: bfloat16 [784, 16, 768], P('dp'), may hold values from -6 to 6
- image_tokens: bfloat16 [224, 50, 768], P(('dp', 'mp')), may hold values from -6 to 6
- image_attend: bfloat16 [3, 768, 768], replicated, may hold values from -0.21875 to 0.21875
- image_output: bfloat16 [768, 768], replicated, may hold values from -0.4375 to 0.4375
- image_expand: bfloat16 [768, 3072], replicated, may hold values from -0.21875 to 0.21875
- image_reduce: bfloat16 [3072, 768], replicated, may hold values from -0.109375 to 0.109375
- image_gains: float32 [2, 768], replicated, may hold values from 0.1 to 1.9
- caption_attend: bfloat16 [3, 768, 768], P(None, None, 'mp'), may hold values from -0.21875 to 0.21875
- attend_bias: float32 [2, 768], P(None, 'mp'), may hold values from -3 to 3
- caption_output: bfloat16 [768, 768], P('mp'), may hold values from -0.4375 to 0.4375
- output_bias: float32 [768], replicated, may hold values from -1 to 1
- caption_expand: bfloat16 [768, 3072], P(None, 'mp'), may hold values from -0.21875 to 0.21875
- expand_bias: float32 [3072], P('mp'), may hold values from -3 to 3
- caption_reduce: bfloat16 [3072, 768], P('mp'), may hold values from -0.109375 to 0.109375
- reduce_bias: float32 [768], replicated, may hold values from -1 to 1
- norm_gains: float32 [2, 768], replicated, may hold values from 0.1 to 1.9
- norm_shifts: float32 [2, 768], replicated, may hold values from -2 to 2
- log_scale: float32 [1], replicated, may hold values from 3.6 to 4.4
- caption_image: int32 [784], P('dp'), may hold values from 0 to 223, as said below
Outputs:
- contrast_loss: float32 [1], replicated
- gradient_tokens: float32 [784, 16, 768], P('dp')
- gradient_attend: float32 [3, 768, 768], P(None, None, 'mp')
- gradient_attend_bias: float32 [2, 768], P(None, 'mp')
- gradient_output: float32 [768, 768], P('mp')
- gradient_output_bias: float32 [768], replicated
- gradient_expand: float32 [768, 3072], P(None, 'mp')
- gradient_expand_bias: float32 [3072], P('mp')
- gradient_reduce: float32 [3072, 768], P('mp')
- gradient_reduce_bias: float32 [768], replicated
- gradient_gains: float32 [2, 768], replicated
- gradient_shifts: float32 [2, 768], replicated
- gradient_log_scale: float32 [1], replicated
Inputs may be any that keep to these rules, and one draw needn't show every extreme that they name: `caption_image`: every image is named by at least one and at most five captions.
All inputs are finite; a program needn't handle non-finite values.
Results may differ from a plain program's by a relative error of at most 0.014.
Values may be sent and summed in bfloat16 or wider, within the bound.
A program may use at most 128 MiB of HBM per device.

v0:
```python
from functools import partial

import jax
import jax.numpy as jnp
from jax import lax
from jax.sharding import PartitionSpec as P

HEAD_DIM = 64


def merged(array, axis, combine):
    everything = jax.tree.map(lambda part: lax.all_gather(part, axis), array)
    leading = jax.tree.map(lambda part: part[0], everything)

    def step(k, so_far):
        return combine(so_far, jax.tree.map(lambda part: part[k], everything))

    return lax.fori_loop(1, lax.axis_size(axis), step, leading)


def norm_rows(values, gains, shifts):
    centred = values - jnp.mean(values, axis=-1, keepdims=True)
    variance = jnp.mean(centred * centred, axis=-1, keepdims=True)
    return centred * lax.rsqrt(variance + 1e-06) * gains + shifts


def softmax_last(logits):
    highest = jnp.max(logits, axis=-1, keepdims=True)
    expos = jnp.exp(logits - highest)
    return expos / jnp.sum(expos, axis=-1, keepdims=True)


def unit_rows(pooled):
    return pooled * lax.rsqrt(jnp.sum(pooled * pooled, axis=-1, keepdims=True) + 1e-06)


def matmul(left_side, right_side):
    return jnp.dot(left_side, right_side, preferred_element_type=jnp.float32)


def contract_last(left_side, right_side):
    return lax.dot_general(
        left_side, right_side, (((1,), (1,)), ((), ())), preferred_element_type=jnp.float32
    )


def outer_sum(left_side, right_side):
    return lax.dot_general(
        left_side, right_side, (((0,), (0,)), ((), ())), preferred_element_type=jnp.float32
    )


def contract(formula, left_side, right_side):
    return jnp.einsum(formula, left_side, right_side, preferred_element_type=jnp.float32)


def image_block(tokens, image_attend, image_output, image_expand, image_reduce, image_gains):
    group_size, length, model_width = tokens.shape
    heads_count = model_width // HEAD_DIM
    heads_shape = (group_size, length, heads_count, HEAD_DIM)
    flattened = tokens.astype(jnp.float32).reshape(group_size * length, model_width)
    normed = norm_rows(flattened, image_gains[0], 0.0).astype(jnp.bfloat16)
    queries = matmul(normed, image_attend[0]).astype(jnp.bfloat16).reshape(heads_shape)
    keyset = matmul(normed, image_attend[1]).astype(jnp.bfloat16).reshape(heads_shape)
    valueset = matmul(normed, image_attend[2]).astype(jnp.bfloat16).reshape(heads_shape)
    weights = softmax_last(
        contract("bqhd,bkhd->bhqk", queries, keyset) * HEAD_DIM ** (-0.5)
    ).astype(jnp.bfloat16)
    mixture = (
        contract("bhqk,bkhd->bqhd", weights, valueset)
        .astype(jnp.bfloat16)
        .reshape(group_size * length, model_width)
    )
    residual = flattened + matmul(mixture, image_output)
    normed_two = norm_rows(residual, image_gains[1], 0.0).astype(jnp.bfloat16)
    activated = jax.nn.gelu(matmul(normed_two, image_expand), approximate=True).astype(jnp.bfloat16)
    outputs = residual + matmul(activated, image_reduce)
    return unit_rows(jnp.mean(outputs.reshape(group_size, length, model_width), axis=1)).astype(
        jnp.bfloat16
    )


def local(
    caption_tokens,
    image_tokens,
    image_attend,
    image_output,
    image_expand,
    image_reduce,
    image_gains,
    caption_attend,
    attend_bias,
    caption_output,
    output_bias,
    caption_expand,
    expand_bias,
    caption_reduce,
    reduce_bias,
    norm_gains,
    norm_shifts,
    log_scale,
    caption_image,
):
    local_embed = image_block(
        image_tokens, image_attend, image_output, image_expand, image_reduce, image_gains
    )
    group_images = lax.all_gather(local_embed, "mp", axis=0, tiled=True)
    captions, length, model_width = caption_tokens.shape
    row_count = captions * length
    heads_local = caption_attend.shape[2] // HEAD_DIM
    head_scale = HEAD_DIM ** (-0.5)

    def split_heads(matrix):
        return matrix.reshape(captions, length, heads_local, HEAD_DIM)

    flattened = caption_tokens.astype(jnp.float32).reshape(row_count, model_width)
    normed, norm_back_one = jax.vjp(norm_rows, flattened, norm_gains[0], norm_shifts[0])
    normed_low = normed.astype(jnp.bfloat16)
    queries = (matmul(normed_low, caption_attend[0]) + attend_bias[0]).astype(jnp.bfloat16)
    keyset = matmul(normed_low, caption_attend[1]).astype(jnp.bfloat16)
    valueset = (matmul(normed_low, caption_attend[2]) + attend_bias[1]).astype(jnp.bfloat16)
    weights = softmax_last(
        contract("bqhd,bkhd->bhqk", split_heads(queries), split_heads(keyset)) * head_scale
    )
    weights_low = weights.astype(jnp.bfloat16)
    mixture = (
        contract("bhqk,bkhd->bqhd", weights_low, split_heads(valueset))
        .astype(jnp.bfloat16)
        .reshape(row_count, heads_local * HEAD_DIM)
    )
    attended = lax.psum(matmul(mixture, caption_output).astype(jnp.bfloat16), "mp").astype(
        jnp.float32
    )
    residual = flattened + (attended + output_bias)
    normed_two, norm_back_two = jax.vjp(norm_rows, residual, norm_gains[1], norm_shifts[1])
    normed_two_low = normed_two.astype(jnp.bfloat16)
    hidden = matmul(normed_two_low, caption_expand) + expand_bias
    activated, activation_back = jax.vjp(partial(jax.nn.gelu, approximate=True), hidden)
    activated_low = activated.astype(jnp.bfloat16)
    reduced = lax.psum(matmul(activated_low, caption_reduce).astype(jnp.bfloat16), "mp").astype(
        jnp.float32
    )
    outputs = residual + (reduced + reduce_bias)
    pooled = jnp.mean(outputs.reshape(captions, length, model_width), axis=1)
    embed, unit_back = jax.vjp(unit_rows, pooled)
    embed_low = embed.astype(jnp.bfloat16)
    scaling = jnp.exp(log_scale[0])
    devices_data = lax.axis_size("dp")
    total_captions = captions * devices_data
    total_images = group_images.shape[0] * devices_data
    portion = lax.all_gather(group_images, "dp", axis=0, tiled=True)
    row_top = jnp.full((captions,), -1e30, jnp.float32)
    portion_rows = portion.shape[0]
    scores = scaling * contract_last(embed_low, portion)
    matches = (caption_image[:, None] == lax.iota(jnp.int32, portion_rows)[None, :]).astype(
        jnp.float32
    )
    new_top = jnp.maximum(row_top, jnp.max(scores, axis=1))
    row_total = jnp.sum(jnp.exp(scores - new_top[:, None]), axis=1)
    row_positive = jnp.sum(scores * matches, axis=1)
    portion_top = jnp.max(scores, axis=0)
    column_top = portion_top
    column_total = jnp.sum(jnp.exp(scores - portion_top[None, :]), axis=0)
    column_positive = jnp.sum(scores * matches, axis=0)
    column_count = jnp.sum(matches, axis=0)
    statistics = (
        new_top,
        row_total,
        row_positive,
        column_top,
        column_total,
        column_positive,
        column_count,
    )

    def combine(former, latter):
        joined_top = jnp.maximum(former[0], latter[0])
        joined_total = former[1] * jnp.exp(former[0] - joined_top) + latter[1] * jnp.exp(
            latter[0] - joined_top
        )
        return (joined_top, joined_total, former[2] + latter[2], former[3] + latter[3])

    column_top, column_total, column_positive, column_count = merged(
        (statistics[3], statistics[4], statistics[5], statistics[6]), "dp", combine
    )
    row_lse = statistics[0] + jnp.log(statistics[1])
    column_lse = column_top + jnp.log(column_total)
    column_inverse = 1.0 / column_count
    row_part = jnp.sum(row_lse - statistics[2])
    column_part = jnp.sum(column_lse - column_positive / column_count)
    image_weight = 0.5 * total_captions / total_images
    portion = lax.all_gather(group_images, "dp", axis=0, tiled=True)
    grad_scale = jnp.zeros((), jnp.float32)
    portion_rows = portion.shape[0]
    scores = scaling * contract_last(embed_low, portion)
    matches = (caption_image[:, None] == lax.iota(jnp.int32, portion_rows)[None, :]).astype(
        jnp.float32
    )
    grad_scores = 0.5 * (jnp.exp(scores - row_lse[:, None]) - matches) + image_weight * (
        jnp.exp(scores - column_lse[None, :]) - matches * column_inverse[None, :]
    )
    grad_scale = grad_scale + jnp.sum(grad_scores * scores)
    grad_cosine = (scaling * grad_scores).astype(jnp.bfloat16)
    grad_embed = matmul(grad_cosine, portion)
    grad_embed, grad_scale = (grad_embed, grad_scale)
    grad_pooled = unit_back(grad_embed)[0]
    grad_rows = jnp.broadcast_to(
        grad_pooled[:, None, :] * (1.0 / length), (captions, length, model_width)
    ).reshape(row_count, model_width)
    grad_rows_low = grad_rows.astype(jnp.bfloat16)
    gradient_reduce_bias = jnp.sum(grad_rows, axis=0)
    gradient_reduce = outer_sum(activated_low, grad_rows_low)
    grad_activated = contract_last(grad_rows_low, caption_reduce)
    grad_hidden = activation_back(grad_activated)[0].astype(jnp.bfloat16)
    gradient_expand_bias = jnp.sum(grad_hidden.astype(jnp.float32), axis=0)
    gradient_expand = outer_sum(normed_two_low, grad_hidden)
    grad_normed_two = lax.psum(
        contract_last(grad_hidden, caption_expand).astype(jnp.bfloat16), "mp"
    ).astype(jnp.float32)
    grad_from_norm, gain_second, shift_second = norm_back_two(grad_normed_two)
    grad_residual = grad_rows + grad_from_norm
    grad_residual_low = grad_residual.astype(jnp.bfloat16)
    gradient_output_bias = jnp.sum(grad_residual, axis=0)
    gradient_output = outer_sum(mixture, grad_residual_low)
    grad_mixture = split_heads(
        contract_last(grad_residual_low, caption_output).astype(jnp.bfloat16)
    )
    grad_probs = contract("bqhd,bkhd->bhqk", grad_mixture, split_heads(valueset))
    grad_valueset = (
        contract("bhqk,bqhd->bkhd", weights_low, grad_mixture)
        .astype(jnp.bfloat16)
        .reshape(row_count, heads_local * HEAD_DIM)
    )
    grad_logits = (
        weights * (grad_probs - jnp.sum(grad_probs * weights, axis=-1, keepdims=True))
    ).astype(jnp.bfloat16)
    grad_queries = (
        (contract("bhqk,bkhd->bqhd", grad_logits, split_heads(keyset)) * head_scale)
        .astype(jnp.bfloat16)
        .reshape(row_count, heads_local * HEAD_DIM)
    )
    grad_keyset = (
        (contract("bhqk,bqhd->bkhd", grad_logits, split_heads(queries)) * head_scale)
        .astype(jnp.bfloat16)
        .reshape(row_count, heads_local * HEAD_DIM)
    )
    gradient_attend = jnp.stack(
        [
            outer_sum(normed_low, grad_queries),
            outer_sum(normed_low, grad_keyset),
            outer_sum(normed_low, grad_valueset),
        ]
    )
    gradient_attend_bias = jnp.stack(
        [
            jnp.sum(grad_queries.astype(jnp.float32), axis=0),
            jnp.sum(grad_valueset.astype(jnp.float32), axis=0),
        ]
    )
    partial_normed = (
        contract_last(grad_queries, caption_attend[0])
        + contract_last(grad_keyset, caption_attend[1])
        + contract_last(grad_valueset, caption_attend[2])
    )
    grad_normed = lax.psum(partial_normed.astype(jnp.bfloat16), "mp").astype(jnp.float32)
    grad_from_first, gain_first, shift_first = norm_back_one(grad_normed)
    gradient_tokens = (grad_residual + grad_from_first).reshape(captions, length, model_width)
    summed = lax.psum(
        (
            gradient_attend,
            gradient_attend_bias,
            gradient_output,
            gradient_output_bias,
            gradient_expand,
            gradient_expand_bias,
            gradient_reduce,
            gradient_reduce_bias,
            jnp.stack([gain_first, gain_second]),
            jnp.stack([shift_first, shift_second]),
            grad_scale,
            row_part,
        ),
        "dp",
    )
    contrast_loss = (0.5 * (summed[11] / total_captions + column_part / total_images)).reshape(1)
    return (
        contrast_loss,
        gradient_tokens,
        summed[0],
        summed[1],
        summed[2],
        summed[3],
        summed[4],
        summed[5],
        summed[6],
        summed[7],
        summed[8],
        summed[9],
        summed[10].reshape(1),
    )


def solution(mesh):
    in_specs = (
        P("dp", None, None),
        P(("dp", "mp"), None, None),
        P(),
        P(),
        P(),
        P(),
        P(),
        P(None, None, "mp"),
        P(None, "mp"),
        P("mp", None),
        P(),
        P(None, "mp"),
        P("mp"),
        P("mp", None),
        P(),
        P(),
        P(),
        P(),
        P("dp"),
    )
    out_specs = (
        P(),
        P("dp", None, None),
        P(None, None, "mp"),
        P(None, "mp"),
        P("mp", None),
        P(),
        P(None, "mp"),
        P("mp"),
        P("mp", None),
        P(),
        P(),
        P(),
        P(),
    )
    return jax.shard_map(local, mesh=mesh, in_specs=in_specs, out_specs=out_specs, check_vma=False)
```

profile of v0, /device:TPU:0, one launch (start us, length us, event | category | flops | bytes accessed | tf_op | source)
XLA Modules:
  0.0 752.0 jit_solution(16923286609924520202)
XLA Ops:
  16.5 2.7 fusion.27
  22.5 2.9 reshape.434
  27.6 9.3 %fusion.126 = (f32[98,3,16]{2,1,0:T(4,128)S(1)}, f32[98,3,16,16]{2,3,1,0:T(8,128)S(1)}) fusion(f32[98,3,16,16]{2,3,1,0:T(8,128)S(1)} %fusion.64), kind=kOutput, calls=%fused_computation.225 | output fusion | flops 301071 | bytes 620928 | tf_op jit(solution)/shard_map/sub | solution.py:29
  40.6 4.0 reshape.436
  44.6 3.5 convolution_convert_fusion.2
  52.3 2.7 convolution_convert_fusion.10
  55.0 2.7 reshape.439
  57.7 2.7 convolution_convert_fusion.9
  60.4 2.7 reshape.440
  63.1 2.7 convolution_convert_fusion.8
  65.7 2.7 reshape.441
  68.5 2.6 fusion.46
  71.0 4.0 fusion.124
  79.4 68.9 %all-reduce.13.cloned.1.call-done = bf16[1568,768]{1,0:T(8,128)(2,1)} async-done(((bf16[1568,768]{1,0:T(8,128)(2,1)}), bf16[1568,768]{1,0:T(8,128)(2,1)}) %all-reduce.13.cloned.1.call-update) | async-done | bytes 2408464 | tf_op jit(solution)/shard_map/psum | solution.py:131
  148.3 5.2 add_add_fusion.4
  153.5 2.7 reduce_sum.372
  156.2 3.2 multiply_reduce_fusion
  167.2 4.6 convolution_convert_fusion.1
  171.9 3.2 fusion.125
  177.5 9.2 %fusion.42 = f32[350,768]{1,0:T(8,128)} fusion(f32[350,768]{1,0:T(8,128)} %get-tuple-element.318, bf16[3072,768]{1,0:T(8,128)(2,1)} %param.26, bf16[768,3072]{1,0:T(8,128)(2,1)} %param.25, f32[768]{0:T(1024)S(1)} %get-tuple-element.257, f32[350]{0:T(512)S(1)} %add_rsqrt_fusion.1, f32[350]{0:T(512)S(1)} %broadcast_multiply_fusion.3), kind=kOutput, calls=%fused_computation.90 | convolution fusion | flops 3314035200 | bytes 11593456 | tf_op jit(solution)/shard_map/dot_general | solution.py:38
  186.7 2.4 reshape.443
  190.8 14.1 %all-gather.4 = bf16[4,7,768]{2,1,0:T(8,128)(2,1)S(1)} all-gather(bf16[1,7,768]{2,1,0:T(8,128)(2,1)S(1)} %fusion.107), channel_id=1, replica_groups=mesh['dp'=8,'mp'=4] {'mp'}, dimensions={0}, use_global_device_ids=true | all-gather | bytes 53760 | tf_op jit(solution)/shard_map/all_gather | solution.py:107
  204.9 10.6 %all-gather.5 = bf16[8,28,768]{2,1,0:T(8,128)(2,1)} all-gather(bf16[1,28,768]{2,1,0:T(8,128)(2,1)S(1)} %reshape.482), channel_id=1, replica_groups=mesh['dp'=8,'mp'=4] {'dp'}, dimensions={0}, use_global_device_ids=true | all-gather | bytes 387072 | tf_op jit(solution)/shard_map/all_gather | solution.py:151
  217.8 51.3 %all-reduce.15.cloned.1.call-done = bf16[1568,768]{1,0:T(8,128)(2,1)} async-done(((bf16[1568,768]{1,0:T(8,128)(2,1)}), bf16[1568,768]{1,0:T(8,128)(2,1)}) %all-reduce.15.cloned.1.call-update) | async-done | bytes 2408464 | tf_op jit(solution)/shard_map/psum | solution.py:140
  269.0 5.8 add_add_fusion.3
  274.8 3.2 reduce_sum.374
  290.5 24.9 %all-reduce.5 = (f32[1792]{0:T(1024)}, f32[1792]{0:T(1024)}, f32[1792]{0:T(1024)}, f32[1792]{0:T(1024)}) all-reduce(f32[1792]{0:T(1024)} %dynamic-update-slice, f32[1792]{0:T(1024)} %dynamic-update-slice.1, f32[1792]{0:T(1024)} %dynamic-update-slice.2, f32[1792]{0:T(1024)} %dynamic-update-slice.3), channel_id=2, replica_groups=mesh['dp'=8,'mp'=4] {'dp'}, use_global_device_ids=true, to_apply=%add | all-reduce | flops 7168 | bytes 57344
  327.1 36.4 %while.21 = (s32[]{:T(128)}, f32[224]{0:T(256)}, f32[224]{0:T(256)}, f32[224]{0:T(256)}, f32[224]{0:T(256)}, /*index=5*/f32[8,224]{1,0:T(8,128)}, f32[8,224]{1,0...) while((s32[]{:T(128)}, f32[224]{0:T(256)}, f32[224]{0:T(256)}, ...), condition=%wide.region_28.0_spmd, body=%wide.region_27.0_spmd.sunk | while | flops 1797 | bytes 18079 | solution.py:18
  367.4 8.0 %convert_reduce_fusion.2 = (f32[768]{0:T(1024)}, bf16[1568,768]{1,0:T(8,128)(2,1)S(1)}) fusion(f32[1568,768]{1,0:T(8,128)} %copy-done.65, f32[768]{0:T(1024)S(1)} %copy-done.61, bf16[1568,768]{1,0:T(8,128)(2,1)S(1)} %bitcast_convert_fusion, bf16[768,768]{1,0:T(8,128)(2,1)S(1)} %copy-done), kind=kOutput, calls=%fused_computation.35 | convolution fusion | flops 1877384448 | bytes 10819584 | tf_op jit(solution)/shard_map/dot_general | solution.py:42
  376.8 3.6 convolution_convert_fusion
  380.5 95.0 %all-reduce.17.cloned.1.call-done = bf16[1568,768]{1,0:T(8,128)(2,1)} async-done(((bf16[1568,768]{1,0:T(8,128)(2,1)}), bf16[1568,768]{1,0:T(8,128)(2,1)}) %all-reduce.17.cloned.1.call-update) | async-done | bytes 2408464 | tf_op jit(solution)/shard_map/psum | solution.py:217
  475.5 5.1 fusion.15
  480.6 4.1 fusion.122
  493.2 3.8 multiply_reduce_fusion.2
  504.5 3.3 copy.87
  507.8 3.0 reshape.447
  510.8 3.3 copy.91
  514.2 3.0 reshape.449
  522.4 6.3 fusion.129
  528.7 7.0 fusion.119
  545.5 73.0 %all-reduce.19.cloned.1.call-done = bf16[1568,768]{1,0:T(8,128)(2,1)} async-done(((bf16[1568,768]{1,0:T(8,128)(2,1)}), bf16[1568,768]{1,0:T(8,128)(2,1)}) %all-reduce.19.cloned.1.call-update) | async-done | bytes 2408464 | tf_op jit(solution)/shard_map/psum | solution.py:265
  618.6 5.4 fusion.16
  624.0 3.3 add_add_fusion
  627.3 3.5 reduce_sum.395
  630.8 7.2 add_add_fusion.2
  638.0 26.4 %all-reduce.4 = (f32[]{:T(128)}, f32[2,192]{1,0:T(2,128)}, f32[768]{0:T(1024)}, f32[768]{0:T(1024)}, f32[768]{0:T(1024)}, /*index=5*/f32[2,768]{1,0:T(2,128)}, f32[2,768]{1,0:T(2,128)}, f32[1]{0:T(128)}) all-reduce(f32[]{:T(128)} %subtract_reduce_fusion.1, ...), channel_id=1, replica_groups=mesh['dp'=8,'mp'=4] {'dp'}, use_global_device_ids=true, to_apply=%region_22.0 | all-reduce | flops 5762 | bytes 46096 | tf_op jit(solution)/shard_map/psum | solution.py:268
  665.0 71.2 %all-reduce.21.cloned.1.call-done = (f32[3,768,192]{1,2,0:T(8,128)}, f32[192,768]{1,0:T(8,128)}, f32[768,768]{1,0:T(8,128)}, f32[768,768]{1,0:T(8,128)}) async-done(((f32[3,768,192]{1,2,0:T(8,128)}, f32[192,768]{1,0:T(8,128)}, f32[768,768]{1,0:T(8,128)}, f32[768,768]{1,0:T(8,128)}), (f32[3,768,192]{1,2,0:T(8,128)}, f32[192,768]{1,0:T(8,128)}, f32[768,768]{1,0:T(8,128)}, ...) | async-done | bytes 7077904 | tf_op jit(solution)/shard_map/psum | solution.py:268
  736.2 2.9 copy.157
  (286 shorter events, 140.4 us)
Async XLA Ops:
  7.2 160.1 %copy-start = (bf16[768,768]{1,0:T(8,128)(2,1)S(1)}, bf16[768,768]{1,0:T(8,128)(2,1)}, u32[]{:S(2)}) copy-start(bf16[768,768]{1,0:T(8,128)(2,1)} %param.34) | copy-start | bytes 3538948
  7.2 141.1 %all-reduce.13.cloned.1.call-start = ((), (), s32[]{:S(2)}) async-start(), calls=%async_computation | async-start | bytes 4816896 | tf_op jit(solution)/shard_map/psum | solution.py:131
  7.2 3.0 copy-start.3
  8.1 3.6 copy-start.48
  8.1 3.6 copy-start.49
  10.3 2.7 copy-start.27
  11.8 147.7 %copy-start.42 = (f32[768]{0:T(1024)}, f32[768]{0:T(1024)S(1)}, u32[]{:S(2)}) copy-start(f32[768]{0:T(1024)S(1)} %get-tuple-element.331) | copy-start | bytes 9220
  27.6 9.4 %copy-start.22 = (bf16[98,16,3,64]{3,2,1,0:T(4,128)(2,1)S(1)}, bf16[98,16,3,64]{3,2,1,0:T(4,128)(2,1)}, u32[]{:S(2)}) copy-start(bf16[98,16,3,64]{3,2,1,0:T(4,128)(2,1)} %reshape.433) | copy-start | bytes 1806340
  44.6 3.8 copy-start.12
  48.1 220.9 %all-reduce.15.cloned.1.call-start = ((), (), s32[]{:S(2)}) async-start(), calls=%async_computation.1 | async-start | bytes 4816896 | tf_op jit(solution)/shard_map/psum | solution.py:140
  71.0 4.0 copy-start.24
  75.9 72.4 %copy-start.52 = (f32[768]{0:T(1024)S(1)}, f32[768]{0:T(1024)}, u32[]{:S(2)}) copy-start(f32[768]{0:T(1024)} %param.31) | copy-start | bytes 9220
  156.2 3.3 copy-start.34
  156.2 3.8 copy-start.2
  160.0 2.9 copy-start.58
  162.9 4.3 copy-start.60
  165.1 2.2 copy-start.65
  171.8 303.6 %all-reduce.17.cloned.1.call-start = ((), (), s32[]{:S(2)}) async-start(), calls=%async_computation.2 | async-start | bytes 4816896 | tf_op jit(solution)/shard_map/psum | solution.py:217
  186.7 29.8 %copy-start.63 = (u32[32]{0:T(128)S(1)}, u32[32]{0:T(128)}, u32[]{:S(2)}) copy-start(u32[32]{0:T(128)} %constant.112) | copy-start | bytes 388
  186.7 82.3 %copy-start.53 = (f32[768]{0:T(1024)S(1)}, f32[768]{0:T(1024)}, u32[]{:S(2)}) copy-start(f32[768]{0:T(1024)} %param.35) | copy-start | bytes 9220
  363.4 4.0 copy-start.61
  367.4 8.0 %copy-start.17 = (bf16[1568,768]{1,0:T(8,128)(2,1)}, bf16[1568,768]{1,0:T(8,128)(2,1)S(1)}, u32[]{:S(2)}) copy-start(bf16[1568,768]{1,0:T(8,128)(2,1)S(1)} %bitcast_convert_fusion) | copy-start | bytes 7225348
  367.4 9.4 %copy-start.59 = (bf16[768,768]{1,0:T(8,128)(2,1)S(1)}, bf16[768,768]{1,0:T(8,128)(2,1)}, u32[]{:S(2)}) copy-start(bf16[768,768]{1,0:T(8,128)(2,1)} %param.32) | copy-start | bytes 3538948
  380.4 95.1 %copy-start.35 = (f32[1568]{0:T(1024)S(1)}, f32[1568]{0:T(1024)}, u32[]{:S(2)}) copy-start(f32[1568]{0:T(1024)} %copy-done.34) | copy-start | bytes 18820
  380.4 95.1 %copy-start.37 = (f32[1568]{0:T(1024)S(1)}, f32[1568]{0:T(1024)}, u32[]{:S(2)}) copy-start(f32[1568]{0:T(1024)} %copy-done.36) | copy-start | bytes 18820
  380.4 95.1 %copy-start.43 = (f32[768]{0:T(1024)S(1)}, f32[768]{0:T(1024)}, u32[]{:S(2)}) copy-start(f32[768]{0:T(1024)} %copy-done.42) | copy-start | bytes 9220
  380.4 100.1 %copy-start.39 = (f32[1568]{0:T(1024)S(1)}, f32[1568]{0:T(1024)}, u32[]{:S(2)}) copy-start(f32[1568]{0:T(1024)} %copy-done.38) | copy-start | bytes 18820
  380.4 238.1 %all-reduce.19.cloned.1.call-start = ((), (), s32[]{:S(2)}) async-start(), calls=%async_computation.3 | async-start | bytes 4816896 | tf_op jit(solution)/shard_map/psum | solution.py:265
  475.5 5.1 copy-start.11
  484.7 2.2 copy-start.5
  484.8 3.6 copy-start.32
  490.2 3.0 copy-start.30
  493.2 3.8 copy-start.8
  493.2 3.8 copy-start.23
  522.1 6.7 copy-start.62
  522.1 214.1 %all-reduce.21.cloned.1.call-start = ((), (), s32[]{:S(2)}) async-start(), calls=%async_computation.4 | async-start | bytes 14155776 | tf_op jit(solution)/shard_map/psum | solution.py:268
  522.4 6.3 copy-start.18
  528.7 7.0 copy-start.16
  538.1 2.3 copy-start.10
  538.1 2.5 copy-start.13
  542.2 76.4 %copy-start.41 = (f32[768]{0:T(1024)S(1)}, f32[768]{0:T(1024)}, u32[]{:S(2)}) copy-start(f32[768]{0:T(1024)} %copy-done.40) | copy-start | bytes 9220
  618.6 5.4 copy-start.4
  618.6 5.4 copy-start.6
  630.8 7.2 copy-start.54
  736.2 3.0 copy-start.31
  736.2 3.8 copy-start.21
  739.9 2.5 copy-start.20
  739.9 3.9 copy-start.1
  (23 other events, 32.9 us)
Sparse Core Ops, SparseCore 0:
  48.2 100.0 all-reduce.12
  172.0 97.0 all-reduce.14
  380.5 94.8 all-reduce.16
  522.2 96.3 all-reduce.18
  623.2 112.8 all-reduce.20
where the time goes:
time: 762 us; the launch traced here: 752 us
  waiting for transfers between devices  359 us (47%)
  other arithmetic  110 us (14%)
  local copies, waits for them, and re-layouts  100 us (13%)
  matrix products  86.8 us (11%)
  blocking collectives  75.9 us (10%)
  between operations  18.8 us (2%)
    psum x1, waiting for transfers between devices, local(): lax.psum(contract_last(grad_hidden, caption_expand).astype(jnp.bfloat16),...  95 us
    psum x1, waiting for transfers between devices, local(): lax.psum(partial_normed.astype(jnp.bfloat16), 'mp').astype(jnp.float32)  73 us
    psum x1, waiting for transfers between devices, local(): lax.psum((gradient_attend, gradient_attend_bias, gradient_output, gradien...  71.2 us
    psum x1, waiting for transfers between devices, local(): lax.psum(matmul(mixture, caption_output).astype(jnp.bfloat16), 'mp')  68.9 us
    psum x1, waiting for transfers between devices, local(): lax.psum(matmul(activated_low, caption_reduce).astype(jnp.bfloat16), 'mp')  51.3 us
    dot_general x12, matrix products, matmul(): return jnp.dot(left_side, right_side, preferred_element_type=jnp.float32)  36.2 us
    unnamed x147, local copies, waits for them, and re-layouts  30.9 us
    psum x1, blocking collectives, local(): lax.psum((gradient_attend, gradient_attend_bias, gradient_output, gradien...  26.4 us
  transfers between devices with their start and end apart: 5, of which 5 were waited for; matrix products, arithmetic and copies ran while one was open for 12% of the time, Pallas kernels for 0%

commit v1 on v0

--- a/solution.py
+++ b/solution.py
@@ -6,16 +6,6 @@
 from jax.sharding import PartitionSpec as P
 
 HEAD_DIM = 64
-
-
-def merged(array, axis, combine):
-    everything = jax.tree.map(lambda part: lax.all_gather(part, axis), array)
-    leading = jax.tree.map(lambda part: part[0], everything)
-
-    def step(k, so_far):
-        return combine(so_far, jax.tree.map(lambda part: part[k], everything))
-
-    return lax.fori_loop(1, lax.axis_size(axis), step, leading)
 
 
 def norm_rows(values, gains, shifts):
@@ -74,10 +64,12 @@
     residual = flattened + matmul(mixture, image_output)
     normed_two = norm_rows(residual, image_gains[1], 0.0).astype(jnp.bfloat16)
     activated = jax.nn.gelu(matmul(normed_two, image_expand), approximate=True).astype(jnp.bfloat16)
-    outputs = residual + matmul(activated, image_reduce)
-    return unit_rows(jnp.mean(outputs.reshape(group_size, length, model_width), axis=1)).astype(
-        jnp.bfloat16
-    )
+    activated_mean = jnp.mean(
+        activated.astype(jnp.float32).reshape(group_size, length, activated.shape[1]), axis=1
+    )
+    residual_mean = jnp.mean(residual.reshape(group_size, length, model_width), axis=1)
+    pooled = residual_mean + matmul(activated_mean.astype(jnp.bfloat16), image_reduce)
+    return unit_rows(pooled).astype(jnp.bfloat16)
 
 
 def local(
@@ -137,11 +129,15 @@
     hidden = matmul(normed_two_low, caption_expand) + expand_bias
     activated, activation_back = jax.vjp(partial(jax.nn.gelu, approximate=True), hidden)
     activated_low = activated.astype(jnp.bfloat16)
-    reduced = lax.psum(matmul(activated_low, caption_reduce).astype(jnp.bfloat16), "mp").astype(
+    activated_mean = jnp.mean(
+        activated_low.astype(jnp.float32).reshape(captions, length, activated.shape[1]), axis=1
+    ).astype(jnp.bfloat16)
+    reduced = lax.psum(matmul(activated_mean, caption_reduce).astype(jnp.bfloat16), "mp").astype(
         jnp.float32
     )
-    outputs = residual + (reduced + reduce_bias)
-    pooled = jnp.mean(outputs.reshape(captions, length, model_width), axis=1)
+    pooled = jnp.mean(residual.reshape(captions, length, model_width), axis=1) + (
+        reduced + reduce_bias
+    )
     embed, unit_back = jax.vjp(unit_rows, pooled)
     embed_low = embed.astype(jnp.bfloat16)
     scaling = jnp.exp(log_scale[0])
@@ -163,54 +159,37 @@
     column_total = jnp.sum(jnp.exp(scores - portion_top[None, :]), axis=0)
     column_positive = jnp.sum(scores * matches, axis=0)
     column_count = jnp.sum(matches, axis=0)
-    statistics = (
-        new_top,
-        row_total,
-        row_positive,
-        column_top,
-        column_total,
-        column_positive,
-        column_count,
-    )
-
-    def combine(former, latter):
-        joined_top = jnp.maximum(former[0], latter[0])
-        joined_total = former[1] * jnp.exp(former[0] - joined_top) + latter[1] * jnp.exp(
-            latter[0] - joined_top
-        )
-        return (joined_top, joined_total, former[2] + latter[2], former[3] + latter[3])
-
-    column_top, column_total, column_positive, column_count = merged(
-        (statistics[3], statistics[4], statistics[5], statistics[6]), "dp", combine
-    )
+    everything = lax.all_gather(
+        jnp.stack([column_top, column_total, column_positive, column_count]), "dp"
+    )
+    column_top = jnp.max(everything[:, 0], axis=0)
+    column_total = jnp.sum(everything[:, 1] * jnp.exp(everything[:, 0] - column_top[None]), axis=0)
+    column_positive = jnp.sum(everything[:, 2], axis=0)
+    column_count = jnp.sum(everything[:, 3], axis=0)
+    statistics = (new_top, row_total, row_positive)
     row_lse = statistics[0] + jnp.log(statistics[1])
     column_lse = column_top + jnp.log(column_total)
     column_inverse = 1.0 / column_count
     row_part = jnp.sum(row_lse - statistics[2])
     column_part = jnp.sum(column_lse - column_positive / column_count)
     image_weight = 0.5 * total_captions / total_images
-    portion = lax.all_gather(group_images, "dp", axis=0, tiled=True)
-    grad_scale = jnp.zeros((), jnp.float32)
-    portion_rows = portion.shape[0]
-    scores = scaling * contract_last(embed_low, portion)
-    matches = (caption_image[:, None] == lax.iota(jnp.int32, portion_rows)[None, :]).astype(
-        jnp.float32
-    )
     grad_scores = 0.5 * (jnp.exp(scores - row_lse[:, None]) - matches) + image_weight * (
         jnp.exp(scores - column_lse[None, :]) - matches * column_inverse[None, :]
     )
-    grad_scale = grad_scale + jnp.sum(grad_scores * scores)
+    grad_scale = jnp.sum(grad_scores * scores)
     grad_cosine = (scaling * grad_scores).astype(jnp.bfloat16)
     grad_embed = matmul(grad_cosine, portion)
-    grad_embed, grad_scale = (grad_embed, grad_scale)
     grad_pooled = unit_back(grad_embed)[0]
     grad_rows = jnp.broadcast_to(
         grad_pooled[:, None, :] * (1.0 / length), (captions, length, model_width)
     ).reshape(row_count, model_width)
-    grad_rows_low = grad_rows.astype(jnp.bfloat16)
-    gradient_reduce_bias = jnp.sum(grad_rows, axis=0)
-    gradient_reduce = outer_sum(activated_low, grad_rows_low)
-    grad_activated = contract_last(grad_rows_low, caption_reduce)
+    gradient_reduce_bias = jnp.sum(grad_pooled, axis=0)
+    grad_pooled_low = grad_pooled.astype(jnp.bfloat16)
+    gradient_reduce = outer_sum(activated_mean, grad_pooled_low)
+    grad_activated = jnp.broadcast_to(
+        (contract_last(grad_pooled_low, caption_reduce) * (1.0 / length))[:, None, :],
+        (captions, length, caption_reduce.shape[0]),
+    ).reshape(row_count, caption_reduce.shape[0])
     grad_hidden = activation_back(grad_activated)[0].astype(jnp.bfloat16)
     gradient_expand_bias = jnp.sum(grad_hidden.astype(jnp.float32), axis=0)
     gradient_expand = outer_sum(normed_two_low, grad_hidden)
@@ -265,15 +244,19 @@
     grad_normed = lax.psum(partial_normed.astype(jnp.bfloat16), "mp").astype(jnp.float32)
     grad_from_first, gain_first, shift_first = norm_back_one(grad_normed)
     gradient_tokens = (grad_residual + grad_from_first).reshape(captions, length, model_width)
-    summed = lax.psum(
+    large = lax.psum(
+        [
+            part.astype(jnp.bfloat16)
+            for part in (gradient_attend, gradient_output, gradient_expand, gradient_reduce)
+        ],
+        "dp",
+    )
+    large = [part.astype(jnp.float32) for part in large]
+    small = lax.psum(
         (
-            gradient_attend,
             gradient_attend_bias,
-            gradient_output,
             gradient_output_bias,
-            gradient_expand,
             gradient_expand_bias,
-            gradient_reduce,
             gradient_reduce_bias,
             jnp.stack([gain_first, gain_second]),
             jnp.stack([shift_first, shift_second]),
@@ -281,6 +264,20 @@
             row_part,
         ),
         "dp",
+    )
+    summed = (
+        large[0],
+        small[0],
+        large[1],
+        small[1],
+        large[2],
+        small[2],
+        large[3],
+        small[3],
+        small[4],
+        small[5],
+        small[6],
+        small[7],
     )
     contrast_loss = (0.5 * (summed[11] / total_captions + column_part / total_images)).reshape(1)
     return (

time: 762 us -> 607 us (0.80)
  waiting for transfers between devices: 359 us -> 290 us
  local copies, waits for them, and re-layouts: 100 us -> 60.7 us
  other arithmetic: 110 us -> 90.2 us
  blocking collectives: 75.9 us -> 57.5 us
    psum x2, waiting for transfers between devices: 122 us -> 70.1 us  [the longest x1 65.3 us: local(): lax.psum([part.astype(jnp.bfloat16) for part in (gradient_attend, gradien...]
    add x22 -> x0, other arithmetic: 32.1 us -> none  [the longest x7 8.89 us: combine(): former[1] * jnp.exp(former[0] - joined_top)]
    psum x1, waiting for transfers between devices: 68.9 us -> 38.7 us  [local(): lax.psum(matmul(mixture, caption_output).astype(jnp.bfloat16), 'mp')]
    unnamed x1 -> x0, blocking collectives: 24.9 us -> none
    unnamed x147 -> x138, local copies, waits for them, and re-layouts: 30.9 us -> 9.31 us
    psum x1, waiting for transfers between devices: 73 us -> 92.7 us  [local(): lax.psum(partial_normed.astype(jnp.bfloat16), 'mp').astype(jnp.float32)]
    dynamic_slice x14 -> x0, local copies, waits for them, and re-layouts: 10.1 us -> none  [step(): return combine(so_far, jax.tree.map(lambda part: part[k], everything))]
    reduce_sum x5 -> x9, other arithmetic: 7.09 us -> 17 us  [the longest x1 6.07 us: local(): gradient_expand_bias = jnp.sum(grad_hidden.astype(jnp.float32), axis=0)]
  transfers between devices with their start and end apart: 5 -> 5, of which waited for: 5 -> 5; matrix products, arithmetic and copies ran while one was open for 12% -> 14% of each run, Pallas kernels for 0% -> 0%
where the time goes in v1:
time: 607 us; the launch traced here: 598 us
  waiting for transfers between devices  290 us (48%)
  other arithmetic  90.2 us (15%)
  matrix products  80.7 us (13%)
  local copies, waits for them, and re-layouts  60.7 us (10%)
  blocking collectives  57.5 us (9%)
  between operations  18.3 us (3%)
    psum x1, waiting for transfers between devices, local(): lax.psum(partial_normed.astype(jnp.bfloat16), 'mp').astype(jnp.float32)  92.7 us
    psum x1, waiting for transfers between devices, local(): lax.psum(contract_last(grad_hidden, caption_expand).astype(jnp.bfloat16),...  88.7 us
    psum x1, waiting for transfers between devices, local(): lax.psum([part.astype(jnp.bfloat16) for part in (gradient_attend, gradien...  65.3 us
    psum x1, waiting for transfers between devices, local(): lax.psum(matmul(mixture, caption_output).astype(jnp.bfloat16), 'mp')  38.7 us
    dot_general x13, matrix products, matmul(): return jnp.dot(left_side, right_side, preferred_element_type=jnp.float32)  37.7 us
    psum x1, blocking collectives, local(): lax.psum((gradient_attend_bias, gradient_output_bias, gradient_expand_bia...  24.6 us
    dot_general x6, matrix products, outer_sum(): lax.dot_general(left_side, right_side, (((0,), (0,)), ((), ())), preferre...  16.4 us
    dot_general x8, matrix products, contract(): jnp.einsum(formula, left_side, right_side, preferred_element_type=jnp.flo...  15.5 us
  transfers between devices with their start and end apart: 5, of which 5 were waited for; matrix products, arithmetic and copies ran while one was open for 14% of the time, Pallas kernels for 0%

profile of v1, /device:TPU:0, one launch (start us, length us, event | category | flops | bytes accessed | tf_op | source)
XLA Modules:
  0.0 598.3 jit_solution(6334393651033239990)
XLA Ops:
  16.6 2.7 fusion.30
  22.5 2.9 reshape.458
  27.7 9.3 %fusion.131 = (f32[98,3,16]{2,1,0:T(4,128)S(1)}, f32[98,3,16,16]{2,3,1,0:T(8,128)S(1)}) fusion(f32[98,3,16,16]{2,3,1,0:T(8,128)S(1)} %fusion.66), kind=kOutput, calls=%fused_computation.244 | output fusion | flops 301071 | bytes 620928 | tf_op jit(solution)/shard_map/sub | solution.py:19
  40.6 4.0 reshape.460
  44.6 3.6 convolution_convert_fusion.1
  52.0 2.9 convolution_convert_fusion.9
  54.9 2.7 convolution_convert_fusion.10
  57.6 2.7 convolution_convert_fusion.11
  60.2 2.7 reshape.465
  63.0 2.7 reshape.466
  65.7 2.7 reshape.467
  68.4 2.6 fusion.45
  71.0 4.0 fusion.129
  78.0 2.6 copy.83
  82.8 3.2 fusion.130
  89.9 7.3 %fusion.32 = f32[350,3072]{1,0:T(8,128)} fusion(bf16[768,3072]{1,0:T(8,128)(2,1)} %param.23, f32[350,768]{1,0:T(8,128)} %get-tuple-element.71, f32[768]{0:T(1024)S(1)} %get-tuple-element.33, f32[350]{0:T(512)S(1)} %add_rsqrt_fusion.1, f32[350]{0:T(512)S(1)} %broadcast_multiply_fusion.4), kind=kOutput, calls=%fused_computation.72 | convolution fusion | flops 1663334400 | bytes 10100464 | tf_op jit(solution)/shard_map/dot_general | solution.py:28
  97.2 4.6 reshape.488
  103.2 3.0 reduce_sum.428
  106.2 3.3 multiply_reduce_fusion.10
  109.6 38.7 %all-reduce.8.cloned.1.call-done = bf16[1568,768]{1,0:T(8,128)(2,1)} async-done(((bf16[1568,768]{1,0:T(8,128)(2,1)}), bf16[1568,768]{1,0:T(8,128)(2,1)}) %all-reduce.8.cloned.1.call-update) | async-done | bytes 2408464 | tf_op jit(solution)/shard_map/psum | solution.py:123
  148.3 5.2 add_add_fusion.3
  153.6 2.7 reduce_sum.418
  156.3 3.2 multiply_reduce_fusion
  161.2 5.1 multiply_convert_fusion
  169.8 13.3 %all-gather.1 = bf16[4,7,768]{2,1,0:T(8,128)(2,1)S(1)} all-gather(bf16[1,7,768]{2,1,0:T(8,128)(2,1)S(1)} %fusion.108), channel_id=1, replica_groups=mesh['dp'=8,'mp'=4] {'mp'}, dimensions={0}, use_global_device_ids=true | all-gather | bytes 53760 | tf_op jit(solution)/shard_map/all_gather | solution.py:99
  183.2 10.5 %all-gather.2 = bf16[8,28,768]{2,1,0:T(8,128)(2,1)} all-gather(bf16[1,28,768]{2,1,0:T(8,128)(2,1)S(1)} %reshape.492), channel_id=1, replica_groups=mesh['dp'=8,'mp'=4] {'dp'}, dimensions={0}, use_global_device_ids=true | all-gather | bytes 387072 | tf_op jit(solution)/shard_map/all_gather | solution.py:147
  194.8 3.2 reduce_sum.417
  198.0 4.8 all-reduce.10.cloned.1.call-done
  206.3 9.0 %all-gather.3 = f32[8,4,224]{2,1,0:T(4,128)S(1)} all-gather(f32[1,4,224]{2,1,0:T(4,128)S(1)} %maximum_bitcast_fusion), channel_id=2, replica_groups=mesh['dp'=8,'mp'=4] {'dp'}, dimensions={0}, use_global_device_ids=true | all-gather | bytes 32256 | tf_op jit(solution)/shard_map/all_gather | solution.py:162
  218.7 6.1 %convert_reduce_fusion.3 = (f32[768]{0:T(1024)}, bf16[1568,768]{1,0:T(8,128)(2,1)S(1)}) fusion(f32[1568,768]{1,0:T(8,128)} %get-tuple-element.77, f32[768]{0:T(1024)S(1)} %copy-done.64, f32[98,768]{1,0:T(8,128)S(1)} %convolution_multiply_fusion), kind=kLoop, calls=%fused_computation.35 | loop fusion | flops 27696384 | bytes 7532544 | tf_op jit(solution)/shard_map/reduce_sum | solution.py:194
  226.2 3.5 convolution_convert_fusion
  232.3 5.2 convolution_convert_fusion.8
  237.5 88.7 %all-reduce.12.cloned.1.call-done = bf16[1568,768]{1,0:T(8,128)(2,1)} async-done(((bf16[1568,768]{1,0:T(8,128)(2,1)}), bf16[1568,768]{1,0:T(8,128)(2,1)}) %all-reduce.12.cloned.1.call-update) | async-done | bytes 2408464 | tf_op jit(solution)/shard_map/psum | solution.py:196
  326.1 5.1 fusion.15
  331.3 4.1 fusion.126
  342.0 3.8 multiply_reduce_fusion.2
  353.2 2.5 fusion.58
  357.8 3.0 reshape.476
  360.9 3.2 fusion.57
  366.1 3.0 reshape.478
  381.0 65.3 %all-reduce.16.cloned.1.call-done = (bf16[3,768,192]{1,2,0:T(8,128)(2,1)}, bf16[192,768]{1,0:T(8,128)(2,1)}, bf16[768,768]{1,0:T(8,128)(2,1)}, bf16[768,768]{1,0:T(8,128)(2,1)}) async-done(((bf16[3,768,192]{1,2,0:T(8,128)(2,1)}, bf16[192,768]{1,0:T(8,128)(2,1)}, bf16[768,768]{1,0:T(8,128)(2,1)}, bf16[768,768]{1,0:T(8,128)(2,1)}), (bf16[3,768,192]{1,2,0:T(8,128)(2,1)}, bf16[192,768]{1,0:T(8,128)(2,1)}, ...) | async-done | bytes 3538960 | tf_op jit(solution)/shard_map/psum | solution.py:247
  448.2 2.5 convert_element_type.230
  454.0 92.7 %all-reduce.14.cloned.1.call-done = bf16[1568,768]{1,0:T(8,128)(2,1)} async-done(((bf16[1568,768]{1,0:T(8,128)(2,1)}), bf16[1568,768]{1,0:T(8,128)(2,1)}) %all-reduce.14.cloned.1.call-update) | async-done | bytes 2408464 | tf_op jit(solution)/shard_map/psum | solution.py:244
  546.7 5.4 fusion.16
  552.1 3.0 add_add_fusion
  555.1 2.7 reduce_sum.445
  557.9 7.1 %add_add_fusion.2 = (f32[1568,768]{1,0:T(8,128)}, f32[768]{0:T(1024)S(1)}) fusion(f32[1568,768]{1,0:T(8,128)} %add_add_fusion, f32[1568,768]{1,0:T(8,128)} %copy-done.5, f32[1568]{0:T(1024)S(1)} %negate_multiply_fusion, f32[1568]{0:T(1024)S(1)} %negate_multiply_fusion.1, f32[98,768]{1,0:T(8,128)S(1)} %copy-done.18), kind=kLoop, calls=%fused_computation.36 | loop fusion | flops 6020352 | bytes 14767360 | tf_op jit(solution)/shard_map/add | solution.py:246
  565.0 24.6 %all-reduce = (f32[]{:T(128)}, f32[2,192]{1,0:T(2,128)}, f32[768]{0:T(1024)}, f32[768]{0:T(1024)}, f32[768]{0:T(1024)}, /*index=5*/f32[2,768]{1,0:T(2,128)}, f32[2,768]{1,0:T(2,128)}, f32[1]{0:T(128)}) all-reduce(f32[]{:T(128)} %subtract_reduce_fusion.1, f32[2,192]{1,0:T(2,128)S(1)} %pad_maximum_fusion.3, ...), channel_id=1, replica_groups=mesh['dp'=8,'mp'=4] {'dp'}, use_global_device_ids=true, to_apply=%region_24.0 | all-reduce | flops 5762 | bytes 46096 | tf_op jit(solution)/shard_map/psum | solution.py:255
  (242 shorter events, 83.1 us)
Async XLA Ops:
  7.2 154.0 %copy-start = (bf16[768,768]{1,0:T(8,128)(2,1)S(1)}, bf16[768,768]{1,0:T(8,128)(2,1)}, u32[]{:S(2)}) copy-start(bf16[768,768]{1,0:T(8,128)(2,1)} %param.30) | copy-start | bytes 3538948
  7.2 141.1 %all-reduce.8.cloned.1.call-start = ((), (), s32[]{:S(2)}) async-start(), calls=%async_computation | async-start | bytes 4816896 | tf_op jit(solution)/shard_map/psum | solution.py:123
  7.2 3.0 copy-start.3
  8.1 3.6 copy-start.59
  8.1 3.6 copy-start.60
  10.3 2.7 copy-start.33
  11.8 147.7 %copy-start.51 = (f32[768]{0:T(1024)}, f32[768]{0:T(1024)S(1)}, u32[]{:S(2)}) copy-start(f32[768]{0:T(1024)S(1)} %get-tuple-element.88) | copy-start | bytes 9220
  27.7 9.4 %copy-start.24 = (bf16[98,16,3,64]{3,2,1,0:T(4,128)(2,1)S(1)}, bf16[98,16,3,64]{3,2,1,0:T(4,128)(2,1)}, u32[]{:S(2)}) copy-start(bf16[98,16,3,64]{3,2,1,0:T(4,128)(2,1)} %reshape.457) | copy-start | bytes 1806340
  44.6 3.8 copy-start.10
  48.1 154.7 %all-reduce.10.cloned.1.call-start = ((), (), s32[]{:S(2)}) async-start(), calls=%async_computation.1 | async-start | bytes 319488 | tf_op jit(solution)/shard_map/psum | solution.py:135
  52.0 2.9 copy-start.37
  71.0 4.0 copy-start.26
  106.2 42.1 %copy-start.65 = (f32[768]{0:T(1024)S(1)}, f32[768]{0:T(1024)}, u32[]{:S(2)}) copy-start(f32[768]{0:T(1024)} %param.29) | copy-start | bytes 9220
  156.2 3.3 copy-start.41
  156.2 3.8 copy-start.2
  161.2 5.1 copy-start.23
  169.0 157.1 %all-reduce.12.cloned.1.call-start = ((), (), s32[]{:S(2)}) async-start(), calls=%async_computation.2 | async-start | bytes 4816896 | tf_op jit(solution)/shard_map/psum | solution.py:196
  194.8 8.0 %copy-start.49 = (f32[768]{0:T(1024)S(1)}, f32[768]{0:T(1024)}, u32[]{:S(2)}) copy-start(f32[768]{0:T(1024)} %param.33) | copy-start | bytes 9220
  202.8 14.6 %copy-start.19 = (bf16[98,768]{1,0:T(8,128)(2,1)S(1)}, bf16[98,768]{1,0:T(8,128)(2,1)}, u32[]{:S(2)}) copy-start(bf16[98,768]{1,0:T(8,128)(2,1)} %all-reduce.10.cloned.1.call-done) | copy-start | bytes 451588
  202.8 14.6 %copy-start.50 = (f32[768]{0:T(1024)S(1)}, f32[768]{0:T(1024)}, u32[]{:S(2)}) copy-start(f32[768]{0:T(1024)} %param.33) | copy-start | bytes 9220
  202.8 15.3 %copy-start.13 = (bf16[768,768]{1,0:T(8,128)(2,1)S(1)}, bf16[768,768]{1,0:T(8,128)(2,1)}, u32[]{:S(2)}) copy-start(bf16[768,768]{1,0:T(8,128)(2,1)} %param.32) | copy-start | bytes 3538948
  205.3 13.3 %copy-start.64 = (f32[768]{0:T(1024)S(1)}, f32[768]{0:T(1024)}, u32[]{:S(2)}) copy-start(f32[768]{0:T(1024)} %param.31) | copy-start | bytes 9220
  206.3 11.9 %copy-start.66 = (f32[98]{0:T(128)}, f32[98]{0:T(128)S(1)}, u32[]{:S(2)}) copy-start(f32[98]{0:T(128)S(1)} %log_add_fusion.1) | copy-start | bytes 1180
  216.0 2.1 copy-start.57
  229.8 216.5 %all-reduce.16.cloned.1.call-start = ((), (), s32[]{:S(2)}) async-start(), calls=%async_computation.4 | async-start | bytes 7077888 | tf_op jit(solution)/shard_map/psum | solution.py:247
  229.8 2.4 copy-start.21
  230.7 104.7 %copy-start.17 = (f32[98,768]{1,0:T(8,128)}, f32[98,768]{1,0:T(8,128)S(1)}, u32[]{:S(2)}) copy-start(f32[98,768]{1,0:T(8,128)S(1)} %broadcast_multiply_fusion) | copy-start | bytes 903172
  232.3 93.9 %copy-start.42 = (f32[1568]{0:T(1024)S(1)}, f32[1568]{0:T(1024)}, u32[]{:S(2)}) copy-start(f32[1568]{0:T(1024)} %copy-done.41) | copy-start | bytes 18820
  232.3 93.9 %copy-start.44 = (f32[1568]{0:T(1024)S(1)}, f32[1568]{0:T(1024)}, u32[]{:S(2)}) copy-start(f32[1568]{0:T(1024)} %copy-done.43) | copy-start | bytes 18820
  232.3 93.9 %copy-start.52 = (f32[768]{0:T(1024)S(1)}, f32[768]{0:T(1024)}, u32[]{:S(2)}) copy-start(f32[768]{0:T(1024)} %copy-done.51) | copy-start | bytes 9220
  237.4 93.8 %copy-start.46 = (f32[1568]{0:T(1024)S(1)}, f32[1568]{0:T(1024)}, u32[]{:S(2)}) copy-start(f32[1568]{0:T(1024)} %copy-done.45) | copy-start | bytes 18820
  326.1 5.1 copy-start.9
  335.4 2.2 copy-start.5
  335.5 2.1 copy-start.14
  341.9 3.8 copy-start.8
  341.9 3.8 copy-start.25
  353.2 2.5 copy-start.28
  360.8 3.3 copy-start.27
  369.2 2.5 copy-start.38
  372.7 174.0 %all-reduce.14.cloned.1.call-start = ((), (), s32[]{:S(2)}) async-start(), calls=%async_computation.3 | async-start | bytes 4816896 | tf_op jit(solution)/shard_map/psum | solution.py:244
  446.3 4.4 copy-start.30
  452.3 94.3 %copy-start.48 = (f32[768]{0:T(1024)S(1)}, f32[768]{0:T(1024)}, u32[]{:S(2)}) copy-start(f32[768]{0:T(1024)} %copy-done.47) | copy-start | bytes 9220
  546.7 5.4 copy-start.4
  546.7 5.4 copy-start.6
  555.1 2.7 copy-start.18
  557.9 7.2 %copy-start.53 = (f32[768]{0:T(1024)S(1)}, f32[768]{0:T(1024)}, u32[]{:S(2)}) copy-start(f32[768]{0:T(1024)} %get-tuple-element.52) | copy-start | bytes 9220
  557.9 7.2 %copy-start.54 = (f32[768]{0:T(1024)S(1)}, f32[768]{0:T(1024)}, u32[]{:S(2)}) copy-start(f32[768]{0:T(1024)} %get-tuple-element.50) | copy-start | bytes 9220
  557.9 32.4 %copy-start.1 = (bf16[768,768]{1,0:T(8,128)(2,1)S(1)}, bf16[768,768]{1,0:T(8,128)(2,1)}, u32[]{:S(2)}) copy-start(bf16[768,768]{1,0:T(8,128)(2,1)} %param.30) | copy-start | bytes 3538948
  (25 other events, 34.5 us)
Sparse Core Ops, SparseCore 0:
  48.3 100.0 all-reduce.7
  169.1 33.5 all-reduce.9
  229.9 96.1 all-reduce.11
  372.8 73.4 all-reduce.15
  449.3 97.3 all-reduce.13

commit v2 on v1

v2 whole, which is shorter than its diff:
```python
import functools

import jax
import jax.numpy as jnp
from jax import lax
from jax.experimental import pallas as pl
from jax.experimental.pallas import tpu as pltpu
from jax.sharding import PartitionSpec as P

HEAD_DIM = 64
LEN = 16
PIECE = 48
BLOCK = 112
F32 = jnp.float32
LOW = jnp.bfloat16
FAR = -1e30
GELU_A = 0.7978845608028654
GELU_B = 0.044715


def dot(a, b):
    return lax.dot_general(a, b, (((1,), (0,)), ((), ())), preferred_element_type=F32)


def dot_nt(a, b):
    return lax.dot_general(a, b, (((1,), (1,)), ((), ())), preferred_element_type=F32)


def dot_tn(a, b):
    return lax.dot_general(a, b, (((0,), (0,)), ((), ())), preferred_element_type=F32)


def iota(shape, axis):
    return lax.broadcasted_iota(jnp.int32, shape, axis)


def standard(x):
    width = x.shape[-1]
    centred = x - jnp.sum(x, axis=-1, keepdims=True) * (1.0 / width)
    variance = jnp.sum(centred * centred, axis=-1, keepdims=True) * (1.0 / width)
    scale = lax.rsqrt(variance + 1e-6)
    return centred * scale, scale


def gelu_parts(h):
    square = h * h
    t = jnp.tanh(GELU_A * h * (1.0 + GELU_B * square))
    half = 0.5 * (1.0 + t)
    slope = half + 0.5 * h * (1.0 - t * t) * (GELU_A * (1.0 + 3.0 * GELU_B * square))
    return h * half, slope


def sum8(x):
    return x[0:8] + x[8:16]


def body(
    n_dp,
    n_mp,
    tok_in,
    imt,
    ia_in,
    io_in,
    ie_in,
    ir_in,
    wao_in,
    we_in,
    wr_in,
    par,
    cap,
    red,
    gt,
    sgo,
    W,
    IW,
    TOK,
    N1,
    QKV,
    PR,
    MIX,
    RES,
    N2,
    GP,
    PA,
    ACC,
    GRL,
    GT,
    IP,
    EMB,
    MSG,
    STATS,
    SB,
    HM3,
    BM,
    HM4,
    POOL,
    EL,
    GPL,
    GA,
    RCORE,
    RB1,
    RB2,
    RZ,
    XR,
    XST,
    SG,
    SGR,
    gz_s,
    gz_r,
    ga_s,
    ga_r,
    loc_sem,
    iw_sem,
    tok_sem,
    sb_s,
    sb_r,
    emb_s,
    emb_r,
    st_s,
    st_r,
    stx_s,
    stx_r,
    rs_s,
    rs_r,
    ag_s,
    ag_r,
    xr_s,
    xr_r,
    sg_s,
    sg_r,
    gt_s,
    gt_r,
    out_sem,
):
    d = lax.axis_index("dp")
    m = lax.axis_index("mp")
    n_all = n_dp * n_mp
    me = d * n_mp + m
    bits = n_dp.bit_length() - 1
    extra = bits - 3
    images, image_len = imt.shape[0], imt.shape[1]
    rows = TOK.shape[0] * LEN
    n_cap = TOK.shape[0]
    n_blocks = rows // BLOCK
    width = RES.shape[1]
    shard = QKV.shape[3]
    image_rows = images * 64
    t_all = EMB.shape[0] * 8
    total_images = images * n_all
    total_captions = n_cap * 2 * n_dp

    def bit(v, b):
        return lax.rem(v // (1 << b), 2)

    def flip(v, b):
        return v + (1 - 2 * bit(v, b)) * (1 << b)

    cb, xb, yb = bit(d, 0), bit(d, 1), bit(d, 2)
    half = lax.rem(m, 2)
    pair = flip(m, 0)
    p_a = cb * 4 + yb * 2 + xb
    p_b = 8 + cb * 4 + xb * 2 + yb
    core_dev = (flip(d, 0), m)
    x_dev = (flip(d, 1), m)
    y_dev = (flip(d, 2), m)
    pair_dev = (d, pair)
    sends = []

    def remote(src, dst, ss, rs, dev):
        copy = pltpu.make_async_remote_copy(
            src_ref=src,
            dst_ref=dst,
            send_sem=ss,
            recv_sem=rs,
            device_id=dev,
            device_id_type=pl.DeviceIdType.MESH,
        )
        copy.start()
        sends.append(copy)
        return copy

    def local(src, dst, sem):
        copy = pltpu.make_async_copy(src, dst, sem)
        copy.start()
        return copy

    barrier = pltpu.get_barrier_semaphore()

    def greet(k, carry):
        q = lax.rem(me + k, n_all)
        pl.semaphore_signal(
            barrier,
            inc=1,
            device_id=(q // n_mp, lax.rem(q, n_mp)),
            device_id_type=pl.DeviceIdType.MESH,
        )
        return carry

    lax.fori_loop(1, n_all, greet, 0)

    image_loads = {}

    def load_image(i):
        if i < 3:
            src, slot = ia_in.at[i], i
        elif i == 3:
            src, slot = io_in, 3
        elif i < 8:
            src, slot = ie_in.at[:, :, pl.ds((i - 4) * width, width)], i
        else:
            src, slot = ir_in.at[i - 8], i - 8
        image_loads[i] = local(src, IW.at[slot], iw_sem.at[i])

    for i in range(8):
        load_image(i)
    tok_copy = local(tok_in.at[pl.ds(half * n_cap, n_cap)], TOK, tok_sem)
    sources = (wao_in, we_in, wr_in)
    own_loads = [local(sources[g], W.at[g, m], loc_sem.at[g]) for g in range(3)]

    pl.semaphore_wait(barrier, n_all - 1)

    hops = (1, 3, 2)
    zc, ac = {}, {}

    def gather_z(g):
        for k in hops:
            dev = (d, lax.rem(m + k, n_mp))
            for ab, p in ((0, p_a), (1, p_b)):
                zc[g, k, ab] = remote(
                    sources[g].at[pl.ds(p, 1)],
                    W.at[g, m, pl.ds(p, 1)],
                    gz_s.at[g, k - 1, ab],
                    gz_r.at[g, k - 1, ab],
                    dev,
                )

    def spread(at, stage, ss, rs):
        if stage == 0:
            pieces = ((p_a, 1, x_dev), (p_b, 1, y_dev))
        elif stage == 1:
            pieces = ((cb * 4 + yb * 2, 2, y_dev), (8 + cb * 4 + xb * 2, 2, x_dev))
        else:
            pieces = ((cb * 4, 4, core_dev), (8 + cb * 4, 4, core_dev))
        return [
            remote(at(p, n), at(p, n), ss.at[stage, ab], rs.at[stage, ab], dev)
            for ab, (p, n, dev) in enumerate(pieces)
        ]

    def gather_start(g, stage):
        for k in hops:
            source = lax.rem(m + n_mp - k, n_mp)
            if stage == 0:
                for ab in range(2):
                    zc[g, k, ab].wait_recv()
            else:
                for copy in ac[g, stage - 1, k]:
                    copy.wait_recv()
            ac[g, stage, k] = spread(
                lambda p, n: W.at[g, source, pl.ds(p, n)],
                stage,
                ga_s.at[g, k - 1],
                ga_r.at[g, k - 1],
            )

    def gather_end(g):
        for k in hops:
            for copy in ac[g, 2, k]:
                copy.wait_recv()
        own_loads[g].wait()

    gather_z(0)
    sb_copies = []
    for k in hops:
        sb_copies.append(
            remote(
                par.at[pl.ds(8, 8)],
                SB.at[m],
                sb_s.at[k - 1],
                sb_r.at[k - 1],
                (d, lax.rem(m + k, n_mp)),
            )
        )
    SB[m] = par[8:16]

    HM3[...] = jnp.where(
        iota((3 * BLOCK, shard), 0) // BLOCK == iota((3 * BLOCK, shard), 1) // HEAD_DIM, 1.0, 0.0
    ).astype(LOW)
    BM[...] = jnp.where(
        lax.rem(iota((3 * BLOCK, BLOCK), 0), BLOCK) // LEN == iota((3 * BLOCK, BLOCK), 1) // LEN,
        0.0,
        FAR,
    )
    HM4[...] = jnp.where(
        iota((256, 256), 0) // 64 == iota((256, 256), 1) // HEAD_DIM, 1.0, 0.0
    ).astype(LOW)
    POOL[...] = jnp.where(iota(POOL.shape, 1) // LEN == iota(POOL.shape, 0), 1.0, 0.0).astype(LOW)

    RES[pl.ds(0, image_rows), :] = jnp.zeros((image_rows, width), F32)
    GP[3, pl.ds(0, image_rows), :] = jnp.zeros((image_rows, width), LOW)
    gain_one = par[0:1]
    gain_two = par[1:2]

    def image_norm(i, carry):
        x = imt[i].astype(F32)
        at = pl.multiple_of(i * 64, 64)
        RES[pl.ds(at, image_len), :] = x
        GP[3, pl.ds(at, image_len), :] = (standard(x)[0] * gain_one).astype(LOW)
        return carry

    lax.fori_loop(0, images, image_norm, 0)
    for i in range(3):
        image_loads[i].wait()

    def image_qkv(j, carry):
        GP[j, pl.ds(0, image_rows), :] = dot(
            GP[3, pl.ds(0, image_rows), :], IW[j].reshape(width, width)
        ).astype(LOW)
        return carry

    lax.fori_loop(0, 3, image_qkv, 0)
    for i in range(8, 11):
        load_image(i)
    gather_start(0, 0)
    gather_z(1)

    key_valid = jnp.where(iota((256, 64), 1) < image_len, 0.0, FAR)
    lane_head = iota((64, 256), 1) // HEAD_DIM

    def image_attention(i, carry):
        at = pl.multiple_of(i * 64, 64)
        for n in range(width // 256):
            lanes = slice(256 * n, 256 * n + 256)
            q = GP[0, pl.ds(at, 64), lanes]
            k = GP[1, pl.ds(at, 64), lanes]
            v = GP[2, pl.ds(at, 64), lanes]
            logits = dot_nt(jnp.concatenate([q] * 4, axis=0) * HM4[...], k) * 0.125 + key_valid
            expos = jnp.exp(logits - jnp.max(logits, axis=-1, keepdims=True))
            probs = (expos * (1.0 / jnp.sum(expos, axis=-1, keepdims=True))).astype(LOW)
            o = dot(probs, v)
            mix = jnp.where(
                lane_head < 2,
                jnp.where(lane_head == 0, o[0:64], o[64:128]),
                jnp.where(lane_head == 2, o[128:192], o[192:256]),
            )
            N2[pl.ds(at, 64), lanes] = mix.astype(LOW)
        return carry

    lax.fori_loop(0, images, image_attention, 0)
    gather_start(0, 1)
    image_loads[3].wait()

    def image_out(n, carry):
        lanes = pl.ds(pl.multiple_of(n * 256, 256), 256)
        RES[pl.ds(0, image_rows), lanes] += dot(
            N2[pl.ds(0, image_rows), :], IW[3, :, :, lanes].reshape(width, 256)
        )
        return carry

    lax.fori_loop(0, width // 256, image_out, 0)
    load_image(11)

    def image_norm_two(t, carry):
        at = pl.ds(pl.multiple_of(t * 16, 16), 16)
        GP[3, at, :] = (standard(RES[at, :])[0] * gain_two).astype(LOW)
        return carry

    lax.fori_loop(0, image_rows // 16, image_norm_two, 0, unroll=4)
    IP[...] = jnp.zeros_like(IP)
    for i in range(images):
        IP[i : i + 1, :] = jnp.sum(RES[64 * i : 64 * i + image_len, :], axis=0, keepdims=True) * (
            1.0 / image_len
        )
    image_pool = jnp.where(
        (iota((16, image_rows), 1) // 64 == iota((16, image_rows), 0))
        & (lax.rem(iota((16, image_rows), 1), 64) < image_len),
        1.0,
        0.0,
    ).astype(LOW)
    for i in range(4, 12):
        image_loads[i].wait()

    def image_feed(u, carry):
        ACC[pl.ds(0, image_rows), :] = dot(
            GP[3, pl.ds(0, image_rows), :], IW[4 + u].reshape(width, width)
        )

        def activate(t, inner):
            at = pl.ds(pl.multiple_of(t * 16, 16), 16)
            h = ACC[at, :]
            act = 0.5 * h * (1.0 + jnp.tanh(GELU_A * h * (1.0 + GELU_B * h * h)))
            N2[at, :] = act.astype(LOW)
            return inner

        lax.fori_loop(0, image_rows // 16, activate, 0, unroll=4)
        pooled = (dot(image_pool, N2[pl.ds(0, image_rows), :]) * (1.0 / image_len)).astype(LOW)
        IP[...] += dot(pooled, IW[u].reshape(width, width))
        return carry

    lax.fori_loop(0, 2, image_feed, 0)
    gather_start(0, 2)
    gather_start(1, 0)
    gather_z(2)
    lax.fori_loop(2, 4, image_feed, 0)
    pooled_image = IP[0:8]
    EMB[me] = (
        pooled_image
        * lax.rsqrt(jnp.sum(pooled_image * pooled_image, axis=-1, keepdims=True) + 1e-6)
    ).astype(LOW)

    def send_embed(k, carry):
        q = lax.rem(me + k, n_all)
        pltpu.make_async_remote_copy(
            src_ref=EMB.at[me],
            dst_ref=EMB.at[me],
            send_sem=emb_s,
            recv_sem=emb_r,
            device_id=(q // n_mp, lax.rem(q, n_mp)),
            device_id_type=pl.DeviceIdType.MESH,
        ).start()
        return carry

    lax.fori_loop(1, n_all, send_embed, 0)

    tok_copy.wait()
    g1, g2 = par[4:5], par[5:6]
    b1, b2 = par[6:7], par[7:8]

    def norm_one(t, carry):
        at = pl.ds(pl.multiple_of(t * LEN, LEN), LEN)
        N1[at, :] = (standard(TOK[t].astype(F32))[0] * g1 + b1).astype(LOW)
        return carry

    lax.fori_loop(0, n_cap, norm_one, 0, unroll=7)
    for copy in sb_copies:
        copy.wait_recv()
    gather_end(0)

    def project(t, carry):
        s, j = t // 3, lax.rem(t, 3)
        weight = W[0, s, pl.ds(4 * j, 4)].reshape(shard, width)
        QKV[j, s] = (dot_nt(N1[...], weight) + SB[s, pl.ds(j, 1), 0:shard]).astype(LOW)
        return carry

    lax.fori_loop(0, 3 * n_mp, project, 0)
    gather_start(1, 1)
    lane_three = iota((BLOCK, shard), 1) // HEAD_DIM

    def join_heads(o):
        return jnp.where(
            lane_three == 0,
            o[0:BLOCK],
            jnp.where(lane_three == 1, o[BLOCK : 2 * BLOCK], o[2 * BLOCK : 3 * BLOCK]),
        )

    def attention(b, carry):
        at = pl.ds(pl.multiple_of(b * BLOCK, 16), BLOCK)
        for s in range(n_mp):
            q = jnp.concatenate([QKV[0, s, at, :]] * 3, axis=0) * HM3[...]
            logits = dot_nt(q, QKV[1, s, at, :]) * 0.125 + BM[...]
            expos = jnp.exp(logits - jnp.max(logits, axis=-1, keepdims=True))
            probs = (expos * (1.0 / jnp.sum(expos, axis=-1, keepdims=True))).astype(LOW)
            PR[s, b] = probs
            MIX[s, at, :] = join_heads(dot(probs, QKV[2, s, at, :])).astype(LOW)
        return carry

    lax.fori_loop(0, n_blocks, attention, 0)
    gather_start(1, 2)
    gather_start(2, 0)

    def attend_out(n, carry):
        lanes = pl.ds(pl.multiple_of(n * 256, 256), 256)
        total = dot(MIX[0], W[0, 0, pl.ds(12, 4), :, lanes].reshape(shard, 256))
        for s in range(1, n_mp):
            total += dot(MIX[s], W[0, s, pl.ds(12, 4), :, lanes].reshape(shard, 256))
        ACC[:, lanes] = total
        return carry

    lax.fori_loop(0, width // 256, attend_out, 0)
    out_bias = par[2:3]

    def norm_two(t, carry):
        at = pl.ds(pl.multiple_of(t * LEN, LEN), LEN)
        x = TOK[t].astype(F32) + (ACC[at, :] + out_bias)
        RES[at, :] = x
        N2[at, :] = (standard(x)[0] * g2 + b2).astype(LOW)
        return carry

    lax.fori_loop(0, n_cap, norm_two, 0, unroll=7)
    gather_end(1)
    gather_start(2, 1)

    def feed(s, carry):
        ACC[...] = dot(N2[...], W[1, s].reshape(width, width))
        bias = SB[s, 3:4, :]

        def activate(t, inner):
            at = pl.ds(pl.multiple_of(t * LEN, LEN), LEN)
            act, slope = gelu_parts(ACC[at, :] + bias)
            GT[at, :] = act.astype(LOW)
            GP[s, at, :] = slope.astype(LOW)
            return inner

        lax.fori_loop(0, n_cap, activate, 0, unroll=7)
        PA[s] = (dot(POOL[...], GT[...]) * (1.0 / LEN)).astype(LOW)
        return carry

    lax.fori_loop(0, n_mp, feed, 0)
    gather_start(2, 2)

    def pool_residual(n, carry):
        lanes = pl.ds(pl.multiple_of(n * 128, 128), 128)
        res = RES[:, lanes]
        res_high = res.astype(LOW)
        res_low = (res - res_high.astype(F32)).astype(LOW)
        EL[:, lanes] = (dot(POOL[...], res_high) + dot(POOL[...], res_low)) * (1.0 / LEN)
        return carry

    lax.fori_loop(0, width // 128, pool_residual, 0)
    pooled = EL[...] + par[3:4]
    gather_end(2)
    for s in range(n_mp):
        pooled += dot(PA[s], W[2, s].reshape(width, width))
    inverse = lax.rsqrt(jnp.sum(pooled * pooled, axis=-1, keepdims=True) + 1e-6)
    embed = pooled * inverse
    EL[...] = embed

    pltpu.make_async_copy(EMB.at[pl.ds(0, n_all - 1)], EMB.at[pl.ds(0, n_all - 1)], emb_r).wait()
    group = min(n_all, 32)

    def embeds(c):
        part = EMB[c * group : c * group + group].astype(F32)
        return part.reshape(group * 8, width).astype(LOW)

    scaling = jnp.exp(par[12:13, 0:1])
    embed_low = embed.astype(LOW)
    scores = scaling * jnp.concatenate(
        [dot_nt(embed_low, embeds(c)) for c in range(n_all // group)], axis=1
    )
    cap_rows = scores.shape[0]
    column = iota((cap_rows, t_all), 1)
    col_ok = lax.rem(column, 8) < images
    row_ok = iota((cap_rows, t_all), 0) < n_cap
    image_id = (column // 8) * images + lax.rem(column, 8)
    matches = jnp.where((cap[half] == image_id) & col_ok & row_ok, 1.0, 0.0)
    by_row = jnp.where(col_ok, scores, FAR)
    row_top = jnp.max(by_row, axis=1, keepdims=True)
    row_lse = row_top + jnp.log(jnp.sum(jnp.exp(by_row - row_top), axis=1, keepdims=True))
    row_positive = jnp.sum(scores * matches, axis=1, keepdims=True)
    row_part = jnp.sum(
        jnp.where(iota((cap_rows, 1), 0) < n_cap, row_lse - row_positive, 0.0), axis=0, keepdims=True
    )
    by_column = jnp.where(row_ok, scores, FAR)
    top = jnp.max(by_column, axis=0, keepdims=True)
    MSG[...] = jnp.zeros_like(MSG)
    MSG[0:1, :] = top
    MSG[1:2, :] = jnp.sum(jnp.exp(by_column - top), axis=0, keepdims=True)
    MSG[2:3, :] = jnp.sum(scores * matches, axis=0, keepdims=True)
    MSG[3:4, :] = jnp.sum(matches, axis=0, keepdims=True)
    MSG[4:5, :] = jnp.broadcast_to(row_part, (1, t_all))
    low = lax.rem(d, 8)
    slot = low * 2 + half
    STATS[slot] = MSG[...]

    def send_stats(k, carry):
        q = lax.rem(slot + k, 16)
        pltpu.make_async_remote_copy(
            src_ref=MSG,
            dst_ref=STATS.at[slot],
            send_sem=st_s,
            recv_sem=st_r,
            device_id=(d - low + q // 2, m - half + lax.rem(q, 2)),
            device_id_type=pl.DeviceIdType.MESH,
        ).start()
        return carry

    lax.fori_loop(1, 16, send_stats, 0)
    pltpu.make_async_copy(STATS.at[pl.ds(0, 15)], STATS.at[pl.ds(0, 15)], st_r).wait()
    top = jnp.max(STATS[:, 0, :], axis=0, keepdims=True)
    total = jnp.sum(STATS[:, 1, :] * jnp.exp(STATS[:, 0, :] - top), axis=0, keepdims=True)
    positive = jnp.sum(STATS[:, 2, :], axis=0, keepdims=True)
    count = jnp.sum(STATS[:, 3, :], axis=0, keepdims=True)
    row_sum = jnp.sum(STATS[:, 4, :], axis=0, keepdims=True)
    for x in range(extra):
        XST[0, x] = jnp.concatenate(
            [top, total, positive, count, row_sum, jnp.zeros((3, t_all), F32)], axis=0
        )
        remote(
            XST.at[0, x], XST.at[1, x], stx_s.at[x], stx_r.at[x], (flip(d, 3 + x), m)
        ).wait_recv()
        other = XST[1, x]
        joined = jnp.maximum(top, other[0:1])
        total = total * jnp.exp(top - joined) + other[1:2] * jnp.exp(other[0:1] - joined)
        top = joined
        positive = positive + other[2:3]
        count = count + other[3:4]
        row_sum = row_sum + other[4:5]
    ok = col_ok[0:1]
    count = jnp.where(ok, count, 1.0)
    col_lse = top + jnp.log(total)
    column_part = jnp.sum(
        jnp.where(ok, col_lse - positive / count, 0.0), axis=1, keepdims=True
    )
    loss = 0.5 * (row_sum[:, 0:1] * (1.0 / total_captions) + column_part * (1.0 / total_images))
    weight = 0.5 * total_captions / total_images
    grad_scores = 0.5 * (jnp.exp(by_row - row_lse) - matches) + weight * (
        jnp.exp(by_column - col_lse) - matches * (1.0 / count)
    )
    grad_scores = jnp.where(col_ok & row_ok, grad_scores, 0.0)
    grad_log = jnp.sum(
        jnp.sum(grad_scores * scores, axis=1, keepdims=True), axis=0, keepdims=True
    )
    embed = EL[...]
    grad_cosine = (scaling * grad_scores).astype(LOW)
    grad_embed = dot(grad_cosine[:, 0 : group * 8], embeds(0))
    for c in range(1, n_all // group):
        grad_embed += dot(grad_cosine[:, c * group * 8 : (c + 1) * group * 8], embeds(c))
    grad_pooled = (
        grad_embed - embed * jnp.sum(embed * grad_embed, axis=-1, keepdims=True)
    ) * inverse
    SG[0] = jnp.zeros(SG.shape[1:], F32)
    SG[0, 13:14, :] = jnp.sum(grad_pooled, axis=0, keepdims=True)
    SG[0, 18:19, :] = jnp.broadcast_to(grad_log, (1, width))
    GPL[0] = grad_pooled.astype(LOW)
    grad_rows = grad_pooled * (1.0 / LEN)
    EL[...] = grad_rows
    GPL[1] = grad_rows.astype(LOW)

    def part(g, i):
        return IW.at[2 * g + i]

    places = (4, 7, 6)

    def whole(g):
        return IW.at[places[g]]

    def settle(copies):
        for copy in copies:
            copy.wait_send()
        sends[:] = [other for other in sends if all(other is not copy for copy in copies)]

    def add_pieces(g, i, p, n, read):
        for r in range(n):
            IW[2 * g + i, p + r] = IW[2 * g + i, p + r] + read(r)

    state = {}
    stores = []

    def reduce_step(g, step):
        if step == 0:
            if g == 0:
                settle([copy for old in range(4) for copy in state[2, old]])
            copies = []
            for i in range(2):
                for ab in range(2):
                    p = 8 * ab + 4 * (1 - cb)
                    copies.append(
                        remote(
                            part(g, i).at[pl.ds(p, 4)],
                            RCORE.at[g % 2, i, ab],
                            rs_s.at[g, 0, 2 * i + ab],
                            rs_r.at[g, 0, 2 * i + ab],
                            core_dev,
                        )
                    )
            state[g, 0] = copies
        elif step == 1:
            for copy in state[g, 0]:
                copy.wait_recv()
            for i in range(2):
                for ab in range(2):
                    add_pieces(
                        g, i, 8 * ab + 4 * cb, 4, lambda r, i=i, ab=ab: RCORE[g % 2, i, ab, r]
                    )
            copies = []
            for i in range(2):
                for ab, b, dev in ((0, yb, y_dev), (1, xb, x_dev)):
                    p = 8 * ab + 4 * cb + 2 * (1 - b)
                    copies.append(
                        remote(
                            part(g, i).at[pl.ds(p, 2)],
                            RB1.at[g % 2, i, ab],
                            rs_s.at[g, 1, 2 * i + ab],
                            rs_r.at[g, 1, 2 * i + ab],
                            dev,
                        )
                    )
            state[g, 1] = copies
        elif step == 2:
            for copy in state[g, 1]:
                copy.wait_recv()
            for i in range(2):
                for ab, b in ((0, yb), (1, xb)):
                    add_pieces(
                        g,
                        i,
                        8 * ab + 4 * cb + 2 * b,
                        2,
                        lambda r, i=i, ab=ab: RB1[g % 2, i, ab, r],
                    )
            copies = []
            for i in range(2):
                for ab, b, c, dev in ((0, yb, xb, x_dev), (1, xb, yb, y_dev)):
                    p = 8 * ab + 4 * cb + 2 * b + 1 - c
                    copies.append(
                        remote(
                            part(g, i).at[pl.ds(p, 1)],
                            RB2.at[g % 2, i, ab],
                            rs_s.at[g, 2, 2 * i + ab],
                            rs_r.at[g, 2, 2 * i + ab],
                            dev,
                        )
                    )
            state[g, 2] = copies
        elif step == 3:
            for copy in state[g, 2]:
                copy.wait_recv()
            for i in range(2):
                for ab, p in ((0, p_a), (1, p_b)):
                    add_pieces(g, i, p, 1, lambda r, i=i, ab=ab: RB2[g % 2, i, ab, r])
            state[g, 3] = [
                remote(
                    part(g, 1).at[pl.ds(p, 1)],
                    RZ.at[g, ab],
                    rs_s.at[g, 3, ab],
                    rs_r.at[g, 3, ab],
                    pair_dev,
                )
                for ab, p in ((0, p_a), (1, p_b))
            ]
        elif step == 4:
            for copy in state[g, 3]:
                copy.wait_recv()
            for ab, p in ((0, p_a), (1, p_b)):
                IW[places[g], p] = IW[2 * g, p] + RZ[g, ab, 0]
            for x in range(extra):
                copies = [
                    remote(
                        whole(g).at[pl.ds(p, 1)],
                        XR.at[g % 2, x, ab],
                        xr_s.at[g, x, ab],
                        xr_r.at[g, x, ab],
                        (flip(d, 3 + x), m),
                    )
                    for ab, p in ((0, p_a), (1, p_b))
                ]
                for copy in copies:
                    copy.wait_recv()
                settle(copies)
                for ab, p in ((0, p_a), (1, p_b)):
                    IW[places[g], p] = IW[places[g], p] + XR[g % 2, x, ab, 0]
            state[g, 4] = spread(
                lambda p, n: whole(g).at[pl.ds(p, n)], 0, ag_s.at[g], ag_r.at[g]
            )
        elif step in (5, 6):
            for copy in state[g, step - 1]:
                copy.wait_recv()
            state[g, step] = spread(
                lambda p, n: whole(g).at[pl.ds(p, n)], step - 4, ag_s.at[g], ag_r.at[g]
            )
        else:
            for copy in state[g, 6]:
                copy.wait_recv()
            stores.append(local(whole(g), red.at[g], out_sem.at[g]))

    shards = (m, pair)
    for i in range(2):
        IW[4 + i] = dot_tn(PA[shards[i]], GPL[0]).astype(LOW).reshape(16, PIECE, width)
    reduce_step(2, 0)

    def grad_activation(s, carry):
        GA[s] = dot_nt(GPL[1], W[2, s].reshape(width, width))
        return carry

    lax.fori_loop(0, n_mp, grad_activation, 0)
    reduce_step(2, 1)
    ones = jnp.ones((16, rows), LOW)

    def grad_hidden(s, carry):
        def scale(t, inner):
            at = pl.ds(pl.multiple_of(t * LEN, LEN), LEN)
            GP[s, at, :] = (GP[s, at, :].astype(F32) * GA[s, pl.ds(t, 1), :]).astype(LOW)
            return inner

        lax.fori_loop(0, n_cap, scale, 0, unroll=7)
        SG[0, pl.ds(8 + s, 1), :] = dot(ones, GP[s])[0:1]
        return carry

    lax.fori_loop(0, n_mp, grad_hidden, 0)
    reduce_step(2, 2)

    def expand_gradient(i, carry):
        s = m + i * (pair - m)
        IW[2 + i] = dot_tn(N2[...], GP[s]).astype(LOW).reshape(16, PIECE, width)
        return carry

    lax.fori_loop(0, 2, expand_gradient, 0)
    reduce_step(1, 0)
    reduce_step(2, 3)

    def grad_norm_two(n, carry):
        p = pl.ds(8 * n, 8)
        total = dot_nt(GP[0], W[1, 0, p].reshape(8 * PIECE, width))
        for s in range(1, n_mp):
            total += dot_nt(GP[s], W[1, s, p].reshape(8 * PIECE, width))
        ACC[:, pl.ds(pl.multiple_of(n * 384, 128), 384)] = total
        return carry

    lax.fori_loop(0, 2, grad_norm_two, 0)
    reduce_step(1, 1)
    reduce_step(2, 4)

    def norm_back(e, gain, x):
        xhat, scale = standard(x)
        eg = e * gain
        c1 = jnp.sum(eg, axis=-1, keepdims=True) * (1.0 / width)
        c2 = jnp.sum(eg * xhat, axis=-1, keepdims=True) * (1.0 / width)
        return (eg - c1 - xhat * c2) * scale, sum8(e * xhat), sum8(e)

    zero8 = jnp.zeros((8, width), F32)

    def back_two(t, carry):
        at = pl.ds(pl.multiple_of(t * LEN, LEN), LEN)
        dv, dg, db = norm_back(ACC[at, :], g2, RES[at, :])
        g = EL[pl.ds(t, 1), :] + dv
        RES[at, :] = g
        GRL[at, :] = g.astype(LOW)
        return carry[0] + dg, carry[1] + db, carry[2] + sum8(g)

    dg, db, do = lax.fori_loop(0, n_cap, back_two, (zero8, zero8, zero8), unroll=7)
    SG[0, 15:16, :] = jnp.sum(dg, axis=0, keepdims=True)
    SG[0, 17:18, :] = jnp.sum(db, axis=0, keepdims=True)
    SG[0, 12:13, :] = jnp.sum(do, axis=0, keepdims=True)

    for i in range(2):
        IW[i, pl.ds(12, 4)] = dot_tn(MIX[shards[i]], GRL[...]).astype(LOW).reshape(4, PIECE, width)
    reduce_step(1, 2)
    reduce_step(2, 5)

    def grad_mixture(s, carry):
        MIX[s] = dot_nt(GRL[...], W[0, s, pl.ds(12, 4)].reshape(shard, width)).astype(LOW)
        return carry

    lax.fori_loop(0, n_mp, grad_mixture, 0)
    reduce_step(2, 6)

    def attention_back(b, carry):
        at = pl.ds(pl.multiple_of(b * BLOCK, 16), BLOCK)
        for s in range(n_mp):
            q = jnp.concatenate([QKV[0, s, at, :]] * 3, axis=0) * HM3[...]
            g = jnp.concatenate([MIX[s, at, :]] * 3, axis=0) * HM3[...]
            k = QKV[1, s, at, :]
            v = QKV[2, s, at, :]
            low_probs = PR[s, b]
            probs = low_probs.astype(F32)
            grad_probs = dot_nt(g, v)
            inner = jnp.sum(grad_probs * probs, axis=-1, keepdims=True)
            grad_logits = (probs * (grad_probs - inner)).astype(LOW)
            QKV[2, s, at, :] = dot_tn(low_probs, g).astype(LOW)
            QKV[0, s, at, :] = (join_heads(dot(grad_logits, k)) * 0.125).astype(LOW)
            QKV[1, s, at, :] = (dot_tn(grad_logits, q) * 0.125).astype(LOW)
        return carry

    lax.fori_loop(0, n_blocks, attention_back, 0)
    reduce_step(1, 3)

    def grad_norm_one(n, carry):
        lanes = pl.ds(pl.multiple_of(n * 256, 256), 256)
        total = None
        for s in range(n_mp):
            for j in range(3):
                term = dot(QKV[j, s], W[0, s, pl.ds(4 * j, 4), :, lanes].reshape(shard, 256))
                total = term if total is None else total + term
        ACC[:, lanes] = total
        return carry

    lax.fori_loop(0, width // 256, grad_norm_one, 0)
    reduce_step(1, 4)

    def back_one(t, carry):
        at = pl.ds(pl.multiple_of(t * LEN, LEN), LEN)
        dv, dg, db = norm_back(ACC[at, :], g1, TOK[t].astype(F32))
        GT[at, :] = (RES[at, :] + dv).astype(LOW)
        return carry[0] + dg, carry[1] + db

    dg, db = lax.fori_loop(0, n_cap, back_one, (zero8, zero8), unroll=7)
    SG[0, 14:15, :] = jnp.sum(dg, axis=0, keepdims=True)
    SG[0, 16:17, :] = jnp.sum(db, axis=0, keepdims=True)
    gt_copy = remote(GT, gt.at[half], gt_s, gt_r, pair_dev)
    stores.append(local(GT, gt.at[half], out_sem.at[3]))

    def attend_gradient(t, carry):
        i, j = t // 3, lax.rem(t, 3)
        s = m + i * (pair - m)
        IW[i, pl.ds(4 * j, 4)] = dot_tn(QKV[j, s], N1[...]).astype(LOW).reshape(4, PIECE, width)
        return carry

    lax.fori_loop(0, 6, attend_gradient, 0)
    reduce_step(0, 0)

    def bias_gradient(s, carry):
        SG[0, pl.ds(s, 1), 0:shard] = dot(ones, QKV[0, s])[0:1]
        SG[0, pl.ds(4 + s, 1), 0:shard] = dot(ones, QKV[2, s])[0:1]
        return carry

    lax.fori_loop(0, n_mp, bias_gradient, 0)
    reduce_step(1, 5)

    small_devs = [core_dev, y_dev, x_dev, pair_dev] + [(flip(d, 3 + x), m) for x in range(extra)]
    small = {}

    def small_start(i):
        small[i] = remote(SG.at[i], SGR.at[i], sg_s.at[i], sg_r.at[i], small_devs[i])

    def small_end(i):
        small[i].wait_recv()
        SG[i + 1] = SG[i] + SGR[i]

    small_start(0)
    reduce_step(0, 1)
    small_end(0)
    small_start(1)
    reduce_step(1, 6)
    reduce_step(0, 2)
    small_end(1)
    small_start(2)
    reduce_step(0, 3)
    small_end(2)
    small_start(3)
    reduce_step(0, 4)
    small_end(3)
    for i in range(4, 4 + extra):
        small_start(i)
        small_end(i)
    reduce_step(0, 5)
    reduce_step(0, 6)
    last = SG.shape[0] - 1
    sgo[...] = jnp.zeros_like(sgo)
    sgo[0:1, :] = SG[last, pl.ds(m, 1), :]
    sgo[1:2, :] = SG[last, pl.ds(4 + m, 1), :]
    sgo[2:3, :] = SG[last, pl.ds(8 + m, 1), :]
    sgo[3:10, :] = SG[last, 12:19, :]
    sgo[10:11, :] = jnp.broadcast_to(loss, (1, width))
    for g in range(3):
        reduce_step(g, 7)
    gt_copy.wait_recv()
    pltpu.make_async_copy(EMB.at[pl.ds(0, n_all - 1)], EMB.at[pl.ds(0, n_all - 1)], emb_s).wait()
    pltpu.make_async_copy(STATS.at[pl.ds(0, 15)], STATS.at[pl.ds(0, 15)], st_s).wait()
    for copy in sends:
        copy.wait_send()
    for copy in stores:
        copy.wait()


def local_step(
    n_dp,
    n_mp,
    caption_tokens,
    image_tokens,
    image_attend,
    image_output,
    image_expand,
    image_reduce,
    image_gains,
    caption_attend,
    attend_bias,
    caption_output,
    output_bias,
    caption_expand,
    expand_bias,
    caption_reduce,
    reduce_bias,
    norm_gains,
    norm_shifts,
    log_scale,
    caption_image,
):
    captions, length, width = caption_tokens.shape
    images, image_len, _ = image_tokens.shape
    shard = caption_attend.shape[2]
    units = caption_expand.shape[1]
    n_cap = captions // 2
    rows = n_cap * length
    n_blocks = rows // BLOCK
    n_all = n_dp * n_mp
    t_all = n_all * 8
    extra = n_dp.bit_length() - 1 - 3
    assert length == LEN and units == width and shard * n_mp == width and width == 16 * PIECE

    def pieces(a):
        return a.reshape(a.shape[:-2] + (16, PIECE, a.shape[-1]))

    wao = pieces(
        jnp.concatenate(
            [jnp.swapaxes(caption_attend, 1, 2).reshape(3 * shard, width), caption_output], axis=0
        )
    )

    def row(a):
        return jnp.pad(a.reshape(1, -1), ((0, 0), (0, width - a.size)))

    zero_row = jnp.zeros((1, width), F32)
    par = jnp.concatenate(
        [
            image_gains,
            row(output_bias),
            row(reduce_bias),
            norm_gains,
            norm_shifts,
            row(attend_bias[0]),
            zero_row,
            row(attend_bias[1]),
            row(expand_bias),
            row(log_scale),
            zero_row,
            zero_row,
            zero_row,
        ],
        axis=0,
    )
    cap = jnp.pad(
        caption_image.reshape(2, n_cap, 1), ((0, 0), (0, 64 - n_cap), (0, 0)), constant_values=-1
    )
    any_space = pl.BlockSpec(memory_space=pl.ANY)
    vmem = pl.BlockSpec(memory_space=pltpu.VMEM)
    nx = max(extra, 1)
    dma = pltpu.SemaphoreType.DMA
    scratch = [
        pltpu.VMEM((3, n_mp, 16, PIECE, width), LOW),
        pltpu.VMEM((8, 16, PIECE, width), LOW),
        pltpu.VMEM((n_cap, length, width), LOW),
        pltpu.VMEM((rows, width), LOW),
        pltpu.VMEM((3, n_mp, rows, shard), LOW),
        pltpu.VMEM((n_mp, n_blocks, 3 * BLOCK, BLOCK), LOW),
        pltpu.VMEM((n_mp, rows, shard), LOW),
        pltpu.VMEM((rows, width), F32),
        pltpu.VMEM((rows, width), LOW),
        pltpu.VMEM((n_mp, rows, width), LOW),
        pltpu.VMEM((n_mp, 64, width), LOW),
        pltpu.VMEM((rows, width), F32),
        pltpu.VMEM((rows, width), LOW),
        pltpu.VMEM((rows, width), LOW),
        pltpu.VMEM((16, width), F32),
        pltpu.VMEM((n_all, 8, width), LOW),
        pltpu.VMEM((8, t_all), F32),
        pltpu.VMEM((16, 8, t_all), F32),
        pltpu.VMEM((n_mp, 8, width), F32),
        pltpu.VMEM((3 * BLOCK, shard), LOW),
        pltpu.VMEM((3 * BLOCK, BLOCK), F32),
        pltpu.VMEM((256, 256), LOW),
        pltpu.VMEM((64, rows), LOW),
        pltpu.VMEM((64, width), F32),
        pltpu.VMEM((2, 64, width), LOW),
        pltpu.VMEM((n_mp, 64, width), F32),
        pltpu.VMEM((2, 2, 2, 4, PIECE, width), LOW),
        pltpu.VMEM((2, 2, 2, 2, PIECE, width), LOW),
        pltpu.VMEM((2, 2, 2, 1, PIECE, width), LOW),
        pltpu.VMEM((3, 2, 1, PIECE, width), LOW),
        pltpu.VMEM((2, nx, 2, 1, PIECE, width), LOW),
        pltpu.VMEM((2, nx, 8, t_all), F32),
        pltpu.VMEM((5 + extra, 24, width), F32),
        pltpu.VMEM((4 + extra, 24, width), F32),
        dma((3, 3, 2)),
        dma((3, 3, 2)),
        dma((3, 3, 3, 2)),
        dma((3, 3, 3, 2)),
        dma((3,)),
        dma((12,)),
        dma,
        dma((3,)),
        dma((3,)),
        dma,
        dma,
        dma,
        dma,
        dma((nx,)),
        dma((nx,)),
        dma((3, 4, 4)),
        dma((3, 4, 4)),
        dma((3, 3, 2)),
        dma((3, 3, 2)),
        dma((3, nx, 2)),
        dma((3, nx, 2)),
        dma((4 + extra,)),
        dma((4 + extra,)),
        dma,
        dma,
        dma((4,)),
    ]
    red, gt, sgo = pl.pallas_call(
        functools.partial(body, n_dp, n_mp),
        out_shape=(
            jax.ShapeDtypeStruct((3, 16, PIECE, width), LOW),
            jax.ShapeDtypeStruct((2, rows, width), LOW),
            jax.ShapeDtypeStruct((16, width), F32),
        ),
        in_specs=[any_space, vmem] + [any_space] * 7 + [vmem, vmem],
        out_specs=(any_space, any_space, vmem),
        scratch_shapes=scratch,
        compiler_params=pltpu.CompilerParams(
            collective_id=0, has_side_effects=True, vmem_limit_bytes=66_000_000
        ),
        name="step",
    )(
        caption_tokens,
        image_tokens,
        pieces(image_attend),
        pieces(image_output),
        pieces(image_expand),
        image_reduce.reshape(-1, 16, PIECE, width),
        wao,
        pieces(caption_expand),
        pieces(caption_reduce),
        par,
        cap,
    )
    red = red.astype(F32).reshape(3, width, width)
    gradient_attend = jnp.swapaxes(red[0, : 3 * shard].reshape(3, shard, width), 1, 2)
    return (
        sgo[10, 0:1],
        gt.astype(F32).reshape(captions, length, width),
        gradient_attend,
        sgo[0:2, :shard],
        red[0, 3 * shard :],
        sgo[3],
        red[1],
        sgo[2],
        red[2],
        sgo[4],
        sgo[5:7],
        sgo[7:9],
        sgo[9, 0:1],
    )


def solution(mesh):
    in_specs = (
        P("dp", None, None),
        P(("dp", "mp"), None, None),
        P(),
        P(),
        P(),
        P(),
        P(),
        P(None, None, "mp"),
        P(None, "mp"),
        P("mp", None),
        P(),
        P(None, "mp"),
        P("mp"),
        P("mp", None),
        P(),
        P(),
        P(),
        P(),
        P("dp"),
    )
    out_specs = (
        P(),
        P("dp", None, None),
        P(None, None, "mp"),
        P(None, "mp"),
        P("mp", None),
        P(),
        P(None, "mp"),
        P("mp"),
        P("mp", None),
        P(),
        P(),
        P(),
        P(),
    )
    step = functools.partial(local_step, mesh.shape["dp"], mesh.shape["mp"])
    return jax.shard_map(step, mesh=mesh, in_specs=in_specs, out_specs=out_specs, check_vma=False)
```

time: 607 us -> 230 us (0.38); the launches traced: 598 us -> 228 us
  waiting for transfers between devices: 290 us -> 0 us
  Pallas kernels: 0 us -> 202 us
  other arithmetic: 90.2 us -> 8.13 us
  matrix products: 80.7 us -> 0 us
  blocking collectives: 57.5 us -> 0 us
  local copies, waits for them, and re-layouts: 60.7 us -> 16.7 us
  between operations: 18.3 us -> 1.36 us
    psum x5 -> x0, waiting for transfers between devices: 290 us -> none  [the longest x1 92.7 us: local(): lax.psum(partial_normed.astype(jnp.bfloat16), 'mp').astype(jnp.float32)]
    pallas_call x0 -> x1, Pallas kernels: none -> 202 us  [local_step(): pl.pallas_call(functools.partial(body, n_dp, n_mp), out_shape=(jax.ShapeD...]
    dot_general x34 -> x0, matrix products: 80.7 us -> none  [the longest x13 37.7 us: matmul(): return jnp.dot(left_side, right_side, preferred_element_type=jnp.float32)]
    reduce_sum x23 -> x0, other arithmetic: 47.5 us -> none  [the longest x5 11.8 us: norm_rows(): centred = values - jnp.mean(values, axis=-1, keepdims=True)]
    reshape x19 -> x4, local copies, waits for them, and re-layouts: 36.5 us -> 2.23 us  [the longest x3 2.07 us: row(): return jnp.pad(a.reshape(1, -1), ((0, 0), (0, width - a.size)))]
    all_gather x3 -> x0, blocking collectives: 32.9 us -> none  [the longest x1 13.3 us: local(): group_images = lax.all_gather(local_embed, 'mp', axis=0, tiled=True)]
    psum x1 -> x0, blocking collectives: 24.6 us -> none  [local(): lax.psum((gradient_attend_bias, gradient_output_bias, gradient_expand_bia...]
    convert_element_type x10 -> x0, local copies, waits for them, and re-layouts: 13.6 us -> none  [the longest x1 2.61 us: image_block(): mixture = contract('bhqk,bkhd->bqhd', weights, valueset).astype(jnp.bfloa...]
  transfers between devices with their start and end apart: 5 -> 0, of which waited for: 5 -> 0; matrix products, arithmetic and copies ran while one was open for 14% -> 0% of each run, Pallas kernels for 0% -> 0%
where the time goes in v2:
time: 230 us; the launch traced here: 228 us
  Pallas kernels  202 us (88%)
  local copies, waits for them, and re-layouts  16.7 us (7%)
  other arithmetic  8.13 us (4%)
    pallas_call x1, Pallas kernels, local_step(): pl.pallas_call(functools.partial(body, n_dp, n_mp), out_shape=(jax.ShapeD...  202 us

profile of v2, /device:TPU:0, one launch (start us, length us, event | category | flops | bytes accessed | tf_op | source)
XLA Modules:
  0.0 228.1 jit_solution(11033983469737062025)
XLA Ops:
  0.6 0.0 copy-start.2
  0.7 0.8 fusion.3
  2.1 0.7 reshape.86
  2.8 0.7 reshape.87
  3.5 0.7 reshape.88
  4.2 2.0 concatenate.11.par
  6.2 2.4 %pad_maximum_fusion = bf16[768,768]{1,0:T(8,128)(2,1)} fusion(bf16[192,768]{1,0:T(8,128)(2,1)} %param.28, bf16[576,768]{1,0:T(8,128)(2,1)} %bitcast.37), kind=kLoop, calls=%fused_computation | loop fusion | flops 2359296 | bytes 2359296 | tf_op jit(solution)/shard_map/concatenate | solution.py:993
  8.5 0.0 copy-done.2
  8.5 0.2 reshape.96
  8.7 0.6 pad.18.cap
  9.3 201.9 %step.1 = (bf16[3,16,48,768]{3,2,1,0:T(8,128)(2,1)}, bf16[2,784,768]{2,1,0:T(8,128)(2,1)}, f32[16,768]{1,0:T(8,128)}) custom-call(bf16[98,16,768]{2,1,0:T(8,128)(2,1)} %tok_in.1, bf16[7,50,768]{2,1,0:T(8,128)(2,1)} %imt.1, bf16[3,16,48,768]{3,2,1,0:T(8,128)(2,1)} %bitcast.29, bf16[16,48,768]{2,1,0:T(8,128)(2,1)} %bitcast.34, bf16[16,48,3072]{2,1,0:T(8,128)(2,1)} %bitcast.26, ...), custom_call_target="tpu_custom_call" | custom-call | tf_op jit(solution)/shard_map/step/pallas_call | solution.py:1089
  211.2 1.5 slice_reduce_fusion
  212.7 1.4 fusion.2
  214.1 1.3 fusion.1
  215.4 1.3 slice.48
  216.7 2.9 %convert_element_type.9 = f32[3,16,48,768]{3,2,1,0:T(8,128)S(1)} convert(bf16[3,16,48,768]{3,2,1,0:T(8,128)(2,1)} %get-tuple-element.18) | non-fusion elementwise | flops 1769472 | bytes 10616832 | tf_op jit(solution)/shard_map/convert_element_type | solution.py:1116
  219.6 0.0 copy-start
  219.6 1.3 slice.58
  220.9 0.9 slice_bitcast_fusion
  221.8 0.7 copy-done
  222.4 0.0 copy-start.1
  222.4 2.8 %fusion = (f32[1,16,48,768]{3,2,1,0:T(8,128)}, f32[1,16,48,768]{3,2,1,0:T(8,128)}) fusion(bf16[3,16,48,768]{3,2,1,0:T(8,128)(2,1)S(1)} %copy-done), kind=kLoop, calls=%fused_computation.5 | loop fusion | bytes 9437184 | tf_op jit(solution)/shard_map/slice | solution.py:1127
  225.2 0.0 copy-done.1
  225.2 2.9 %convert.1 = f32[98,16,768]{2,1,0:T(8,128)} convert(bf16[98,16,768]{2,1,0:T(8,128)(2,1)S(1)} %bitcast.30) | non-fusion elementwise | flops 1204224 | bytes 7225344 | tf_op jit(solution)/shard_map/reshape | solution.py:1120
  (5 shorter events, 0.0 us)
Async XLA Ops:
  0.6 7.9 %copy-start.2 = (s32[98]{0:T(128)S(1)}, s32[98]{0:T(128)}, u32[]{:S(2)}) copy-start(s32[98]{0:T(128)} %param.37) | copy-start | bytes 1180
  219.6 2.9 %copy-start = (bf16[3,16,48,768]{3,2,1,0:T(8,128)(2,1)S(1)}, bf16[3,16,48,768]{3,2,1,0:T(8,128)(2,1)}, u32[]{:S(2)}) copy-start(bf16[3,16,48,768]{3,2,1,0:T(8,128)(2,1)} %get-tuple-element.18) | copy-start | bytes 10616836
  222.4 2.8 %copy-start.1 = (bf16[2,784,768]{2,1,0:T(8,128)(2,1)S(1)}, bf16[2,784,768]{2,1,0:T(8,128)(2,1)}, u32[]{:S(2)}) copy-start(bf16[2,784,768]{2,1,0:T(8,128)(2,1)} %get-tuple-element.17) | copy-start | bytes 7225348

commit v3 on v2

v3 whole, which is shorter than its diff:
```python
import functools

import jax
import jax.numpy as jnp
from jax import lax
from jax.experimental import pallas as pl
from jax.experimental.pallas import tpu as pltpu
from jax.sharding import PartitionSpec as P

HEAD_DIM = 64
LEN = 16
PIECE = 48
BLOCK = 112
F32 = jnp.float32
LOW = jnp.bfloat16
FAR = -1e30
GELU_A = 0.7978845608028654
GELU_B = 0.044715


def dot(a, b):
    return lax.dot_general(a, b, (((1,), (0,)), ((), ())), preferred_element_type=F32)


def dot_nt(a, b):
    return lax.dot_general(a, b, (((1,), (1,)), ((), ())), preferred_element_type=F32)


def dot_tn(a, b):
    return lax.dot_general(a, b, (((0,), (0,)), ((), ())), preferred_element_type=F32)


def iota(shape, axis):
    return lax.broadcasted_iota(jnp.int32, shape, axis)


def standard(x):
    width = x.shape[-1]
    centred = x - jnp.sum(x, axis=-1, keepdims=True) * (1.0 / width)
    variance = jnp.sum(centred * centred, axis=-1, keepdims=True) * (1.0 / width)
    scale = lax.rsqrt(variance + 1e-6)
    return centred * scale, scale


def gelu_parts(h):
    square = h * h
    t = jnp.tanh(GELU_A * h * (1.0 + GELU_B * square))
    half = 0.5 * (1.0 + t)
    slope = half + 0.5 * h * (1.0 - t * t) * (GELU_A * (1.0 + 3.0 * GELU_B * square))
    return h * half, slope


def sum8(x):
    return x[0:8] + x[8:16]


def body(
    n_dp,
    n_mp,
    tok_in,
    imt,
    ia_in,
    io_in,
    ie_in,
    ir_in,
    ca_in,
    co_in,
    we_in,
    wr_in,
    image_gains,
    attend_bias,
    output_bias,
    expand_bias,
    reduce_bias,
    norm_gains,
    norm_shifts,
    log_scale,
    cap,
    red,
    gt,
    sgo,
    W,
    IW,
    TOK,
    N1,
    QKV,
    PR,
    MIX,
    RES,
    N2,
    GP,
    PA,
    ACC,
    GRL,
    GT,
    IP,
    EMB,
    MSG,
    STATS,
    SBL,
    SB,
    HM3,
    BM,
    HM4,
    POOL,
    EL,
    GPL,
    GA,
    RCORE,
    RB1,
    RB2,
    RZ,
    XR,
    XST,
    SG,
    SGR,
    gz_s,
    gz_r,
    ga_s,
    ga_r,
    loc_sem,
    ca_sem,
    iw_sem,
    tok_sem,
    sb_s,
    sb_r,
    emb_s,
    emb_r,
    st_s,
    st_r,
    stx_s,
    stx_r,
    rs_s,
    rs_r,
    ag_s,
    ag_r,
    xr_s,
    xr_r,
    sg_s,
    sg_r,
    gt_s,
    gt_r,
    out_sem,
):
    d = lax.axis_index("dp")
    m = lax.axis_index("mp")
    n_all = n_dp * n_mp
    me = d * n_mp + m
    bits = n_dp.bit_length() - 1
    extra = bits - 3
    images, image_len = imt.shape[0], imt.shape[1]
    rows = TOK.shape[0] * LEN
    n_cap = TOK.shape[0]
    n_blocks = rows // BLOCK
    width = RES.shape[1]
    shard = QKV.shape[3]
    image_rows = images * 64
    t_all = EMB.shape[0] * 8
    total_images = images * n_all
    total_captions = n_cap * 2 * n_dp

    def bit(v, b):
        return lax.rem(v // (1 << b), 2)

    def flip(v, b):
        return v + (1 - 2 * bit(v, b)) * (1 << b)

    cb, xb, yb = bit(d, 0), bit(d, 1), bit(d, 2)
    half = lax.rem(m, 2)
    pair = flip(m, 0)
    p_a = cb * 4 + yb * 2 + xb
    p_b = 8 + cb * 4 + xb * 2 + yb
    core_dev = (flip(d, 0), m)
    x_dev = (flip(d, 1), m)
    y_dev = (flip(d, 2), m)
    pair_dev = (d, pair)
    sends = []

    def remote(src, dst, ss, rs, dev):
        copy = pltpu.make_async_remote_copy(
            src_ref=src,
            dst_ref=dst,
            send_sem=ss,
            recv_sem=rs,
            device_id=dev,
            device_id_type=pl.DeviceIdType.MESH,
        )
        copy.start()
        sends.append(copy)
        return copy

    def local(src, dst, sem):
        copy = pltpu.make_async_copy(src, dst, sem)
        copy.start()
        return copy

    barrier = pltpu.get_barrier_semaphore()

    def greet(k, carry):
        q = lax.rem(me + k, n_all)
        pl.semaphore_signal(
            barrier,
            inc=1,
            device_id=(q // n_mp, lax.rem(q, n_mp)),
            device_id_type=pl.DeviceIdType.MESH,
        )
        return carry

    lax.fori_loop(1, n_all, greet, 0)

    image_loads = {}

    def load_image(i):
        if i < 3:
            src, slot = ia_in.at[i], i
        elif i == 3:
            src, slot = io_in, 3
        elif i < 8:
            src, slot = ie_in.at[:, pl.ds((i - 4) * width, width)], i
        else:
            src, slot = ir_in.at[pl.ds((i - 8) * width, width)], i - 8
        image_loads[i] = local(src, IW.at[slot], iw_sem.at[i])

    ca_copies = [
        local(ca_in.at[j], W.at[0, m, pl.ds(shard * j, shard)], ca_sem.at[j]) for j in range(3)
    ]
    own_loads = [local(co_in, W.at[0, m, pl.ds(3 * shard, shard)], loc_sem.at[0])]
    SBL[...] = jnp.zeros_like(SBL)
    SBL[0:1, 0:shard] = attend_bias[0:1, :]
    SBL[2:3, 0:shard] = attend_bias[1:2, :]
    SBL[3:4, :] = expand_bias[...].reshape(1, width)
    SB[m] = SBL[...]
    for copy in ca_copies + own_loads[0:1]:
        copy.wait()
    pl.semaphore_wait(barrier, n_all - 1)

    hops = (1, 2, 3)

    def partner(k):
        other = flip(m, 0) if k % 2 else m
        return flip(other, 1) if k >= 2 else other

    zc, ac = {}, {}
    sources = (W.at[0, m], we_in, wr_in)

    def span(p, n):
        return pl.ds(pl.multiple_of(p * PIECE, 16), n * PIECE)

    def gather_z(g):
        for k in hops:
            dev = (d, partner(k))
            for ab, p in ((0, p_a), (1, p_b)):
                zc[g, k, ab] = remote(
                    sources[g].at[span(p, 1)],
                    W.at[g, m, span(p, 1)],
                    gz_s.at[g, k - 1, ab],
                    gz_r.at[g, k - 1, ab],
                    dev,
                )

    def spread(at, stage, ab, ss, rs):
        if stage == 0:
            p, n, dev = ((p_a, 1, x_dev), (p_b, 1, y_dev))[ab]
        elif stage == 1:
            p, n, dev = ((cb * 4 + yb * 2, 2, y_dev), (8 + cb * 4 + xb * 2, 2, x_dev))[ab]
        else:
            p, n, dev = 8 * ab + cb * 4, 4, core_dev
        return remote(at(p, n), at(p, n), ss.at[stage, ab], rs.at[stage, ab], dev)

    def gather_start(g, stage):
        for k in hops:
            source = partner(k)
            for ab in range(2):
                (zc[g, k, ab] if stage == 0 else ac[g, stage - 1, k, ab]).wait_recv()
                ac[g, stage, k, ab] = spread(
                    lambda p, n: W.at[g, source, span(p, n)],
                    stage,
                    ab,
                    ga_s.at[g, k - 1],
                    ga_r.at[g, k - 1],
                )

    def gather_end(g):
        for k in hops:
            for ab in range(2):
                ac[g, 2, k, ab].wait_recv()
        if g > 0:
            own_loads[g].wait()

    gather_z(0)
    sb_copies = []
    for k in hops:
        sb_copies.append(
            remote(
                SBL,
                SB.at[m],
                sb_s.at[k - 1],
                sb_r.at[k - 1],
                (d, partner(k)),
            )
        )
    for i in range(3):
        load_image(i)
    tok_copy = local(tok_in.at[pl.ds(half * n_cap, n_cap)], TOK, tok_sem)
    for i in range(3, 8):
        load_image(i)
    own_loads.append(local(we_in, W.at[1, m], loc_sem.at[1]))
    own_loads.append(local(wr_in, W.at[2, m], loc_sem.at[2]))
    row_block = iota((BLOCK, BLOCK), 0) >> 4
    near = jnp.where(row_block == (iota((BLOCK, BLOCK), 1) >> 4), 0.0, FAR)
    lane_shard = iota((BLOCK, shard), 1) >> 6
    for h in range(3):
        at = slice(h * BLOCK, (h + 1) * BLOCK)
        HM3[at, :] = jnp.where(lane_shard == h, 1.0, 0.0).astype(LOW)
        BM[at, :] = near
    lane_four = iota((64, 256), 1) >> 6
    for h in range(4):
        HM4[64 * h : 64 * h + 64, :] = jnp.where(lane_four == h, 1.0, 0.0).astype(LOW)
    POOL[...] = jnp.where((iota(POOL.shape, 1) >> 4) == iota(POOL.shape, 0), 1.0, 0.0).astype(LOW)
    RES[pl.ds(0, image_rows), :] = jnp.zeros((image_rows, width), F32)
    GP[3, pl.ds(0, image_rows), :] = jnp.zeros((image_rows, width), LOW)
    gain_one = image_gains[0:1, :]
    gain_two = image_gains[1:2, :]

    def image_norm(i, carry):
        x = imt[i].astype(F32)
        at = pl.multiple_of(i * 64, 64)
        RES[pl.ds(at, image_len), :] = x
        GP[3, pl.ds(at, image_len), :] = (standard(x)[0] * gain_one).astype(LOW)
        return carry

    lax.fori_loop(0, images, image_norm, 0)
    for i in range(3):
        image_loads[i].wait()

    def image_qkv(j, carry):
        GP[j, pl.ds(0, image_rows), :] = dot(
            GP[3, pl.ds(0, image_rows), :], IW[j]
        ).astype(LOW)
        return carry

    lax.fori_loop(0, 3, image_qkv, 0)
    for i in range(8, 11):
        load_image(i)
    gather_start(0, 0)
    gather_z(1)

    key_valid = jnp.where(iota((256, 64), 1) < image_len, 0.0, FAR)
    lane_head = iota((64, 256), 1) >> 6

    def image_attention(i, carry):
        at = pl.multiple_of(i * 64, 64)
        for n in range(width // 256):
            lanes = slice(256 * n, 256 * n + 256)
            q = GP[0, pl.ds(at, 64), lanes]
            k = GP[1, pl.ds(at, 64), lanes]
            v = GP[2, pl.ds(at, 64), lanes]
            logits = dot_nt(jnp.concatenate([q] * 4, axis=0) * HM4[...], k) * 0.125 + key_valid
            expos = jnp.exp(logits - jnp.max(logits, axis=-1, keepdims=True))
            probs = (expos * (1.0 / jnp.sum(expos, axis=-1, keepdims=True))).astype(LOW)
            o = dot(probs, v)
            mix = jnp.where(
                lane_head < 2,
                jnp.where(lane_head == 0, o[0:64], o[64:128]),
                jnp.where(lane_head == 2, o[128:192], o[192:256]),
            )
            N2[pl.ds(at, 64), lanes] = mix.astype(LOW)
        return carry

    lax.fori_loop(0, images, image_attention, 0)
    gather_start(0, 1)
    image_loads[3].wait()

    def image_out(n, carry):
        lanes = pl.ds(pl.multiple_of(n * 256, 256), 256)
        RES[pl.ds(0, image_rows), lanes] += dot(
            N2[pl.ds(0, image_rows), :], IW[3, :, lanes]
        )
        return carry

    lax.fori_loop(0, width // 256, image_out, 0)
    load_image(11)

    def image_norm_two(t, carry):
        at = pl.ds(pl.multiple_of(t * 16, 16), 16)
        GP[3, at, :] = (standard(RES[at, :])[0] * gain_two).astype(LOW)
        return carry

    lax.fori_loop(0, image_rows // 16, image_norm_two, 0, unroll=4)
    IP[...] = jnp.zeros_like(IP)
    for i in range(images):
        IP[i : i + 1, :] = jnp.sum(RES[64 * i : 64 * i + image_len, :], axis=0, keepdims=True) * (
            1.0 / image_len
        )
    image_pool = jnp.where(
        ((iota((16, image_rows), 1) >> 6) == iota((16, image_rows), 0))
        & ((iota((16, image_rows), 1) & 63) < image_len),
        1.0,
        0.0,
    ).astype(LOW)
    for i in range(4, 12):
        image_loads[i].wait()

    def image_feed(u, carry):
        ACC[pl.ds(0, image_rows), :] = dot(
            GP[3, pl.ds(0, image_rows), :], IW[4 + u]
        )

        def activate(t, inner):
            at = pl.ds(pl.multiple_of(t * 16, 16), 16)
            h = ACC[at, :]
            act = 0.5 * h * (1.0 + jnp.tanh(GELU_A * h * (1.0 + GELU_B * h * h)))
            N2[at, :] = act.astype(LOW)
            return inner

        lax.fori_loop(0, image_rows // 16, activate, 0, unroll=4)
        pooled = (dot(image_pool, N2[pl.ds(0, image_rows), :]) * (1.0 / image_len)).astype(LOW)
        IP[...] += dot(pooled, IW[u])
        return carry

    lax.fori_loop(0, 2, image_feed, 0)
    gather_start(1, 0)
    gather_z(2)
    gather_start(0, 2)
    lax.fori_loop(2, 4, image_feed, 0)
    pooled_image = IP[0:8]
    EMB[me] = (
        pooled_image
        * lax.rsqrt(jnp.sum(pooled_image * pooled_image, axis=-1, keepdims=True) + 1e-6)
    ).astype(LOW)

    def send_embed(k, carry):
        q = lax.rem(me + k, n_all)
        pltpu.make_async_remote_copy(
            src_ref=EMB.at[me],
            dst_ref=EMB.at[me],
            send_sem=emb_s,
            recv_sem=emb_r,
            device_id=(q // n_mp, lax.rem(q, n_mp)),
            device_id_type=pl.DeviceIdType.MESH,
        ).start()
        return carry

    lax.fori_loop(1, n_all, send_embed, 0)

    tok_copy.wait()
    g1, g2 = norm_gains[0:1, :], norm_gains[1:2, :]
    b1, b2 = norm_shifts[0:1, :], norm_shifts[1:2, :]

    def norm_one(t, carry):
        at = pl.ds(pl.multiple_of(t * LEN, LEN), LEN)
        N1[at, :] = (standard(TOK[t].astype(F32))[0] * g1 + b1).astype(LOW)
        return carry

    lax.fori_loop(0, n_cap, norm_one, 0, unroll=7)
    for copy in sb_copies:
        copy.wait_recv()
    gather_end(0)

    def project(t, carry):
        s, j = t // 3, lax.rem(t, 3)
        weight = W[0, s, pl.ds(pl.multiple_of(shard * j, 16), shard), :]
        QKV[j, s] = (dot_nt(N1[...], weight) + SB[s, pl.ds(j, 1), 0:shard]).astype(LOW)
        return carry

    gather_start(1, 1)
    lax.fori_loop(0, 3 * n_mp, project, 0)
    gather_start(2, 0)
    lane_three = iota((BLOCK, shard), 1) >> 6

    def join_heads(o):
        return jnp.where(
            lane_three == 0,
            o[0:BLOCK],
            jnp.where(lane_three == 1, o[BLOCK : 2 * BLOCK], o[2 * BLOCK : 3 * BLOCK]),
        )

    def attention(b, carry):
        at = pl.ds(pl.multiple_of(b * BLOCK, 16), BLOCK)
        loaded = [[QKV[j, s, at, :] for j in range(3)] for s in range(n_mp)]
        heads, mask = HM3[...], BM[...]
        every = []
        for q, k, v in loaded:
            logits = dot_nt(jnp.concatenate([q] * 3, axis=0) * heads, k) * 0.125 + mask
            expos = jnp.exp(logits - jnp.max(logits, axis=-1, keepdims=True))
            probs = (expos * (1.0 / jnp.sum(expos, axis=-1, keepdims=True))).astype(LOW)
            every.append((probs, join_heads(dot(probs, v)).astype(LOW)))
        for s, (probs, mixed) in enumerate(every):
            PR[s, b] = probs
            MIX[s, at, :] = mixed
        return carry

    lax.fori_loop(0, n_blocks // 2, attention, 0)
    gather_start(1, 2)
    lax.fori_loop(n_blocks // 2, n_blocks, attention, 0)
    gather_start(2, 1)

    def attend_out(n, carry):
        lanes = pl.ds(pl.multiple_of(n * 256, 256), 256)
        total = dot(MIX[0], W[0, 0, pl.ds(3 * shard, shard), lanes])
        for s in range(1, n_mp):
            total += dot(MIX[s], W[0, s, pl.ds(3 * shard, shard), lanes])
        ACC[:, lanes] = total
        return carry

    lax.fori_loop(0, width // 256, attend_out, 0)
    out_bias = output_bias[...].reshape(1, width)

    def norm_two(t, carry):
        at = pl.ds(pl.multiple_of(t * LEN, LEN), LEN)
        x = TOK[t].astype(F32) + (ACC[at, :] + out_bias)
        RES[at, :] = x
        N2[at, :] = (standard(x)[0] * g2 + b2).astype(LOW)
        return carry

    lax.fori_loop(0, n_cap, norm_two, 0, unroll=7)
    gather_end(1)

    def feed(s, carry):
        ACC[...] = dot(N2[...], W[1, s])
        bias = SB[s, 3:4, :]

        def activate(t, inner):
            at = pl.ds(pl.multiple_of(t * LEN, LEN), LEN)
            act, slope = gelu_parts(ACC[at, :] + bias)
            GT[at, :] = act.astype(LOW)
            GP[s, at, :] = slope.astype(LOW)
            return inner

        lax.fori_loop(0, n_cap, activate, 0, unroll=7)
        PA[s] = (dot(POOL[...], GT[...]) * (1.0 / LEN)).astype(LOW)
        return carry

    lax.fori_loop(0, 2, feed, 0)
    gather_start(2, 2)
    lax.fori_loop(2, n_mp, feed, 0)

    def pool_residual(n, carry):
        lanes = pl.ds(pl.multiple_of(n * 128, 128), 128)
        res = RES[:, lanes]
        res_high = res.astype(LOW)
        res_low = (res - res_high.astype(F32)).astype(LOW)
        EL[:, lanes] = (dot(POOL[...], res_high) + dot(POOL[...], res_low)) * (1.0 / LEN)
        return carry

    lax.fori_loop(0, width // 128, pool_residual, 0)
    pooled = EL[...] + reduce_bias[...].reshape(1, width)
    gather_end(2)
    for s in range(n_mp):
        pooled += dot(PA[s], W[2, s])
    inverse = lax.rsqrt(jnp.sum(pooled * pooled, axis=-1, keepdims=True) + 1e-6)
    embed = pooled * inverse
    EL[...] = embed

    pltpu.make_async_copy(EMB.at[pl.ds(0, n_all - 1)], EMB.at[pl.ds(0, n_all - 1)], emb_r).wait()
    group = min(n_all, 32)

    def embeds(c):
        part = EMB[c * group : c * group + group].astype(F32)
        return part.reshape(group * 8, width).astype(LOW)

    scaling = jnp.exp(log_scale[...].reshape(1, 1))
    embed_low = embed.astype(LOW)
    scores = scaling * jnp.concatenate(
        [dot_nt(embed_low, embeds(c)) for c in range(n_all // group)], axis=1
    )
    cap_rows = scores.shape[0]
    column = iota((cap_rows, t_all), 1)
    col_ok = (column & 7) < images
    row_ok = iota((cap_rows, t_all), 0) < n_cap
    image_id = (column >> 3) * images + (column & 7)
    cap_wide = jnp.broadcast_to(cap[...].reshape(1, 2 * n_cap).astype(F32), (cap_rows, 2 * n_cap))
    mine = iota((cap_rows, 2 * n_cap), 1) == iota((cap_rows, 2 * n_cap), 0) + half * n_cap
    cap_column = jnp.sum(jnp.where(mine, cap_wide, 0.0), axis=1, keepdims=True)
    matches = jnp.where((cap_column == image_id.astype(F32)) & col_ok & row_ok, 1.0, 0.0)
    by_row = jnp.where(col_ok, scores, FAR)
    row_top = jnp.max(by_row, axis=1, keepdims=True)
    row_lse = row_top + jnp.log(jnp.sum(jnp.exp(by_row - row_top), axis=1, keepdims=True))
    row_positive = jnp.sum(scores * matches, axis=1, keepdims=True)
    row_part = jnp.sum(
        jnp.where(iota((cap_rows, 1), 0) < n_cap, row_lse - row_positive, 0.0), axis=0, keepdims=True
    )
    by_column = jnp.where(row_ok, scores, FAR)
    top = jnp.max(by_column, axis=0, keepdims=True)
    MSG[...] = jnp.zeros_like(MSG)
    MSG[0:1, :] = top
    MSG[1:2, :] = jnp.sum(jnp.exp(by_column - top), axis=0, keepdims=True)
    MSG[2:3, :] = jnp.sum(scores * matches, axis=0, keepdims=True)
    MSG[3:4, :] = jnp.sum(matches, axis=0, keepdims=True)
    MSG[4:5, :] = jnp.broadcast_to(row_part, (1, t_all))
    low = lax.rem(d, 8)
    slot = low * 2 + half
    STATS[slot] = MSG[...]

    def send_stats(k, carry):
        q = lax.rem(slot + k, 16)
        pltpu.make_async_remote_copy(
            src_ref=MSG,
            dst_ref=STATS.at[slot],
            send_sem=st_s,
            recv_sem=st_r,
            device_id=(d - low + q // 2, m - half + lax.rem(q, 2)),
            device_id_type=pl.DeviceIdType.MESH,
        ).start()
        return carry

    lax.fori_loop(1, 16, send_stats, 0)
    pltpu.make_async_copy(STATS.at[pl.ds(0, 15)], STATS.at[pl.ds(0, 15)], st_r).wait()
    top = jnp.max(STATS[:, 0, :], axis=0, keepdims=True)
    total = jnp.sum(STATS[:, 1, :] * jnp.exp(STATS[:, 0, :] - top), axis=0, keepdims=True)
    positive = jnp.sum(STATS[:, 2, :], axis=0, keepdims=True)
    count = jnp.sum(STATS[:, 3, :], axis=0, keepdims=True)
    row_sum = jnp.sum(STATS[:, 4, :], axis=0, keepdims=True)
    for x in range(extra):
        XST[0, x] = jnp.concatenate(
            [top, total, positive, count, row_sum, jnp.zeros((3, t_all), F32)], axis=0
        )
        remote(
            XST.at[0, x], XST.at[1, x], stx_s.at[x], stx_r.at[x], (flip(d, 3 + x), m)
        ).wait_recv()
        other = XST[1, x]
        joined = jnp.maximum(top, other[0:1])
        total = total * jnp.exp(top - joined) + other[1:2] * jnp.exp(other[0:1] - joined)
        top = joined
        positive = positive + other[2:3]
        count = count + other[3:4]
        row_sum = row_sum + other[4:5]
    ok = col_ok[0:1]
    count = jnp.where(ok, count, 1.0)
    col_lse = top + jnp.log(total)
    column_part = jnp.sum(
        jnp.where(ok, col_lse - positive / count, 0.0), axis=1, keepdims=True
    )
    loss = 0.5 * (row_sum[:, 0:1] * (1.0 / total_captions) + column_part * (1.0 / total_images))
    weight = 0.5 * total_captions / total_images
    grad_scores = 0.5 * (jnp.exp(by_row - row_lse) - matches) + weight * (
        jnp.exp(by_column - col_lse) - matches * (1.0 / count)
    )
    grad_scores = jnp.where(col_ok & row_ok, grad_scores, 0.0)
    grad_log = jnp.sum(
        jnp.sum(grad_scores * scores, axis=1, keepdims=True), axis=0, keepdims=True
    )
    embed = EL[...]
    grad_cosine = (scaling * grad_scores).astype(LOW)
    grad_embed = dot(grad_cosine[:, 0 : group * 8], embeds(0))
    for c in range(1, n_all // group):
        grad_embed += dot(grad_cosine[:, c * group * 8 : (c + 1) * group * 8], embeds(c))
    grad_pooled = (
        grad_embed - embed * jnp.sum(embed * grad_embed, axis=-1, keepdims=True)
    ) * inverse
    SG[0] = jnp.zeros(SG.shape[1:], F32)
    SG[0, 13:14, :] = jnp.sum(grad_pooled, axis=0, keepdims=True)
    SG[0, 18:19, :] = jnp.broadcast_to(grad_log, (1, width))
    GPL[0] = grad_pooled.astype(LOW)
    grad_rows = grad_pooled * (1.0 / LEN)
    EL[...] = grad_rows
    GPL[1] = grad_rows.astype(LOW)

    def part(g, i):
        return IW.at[2 * g + i]

    places = (4, 7, 6)

    def whole(g):
        return IW.at[places[g]]

    def settle(copies):
        for copy in copies:
            copy.wait_send()
        sends[:] = [other for other in sends if all(other is not copy for copy in copies)]

    state = {}
    stores = []
    axis_one = ((yb, y_dev), (xb, x_dev))
    axis_two = ((xb, x_dev), (yb, y_dev))
    own = (p_a, p_b)

    def scatter(g, stage, i, ab):
        bit_one, dev_one = axis_one[ab]
        bit_two, dev_two = axis_two[ab]
        run = 8 * ab + 4 * cb + 2 * bit_one
        if stage == 0:
            p, n, dst, dev = 8 * ab + 4 * (1 - cb), 4, RCORE.at[g % 2, i, ab], core_dev
        elif stage == 1:
            p, n, dst, dev = 8 * ab + 4 * cb + 2 * (1 - bit_one), 2, RB1.at[g % 2, i, ab], dev_one
        elif stage == 2:
            p, n, dst, dev = run + 1 - bit_two, 1, RB2.at[g % 2, i, ab], dev_two
        else:
            p, n, dst, dev = own[ab], 1, RZ.at[g, ab], pair_dev
        k = 2 * i + ab
        state[g, stage, i, ab] = remote(
            part(g, i).at[span(p, n)], dst, rs_s.at[g, stage, k], rs_r.at[g, stage, k], dev
        )

    def add_in(g, stage, i, ab):
        state[g, stage, i, ab].wait_recv()
        run = 8 * ab + 4 * cb
        if stage == 0:
            at, got = span(run, 4), RCORE[g % 2, i, ab]
        elif stage == 1:
            at, got = span(run + 2 * axis_one[ab][0], 2), RB1[g % 2, i, ab]
        else:
            at, got = span(own[ab], 1), RB2[g % 2, i, ab]
        IW[2 * g + i, at, :] = IW[2 * g + i, at, :] + got

    def gather_back(g, stage, ab):
        state[g, "gather", stage, ab] = spread(
            lambda p, n: whole(g).at[span(p, n)], stage, ab, ag_s.at[g], ag_r.at[g]
        )

    def reduce_start(g, ab):
        if g == 0:
            settle([state.pop((2, a, i, ab)) for a in range(4) for i in range(2) if (2, a, i, ab) in state])
        for i in (1, 0):
            scatter(g, 0, i, ab)

    def reduce_step(g, step):
        if step == 0:
            for ab in range(2):
                reduce_start(g, ab)
        elif step < 4:
            for i in (1, 0):
                for ab in range(2):
                    add_in(g, step - 1, i, ab)
                    if step < 3 or i == 1:
                        scatter(g, step, i, ab)
        elif step == 4:
            for ab in range(2):
                state[g, 3, 1, ab].wait_recv()
                at = span(own[ab], 1)
                IW[places[g], at, :] = IW[2 * g, at, :] + RZ[g, ab]
                for x in range(extra):
                    copy = remote(
                        whole(g).at[at],
                        XR.at[g % 2, x, ab],
                        xr_s.at[g, x, ab],
                        xr_r.at[g, x, ab],
                        (flip(d, 3 + x), m),
                    )
                    copy.wait_recv()
                    settle([copy])
                    IW[places[g], at, :] = IW[places[g], at, :] + XR[g % 2, x, ab]
                gather_back(g, 0, ab)
        elif step < 7:
            for ab in range(2):
                state[g, "gather", step - 5, ab].wait_recv()
                gather_back(g, step - 4, ab)
        else:
            for ab in range(2):
                state[g, "gather", 2, ab].wait_recv()
            stores.append(local(whole(g), red.at[g], out_sem.at[g]))

    shards = (m, pair)
    for i in range(2):
        IW[4 + i] = dot_tn(PA[shards[i]], GPL[0]).astype(LOW)
    reduce_step(2, 0)

    def grad_activation(s, carry):
        GA[s] = dot_nt(GPL[1], W[2, s])
        return carry

    lax.fori_loop(0, n_mp, grad_activation, 0)
    reduce_step(2, 1)
    ones = jnp.ones((16, rows), LOW)

    def grad_hidden(s, carry):
        def scale(t, inner):
            at = pl.ds(pl.multiple_of(t * LEN, LEN), LEN)
            GP[s, at, :] = (GP[s, at, :].astype(F32) * GA[s, pl.ds(t, 1), :]).astype(LOW)
            return inner

        lax.fori_loop(0, n_cap, scale, 0, unroll=7)
        SG[0, pl.ds(8 + s, 1), :] = dot(ones, GP[s])[0:1]
        return carry

    lax.fori_loop(0, n_mp, grad_hidden, 0)
    reduce_step(2, 2)

    def expand_gradient(i, carry):
        s = m + i * (pair - m)
        IW[2 + i] = dot_tn(N2[...], GP[s]).astype(LOW)
        return carry

    lax.fori_loop(0, 2, expand_gradient, 0)
    reduce_step(1, 0)
    reduce_step(2, 3)

    def grad_norm_two(n, carry):
        p = pl.ds(pl.multiple_of(n * 384, 128), 384)
        total = dot_nt(GP[0], W[1, 0, p, :])
        for s in range(1, n_mp):
            total += dot_nt(GP[s], W[1, s, p, :])
        ACC[:, pl.ds(pl.multiple_of(n * 384, 128), 384)] = total
        return carry

    lax.fori_loop(0, 2, grad_norm_two, 0)
    reduce_step(1, 1)
    reduce_step(2, 4)

    def norm_back(e, gain, x):
        xhat, scale = standard(x)
        eg = e * gain
        c1 = jnp.sum(eg, axis=-1, keepdims=True) * (1.0 / width)
        c2 = jnp.sum(eg * xhat, axis=-1, keepdims=True) * (1.0 / width)
        return (eg - c1 - xhat * c2) * scale, sum8(e * xhat), sum8(e)

    zero8 = jnp.zeros((8, width), F32)

    def back_two(t, carry):
        dg, db, do = carry
        found = []
        for u in range(7):
            at = pl.ds(pl.multiple_of((7 * t + u) * LEN, LEN), LEN)
            dv, one, two = norm_back(ACC[at, :], g2, RES[at, :])
            g = EL[pl.ds(7 * t + u, 1), :] + dv
            found.append((at, g))
            dg, db, do = dg + one, db + two, do + sum8(g)
        for at, g in found:
            RES[at, :] = g
            GRL[at, :] = g.astype(LOW)
        return dg, db, do

    dg, db, do = lax.fori_loop(0, n_cap // 7, back_two, (zero8, zero8, zero8))
    SG[0, 15:16, :] = jnp.sum(dg, axis=0, keepdims=True)
    SG[0, 17:18, :] = jnp.sum(db, axis=0, keepdims=True)
    SG[0, 12:13, :] = jnp.sum(do, axis=0, keepdims=True)

    for i in range(2):
        IW[i, 3 * shard : 4 * shard, :] = dot_tn(MIX[shards[i]], GRL[...]).astype(LOW)
    reduce_step(1, 2)
    reduce_step(2, 5)

    def grad_mixture(s, carry):
        MIX[s] = dot_nt(GRL[...], W[0, s, pl.ds(3 * shard, shard), :]).astype(LOW)
        return carry

    lax.fori_loop(0, n_mp, grad_mixture, 0)
    reduce_step(2, 6)

    def attention_back(b, carry):
        at = pl.ds(pl.multiple_of(b * BLOCK, 16), BLOCK)
        loaded = [
            [QKV[j, s, at, :] for j in range(3)] + [MIX[s, at, :], PR[s, b]] for s in range(n_mp)
        ]
        heads = HM3[...]
        every = []
        for q, k, v, g, low_probs in loaded:
            q = jnp.concatenate([q] * 3, axis=0) * heads
            g = jnp.concatenate([g] * 3, axis=0) * heads
            probs = low_probs.astype(F32)
            grad_probs = dot_nt(g, v)
            inner = jnp.sum(grad_probs * probs, axis=-1, keepdims=True)
            grad_logits = (probs * (grad_probs - inner)).astype(LOW)
            every.append(
                (
                    (join_heads(dot(grad_logits, k)) * 0.125).astype(LOW),
                    (dot_tn(grad_logits, q) * 0.125).astype(LOW),
                    dot_tn(low_probs, g).astype(LOW),
                )
            )
        for s, grads in enumerate(every):
            for j in range(3):
                QKV[j, s, at, :] = grads[j]
        return carry

    def attend_gradient(j):
        def one(i, carry):
            s = m + i * (pair - m)
            IW[i, shard * j : shard * (j + 1), :] = dot_tn(QKV[j, s], N1[...]).astype(LOW)
            return carry

        lax.fori_loop(0, 2, one, 0)

    small_gain, small_shift = zero8, zero8
    gt_copies = []
    cuts = (0, 4, n_blocks)
    for r in range(2):
        lax.fori_loop(cuts[r], cuts[r + 1], attention_back, 0)
        reduce_step(1, 3 + r)
        if r == 1:
            attend_gradient(2)
            reduce_start(0, 1)
            attend_gradient(0)
            attend_gradient(1)
            reduce_start(0, 0)
        first, last = cuts[r] * (BLOCK // LEN), cuts[r + 1] * (BLOCK // LEN)
        stripe = pl.ds(first * LEN, (last - first) * LEN)

        def grad_norm_one(n, carry):
            lanes = pl.ds(pl.multiple_of(n * 256, 256), 256)
            total = None
            for s in range(n_mp):
                for j in range(3):
                    term = dot(
                        QKV[j, s, stripe, :],
                        W[0, s, pl.ds(shard * j, shard), lanes],
                    )
                    total = term if total is None else total + term
            ACC[stripe, lanes] = total
            return carry

        lax.fori_loop(0, width // 256, grad_norm_one, 0)
        if r == 1:
            reduce_step(0, 1)

        def back_one(t, carry):
            at = pl.ds(pl.multiple_of(t * LEN, LEN), LEN)
            dv, dg, db = norm_back(ACC[at, :], g1, TOK[t].astype(F32))
            GT[at, :] = (RES[at, :] + dv).astype(LOW)
            return carry[0] + dg, carry[1] + db

        small_gain, small_shift = lax.fori_loop(
            first, last, back_one, (small_gain, small_shift), unroll=7
        )
        gt_copies.append(
            remote(GT.at[stripe], gt.at[half, stripe], gt_s.at[r], gt_r.at[r], pair_dev)
        )
    stores.append(local(GT, gt.at[half], out_sem.at[3]))
    reduce_step(0, 2)
    SG[0, 14:15, :] = jnp.sum(small_gain, axis=0, keepdims=True)
    SG[0, 16:17, :] = jnp.sum(small_shift, axis=0, keepdims=True)

    def bias_gradient(s, carry):
        SG[0, pl.ds(s, 1), 0:shard] = dot(ones, QKV[0, s])[0:1]
        SG[0, pl.ds(4 + s, 1), 0:shard] = dot(ones, QKV[2, s])[0:1]
        return carry

    lax.fori_loop(0, n_mp, bias_gradient, 0)
    small_devs = [core_dev, y_dev, x_dev, pair_dev] + [(flip(d, 3 + x), m) for x in range(extra)]
    small = {}

    def small_start(i):
        small[i] = remote(SG.at[i], SGR.at[i], sg_s.at[i], sg_r.at[i], small_devs[i])

    def small_end(i):
        small[i].wait_recv()
        SG[i + 1] = SG[i] + SGR[i]

    small_start(0)
    reduce_step(1, 5)
    small_end(0)
    small_start(1)
    reduce_step(0, 3)
    small_end(1)
    small_start(2)
    reduce_step(1, 6)
    small_end(2)
    small_start(3)
    reduce_step(2, 7)
    reduce_step(0, 4)
    small_end(3)
    for i in range(4, 4 + extra):
        small_start(i)
        small_end(i)
    reduce_step(0, 5)
    reduce_step(1, 7)
    reduce_step(0, 6)
    last = SG.shape[0] - 1
    sgo[...] = jnp.zeros_like(sgo)
    sgo[0:1, :] = SG[last, pl.ds(m, 1), :]
    sgo[1:2, :] = SG[last, pl.ds(4 + m, 1), :]
    sgo[2:3, :] = SG[last, pl.ds(8 + m, 1), :]
    sgo[3:10, :] = SG[last, 12:19, :]
    sgo[10:11, :] = jnp.broadcast_to(loss, (1, width))
    reduce_step(0, 7)
    for copy in gt_copies:
        copy.wait_recv()
    pltpu.make_async_copy(EMB.at[pl.ds(0, n_all - 1)], EMB.at[pl.ds(0, n_all - 1)], emb_s).wait()
    pltpu.make_async_copy(STATS.at[pl.ds(0, 15)], STATS.at[pl.ds(0, 15)], st_s).wait()
    for copy in sends:
        copy.wait_send()
    for copy in stores:
        copy.wait()


def local_step(
    n_dp,
    n_mp,
    caption_tokens,
    image_tokens,
    image_attend,
    image_output,
    image_expand,
    image_reduce,
    image_gains,
    caption_attend,
    attend_bias,
    caption_output,
    output_bias,
    caption_expand,
    expand_bias,
    caption_reduce,
    reduce_bias,
    norm_gains,
    norm_shifts,
    log_scale,
    caption_image,
):
    captions, length, width = caption_tokens.shape
    images, image_len, _ = image_tokens.shape
    shard = caption_attend.shape[2]
    units = caption_expand.shape[1]
    n_cap = captions // 2
    rows = n_cap * length
    n_blocks = rows // BLOCK
    n_all = n_dp * n_mp
    t_all = n_all * 8
    extra = n_dp.bit_length() - 1 - 3
    assert length == LEN and units == width and shard * n_mp == width and width == 16 * PIECE

    any_space = pl.BlockSpec(memory_space=pl.ANY)
    vmem = pl.BlockSpec(memory_space=pltpu.VMEM)
    nx = max(extra, 1)
    dma = pltpu.SemaphoreType.DMA
    scratch = [
        pltpu.VMEM((3, n_mp, width, width), LOW),
        pltpu.VMEM((8, width, width), LOW),
        pltpu.VMEM((n_cap, length, width), LOW),
        pltpu.VMEM((rows, width), LOW),
        pltpu.VMEM((3, n_mp, rows, shard), LOW),
        pltpu.VMEM((n_mp, n_blocks, 3 * BLOCK, BLOCK), LOW),
        pltpu.VMEM((n_mp, rows, shard), LOW),
        pltpu.VMEM((rows, width), F32),
        pltpu.VMEM((rows, width), LOW),
        pltpu.VMEM((n_mp, rows, width), LOW),
        pltpu.VMEM((n_mp, 64, width), LOW),
        pltpu.VMEM((rows, width), F32),
        pltpu.VMEM((rows, width), LOW),
        pltpu.VMEM((rows, width), LOW),
        pltpu.VMEM((16, width), F32),
        pltpu.VMEM((n_all, 8, width), LOW),
        pltpu.VMEM((8, t_all), F32),
        pltpu.VMEM((16, 8, t_all), F32),
        pltpu.VMEM((8, width), F32),
        pltpu.VMEM((n_mp, 8, width), F32),
        pltpu.VMEM((3 * BLOCK, shard), LOW),
        pltpu.VMEM((3 * BLOCK, BLOCK), F32),
        pltpu.VMEM((256, 256), LOW),
        pltpu.VMEM((64, rows), LOW),
        pltpu.VMEM((64, width), F32),
        pltpu.VMEM((2, 64, width), LOW),
        pltpu.VMEM((n_mp, 64, width), F32),
        pltpu.VMEM((2, 2, 2, 4 * PIECE, width), LOW),
        pltpu.VMEM((2, 2, 2, 2 * PIECE, width), LOW),
        pltpu.VMEM((2, 2, 2, PIECE, width), LOW),
        pltpu.VMEM((3, 2, PIECE, width), LOW),
        pltpu.VMEM((2, nx, 2, PIECE, width), LOW),
        pltpu.VMEM((2, nx, 8, t_all), F32),
        pltpu.VMEM((5 + extra, 24, width), F32),
        pltpu.VMEM((4 + extra, 24, width), F32),
        dma((3, 3, 2)),
        dma((3, 3, 2)),
        dma((3, 3, 3, 2)),
        dma((3, 3, 3, 2)),
        dma((3,)),
        dma((3,)),
        dma((12,)),
        dma,
        dma((3,)),
        dma((3,)),
        dma,
        dma,
        dma,
        dma,
        dma((nx,)),
        dma((nx,)),
        dma((3, 4, 4)),
        dma((3, 4, 4)),
        dma((3, 3, 2)),
        dma((3, 3, 2)),
        dma((3, nx, 2)),
        dma((3, nx, 2)),
        dma((4 + extra,)),
        dma((4 + extra,)),
        dma((2,)),
        dma((2,)),
        dma((4,)),
    ]
    red, gt, sgo = pl.pallas_call(
        functools.partial(body, n_dp, n_mp),
        out_shape=(
            jax.ShapeDtypeStruct((3, width, width), LOW),
            jax.ShapeDtypeStruct((2, rows, width), LOW),
            jax.ShapeDtypeStruct((16, width), F32),
        ),
        in_specs=[any_space, vmem] + [any_space] * 8 + [vmem] * 9,
        out_specs=(any_space, any_space, vmem),
        scratch_shapes=scratch,
        compiler_params=pltpu.CompilerParams(
            collective_id=0, has_side_effects=True, vmem_limit_bytes=66_000_000
        ),
        name="step",
    )(
        caption_tokens,
        image_tokens,
        image_attend,
        image_output,
        image_expand,
        image_reduce,
        jnp.swapaxes(caption_attend, 1, 2),
        caption_output,
        caption_expand,
        caption_reduce,
        image_gains,
        attend_bias,
        output_bias,
        expand_bias,
        reduce_bias,
        norm_gains,
        norm_shifts,
        log_scale,
        caption_image,
    )
    shapes = (
        (1,),
        (captions, length, width),
        (3, shard, width),
        (2, shard),
        (shard, width),
        (width,),
        (width, units),
        (units,),
        (units, width),
        (width,),
        (2, width),
        (2, width),
        (1,),
    )
    large = (1, 2, 4, 6, 8)
    parts = 7
    grads = pl.pallas_call(
        finish,
        out_shape=tuple(jax.ShapeDtypeStruct(shape, F32) for shape in shapes),
        in_specs=[any_space, any_space, vmem],
        out_specs=tuple(any_space if i in large else vmem for i in range(len(shapes))),
        scratch_shapes=[
            pltpu.VMEM((captions, length, width), LOW),
            pltpu.VMEM((captions, length, width), F32),
            pltpu.VMEM((3, width, width), LOW),
            pltpu.VMEM((3, width, width), F32),
            pltpu.VMEM((3, shard, width), F32),
            dma((parts,)),
            dma((parts,)),
            dma((3,)),
            dma((6,)),
        ],
        compiler_params=pltpu.CompilerParams(vmem_limit_bytes=64_000_000),
        name="finish",
    )(red, gt.reshape(captions, length, width), sgo)
    return (*grads[:2], jnp.swapaxes(grads[2], 1, 2), *grads[3:])


def finish(
    red,
    gt,
    small,
    loss,
    tokens,
    attend,
    attend_bias,
    output,
    output_bias,
    expand,
    expand_bias,
    reduce,
    reduce_bias,
    gains,
    shifts,
    log_scale,
    GT,
    TOKENS,
    RED,
    WIDE,
    ATTEND,
    gt_in,
    gt_out,
    red_in,
    red_out,
):
    def copy(src, dst, sem):
        made = pltpu.make_async_copy(src, dst, sem)
        made.start()
        return made

    parts = gt_in.shape[0]
    size = GT.shape[0] // parts
    width = GT.shape[2]
    shard = ATTEND.shape[1]
    order = (0, 1, 2)
    weights = {g: copy(red.at[g], RED.at[g], red_in.at[g]) for g in order}
    pieces = [
        copy(gt.at[pl.ds(i * size, size)], GT.at[pl.ds(i * size, size)], gt_in.at[i])
        for i in range(parts)
    ]
    written = []
    loss[...] = small[10:11, 0:1].reshape(1)
    attend_bias[...] = small[0:2, 0:shard]
    expand_bias[...] = small[2:3, :].reshape(width)
    output_bias[...] = small[3:4, :].reshape(width)
    reduce_bias[...] = small[4:5, :].reshape(width)
    gains[...] = small[5:7, :]
    shifts[...] = small[7:9, :]
    log_scale[...] = small[9:10, 0:1].reshape(1)
    for g in order:
        weights[g].wait()
        if g == 0:
            for j in range(3):
                ATTEND[j] = RED[0, shard * j : shard * (j + 1), :].astype(F32)
                written.append(copy(ATTEND.at[j], attend.at[j], red_out.at[j]))
            WIDE[0, 3 * shard :, :] = RED[0, 3 * shard :, :].astype(F32)
            written.append(copy(WIDE.at[0, pl.ds(3 * shard, shard)], output, red_out.at[3]))
        else:

            def widen(t, carry):
                at = pl.ds(pl.multiple_of(t * 96, 96), 96)
                WIDE[g, at, :] = RED[g, at, :].astype(F32)
                return carry

            lax.fori_loop(0, width // 96, widen, 0)
            written.append(copy(WIDE.at[g], (expand, reduce)[g - 1], red_out.at[3 + g]))
    for i in range(parts):
        pieces[i].wait()
        at = slice(i * size, i * size + size)
        TOKENS[at] = GT[at].astype(F32)
        written.append(
            copy(
                TOKENS.at[pl.ds(i * size, size)], tokens.at[pl.ds(i * size, size)], gt_out.at[i]
            )
        )
    for made in written:
        made.wait()


def solution(mesh):
    in_specs = (
        P("dp", None, None),
        P(("dp", "mp"), None, None),
        P(),
        P(),
        P(),
        P(),
        P(),
        P(None, None, "mp"),
        P(None, "mp"),
        P("mp", None),
        P(),
        P(None, "mp"),
        P("mp"),
        P("mp", None),
        P(),
        P(),
        P(),
        P(),
        P("dp"),
    )
    out_specs = (
        P(),
        P("dp", None, None),
        P(None, None, "mp"),
        P(None, "mp"),
        P("mp", None),
        P(),
        P(None, "mp"),
        P("mp"),
        P("mp", None),
        P(),
        P(),
        P(),
        P(),
    )
    step = functools.partial(local_step, mesh.shape["dp"], mesh.shape["mp"])
    return jax.shard_map(step, mesh=mesh, in_specs=in_specs, out_specs=out_specs, check_vma=False)
```

time: 230 us -> 191 us (0.83)
  local copies, waits for them, and re-layouts: 16.7 us -> 0 us
  Pallas kernels: 202 us -> 189 us
  other arithmetic: 8.13 us -> 0 us
    pallas_call x1, Pallas kernels: 202 us -> 181 us  [local_step(): pl.pallas_call(functools.partial(body, n_dp, n_mp), out_shape=(jax.ShapeD...]
    slice x7 -> x0, local copies, waits for them, and re-layouts: 10.3 us -> none  [the longest x1 2.77 us: local_step(): red[2]]
    pallas_call x0 -> x1, Pallas kernels: none -> 7.71 us  [local_step(): pl.pallas_call(finish, out_shape=tuple((jax.ShapeDtypeStruct(shape, F32)...]
    convert_element_type x1 -> x0, other arithmetic: 2.91 us -> none  [local_step(): red = red.astype(F32).reshape(3, width, width)]
    reshape x1 -> x0, other arithmetic: 2.87 us -> none  [local_step(): gt.astype(F32).reshape(captions, length, width)]
    concatenate x1 -> x0, other arithmetic: 2.35 us -> none  [local_step(): jnp.concatenate([jnp.swapaxes(caption_attend, 1, 2).reshape(3 * shard, wi...]
where the time goes in v3:
time: 191 us; the launch traced here: 190 us
  Pallas kernels  189 us (99%)
    pallas_call x1, Pallas kernels, local_step(): pl.pallas_call(functools.partial(body, n_dp, n_mp), out_shape=(jax.ShapeD...  181 us
    pallas_call x1, Pallas kernels, local_step(): pl.pallas_call(finish, out_shape=tuple((jax.ShapeDtypeStruct(shape, F32)...  7.71 us

profile of v3, /device:TPU:0, one launch (start us, length us, event | category | flops | bytes accessed | tf_op | source)
XLA Modules:
  0.0 190.2 jit_solution(129927656208320216)
XLA Ops:
  1.3 181.0 %step.1 = (bf16[3,768,768]{2,1,0:T(8,128)(2,1)}, bf16[2,784,768]{2,1,0:T(8,128)(2,1)}, f32[16,768]{1,0:T(8,128)}) custom-call(bf16[98,16,768]{2,1,0:T(8,128)(2,1)} %tok_in.1, bf16[7,50,768]{2,1,0:T(8,128)(2,1)} %imt.1, bf16[3,768,768]{2,1,0:T(8,128)(2,1)} %ia_in.1, bf16[768,768]{1,0:T(8,128)(2,1)} %io_in.1, bf16[768,3072]{1,0:T(8,128)(2,1)} %ie_in.1, ...), custom_call_target="tpu_custom_call" | custom-call | tf_op jit(solution)/shard_map/step/pallas_call | solution.py:1079
  182.3 7.7 %finish.1 = (f32[1]{0:T(128)}, f32[98,16,768]{2,1,0:T(8,128)}, f32[3,192,768]{2,1,0:T(8,128)}, f32[2,192]{1,0:T(2,128)}, f32[192,768]{1,0:T(8,128)}, /*index=5*/...) custom-call(bf16[3,768,768]{2,1,0:T(8,128)(2,1)} %get-tuple-element., ...), custom_call_target="tpu_custom_call" | custom-call | tf_op jit(solution)/shard_map/finish/pallas_call | solution.py:1131

commit v4 on v3

--- a/solution.py
+++ b/solution.py
@@ -14,6 +14,38 @@
 F32 = jnp.float32
 LOW = jnp.bfloat16
 FAR = -1e30
+ALL_HOPS = (1, 2, 3)
+RPLAN = {
+    0: ((2, 0),),
+    2: ((2, 1),),
+    4: ((1, 0),),
+    6: ((2, 2), (1, 1)),
+    8: ((2, 3),),
+    10: ((1, 2), (2, 4)),
+    12: ((1, 3), (2, 5)),
+    15: ((1, 4), (2, 6)),
+    16: ((0, 1),),
+    22: ((0, 2),),
+    23: ((1, 5), (0, 3)),
+    24: ((1, 6),),
+    25: ((2, 7), (0, 4)),
+    26: ((1, 7), (0, 5)),
+    27: ((0, 6),),
+    28: ((0, 7),),
+}
+PLAN = {
+    1: ((0, 0, (1,)),),
+    2: ((0, 0, (2, 3)), (1, -1, ()),),
+    3: ((0, 1, (1, 2)),),
+    5: ((0, 1, (3,)),),
+    6: ((0, 2, (1, 2)),),
+    7: ((0, 2, (3,)), (1, 0, ALL_HOPS), (2, -1, ()),),
+    10: ((1, 1, ALL_HOPS),),
+    12: ((2, 0, ALL_HOPS),),
+    13: ((1, 2, ALL_HOPS),),
+    15: ((2, 1, ALL_HOPS),),
+    17: ((2, 2, ALL_HOPS),),
+}
 GELU_A = 0.7978845608028654
 GELU_B = 0.044715
 
@@ -267,8 +299,8 @@
             p, n, dev = 8 * ab + cb * 4, 4, core_dev
         return remote(at(p, n), at(p, n), ss.at[stage, ab], rs.at[stage, ab], dev)
 
-    def gather_start(g, stage):
-        for k in hops:
+    def gather_start(g, stage, ks=(1, 2, 3)):
+        for k in ks:
             source = partner(k)
             for ab in range(2):
                 (zc[g, k, ab] if stage == 0 else ac[g, stage - 1, k, ab]).wait_recv()
@@ -286,6 +318,13 @@
                 ac[g, 2, k, ab].wait_recv()
         if g > 0:
             own_loads[g].wait()
+
+    def tick(place):
+        for g, stage, ks in PLAN.get(place, ()):
+            if stage < 0:
+                gather_z(g)
+            else:
+                gather_start(g, stage, ks)
 
     gather_z(0)
     sb_copies = []
@@ -342,8 +381,7 @@
     lax.fori_loop(0, 3, image_qkv, 0)
     for i in range(8, 11):
         load_image(i)
-    gather_start(0, 0)
-    gather_z(1)
+    tick(1)
 
     key_valid = jnp.where(iota((256, 64), 1) < image_len, 0.0, FAR)
     lane_head = iota((64, 256), 1) >> 6
@@ -368,7 +406,7 @@
         return carry
 
     lax.fori_loop(0, images, image_attention, 0)
-    gather_start(0, 1)
+    tick(2)
     image_loads[3].wait()
 
     def image_out(n, carry):
@@ -418,11 +456,15 @@
         IP[...] += dot(pooled, IW[u])
         return carry
 
-    lax.fori_loop(0, 2, image_feed, 0)
-    gather_start(1, 0)
-    gather_z(2)
-    gather_start(0, 2)
-    lax.fori_loop(2, 4, image_feed, 0)
+    tick(3)
+    lax.fori_loop(0, 1, image_feed, 0)
+    tick(4)
+    lax.fori_loop(1, 2, image_feed, 0)
+    tick(5)
+    lax.fori_loop(2, 3, image_feed, 0)
+    tick(6)
+    lax.fori_loop(3, 4, image_feed, 0)
+    tick(7)
     pooled_image = IP[0:8]
     EMB[me] = (
         pooled_image
@@ -453,6 +495,7 @@
         return carry
 
     lax.fori_loop(0, n_cap, norm_one, 0, unroll=7)
+    tick(8)
     for copy in sb_copies:
         copy.wait_recv()
     gather_end(0)
@@ -463,9 +506,11 @@
         QKV[j, s] = (dot_nt(N1[...], weight) + SB[s, pl.ds(j, 1), 0:shard]).astype(LOW)
         return carry
 
-    gather_start(1, 1)
-    lax.fori_loop(0, 3 * n_mp, project, 0)
-    gather_start(2, 0)
+    tick(9)
+    lax.fori_loop(0, 6, project, 0)
+    tick(10)
+    lax.fori_loop(6, 3 * n_mp, project, 0)
+    tick(11)
     lane_three = iota((BLOCK, shard), 1) >> 6
 
     def join_heads(o):
@@ -490,10 +535,12 @@
             MIX[s, at, :] = mixed
         return carry
 
-    lax.fori_loop(0, n_blocks // 2, attention, 0)
-    gather_start(1, 2)
-    lax.fori_loop(n_blocks // 2, n_blocks, attention, 0)
-    gather_start(2, 1)
+    lax.fori_loop(0, 2, attention, 0)
+    tick(12)
+    lax.fori_loop(2, 4, attention, 0)
+    tick(13)
+    lax.fori_loop(4, n_blocks, attention, 0)
+    tick(14)
 
     def attend_out(n, carry):
         lanes = pl.ds(pl.multiple_of(n * 256, 256), 256)
@@ -514,6 +561,7 @@
         return carry
 
     lax.fori_loop(0, n_cap, norm_two, 0, unroll=7)
+    tick(15)
     gather_end(1)
 
     def feed(s, carry):
@@ -531,9 +579,14 @@
         PA[s] = (dot(POOL[...], GT[...]) * (1.0 / LEN)).astype(LOW)
         return carry
 
-    lax.fori_loop(0, 2, feed, 0)
-    gather_start(2, 2)
-    lax.fori_loop(2, n_mp, feed, 0)
+    lax.fori_loop(0, 1, feed, 0)
+    tick(16)
+    lax.fori_loop(1, 2, feed, 0)
+    tick(17)
+    lax.fori_loop(2, 3, feed, 0)
+    tick(18)
+    lax.fori_loop(3, n_mp, feed, 0)
+    tick(19)
 
     def pool_residual(n, carry):
         lanes = pl.ds(pl.multiple_of(n * 128, 128), 128)
@@ -750,17 +803,22 @@
                 state[g, "gather", 2, ab].wait_recv()
             stores.append(local(whole(g), red.at[g], out_sem.at[g]))
 
+    def back_tick(place):
+        for g, step in RPLAN.get(place, ()):
+            reduce_step(g, step)
+
     shards = (m, pair)
     for i in range(2):
         IW[4 + i] = dot_tn(PA[shards[i]], GPL[0]).astype(LOW)
-    reduce_step(2, 0)
+
+    back_tick(0)
 
     def grad_activation(s, carry):
         GA[s] = dot_nt(GPL[1], W[2, s])
         return carry
 
     lax.fori_loop(0, n_mp, grad_activation, 0)
-    reduce_step(2, 1)
+    back_tick(1)
     ones = jnp.ones((16, rows), LOW)
 
     def grad_hidden(s, carry):
@@ -773,8 +831,10 @@
         SG[0, pl.ds(8 + s, 1), :] = dot(ones, GP[s])[0:1]
         return carry
 
-    lax.fori_loop(0, n_mp, grad_hidden, 0)
-    reduce_step(2, 2)
+    lax.fori_loop(0, 2, grad_hidden, 0)
+    back_tick(2)
+    lax.fori_loop(2, n_mp, grad_hidden, 0)
+    back_tick(3)
 
     def expand_gradient(i, carry):
         s = m + i * (pair - m)
@@ -782,8 +842,7 @@
         return carry
 
     lax.fori_loop(0, 2, expand_gradient, 0)
-    reduce_step(1, 0)
-    reduce_step(2, 3)
+    back_tick(4)
 
     def grad_norm_two(n, carry):
         p = pl.ds(pl.multiple_of(n * 384, 128), 384)
@@ -793,9 +852,10 @@
         ACC[:, pl.ds(pl.multiple_of(n * 384, 128), 384)] = total
         return carry
 
-    lax.fori_loop(0, 2, grad_norm_two, 0)
-    reduce_step(1, 1)
-    reduce_step(2, 4)
+    lax.fori_loop(0, 1, grad_norm_two, 0)
+    back_tick(5)
+    lax.fori_loop(1, 2, grad_norm_two, 0)
+    back_tick(6)
 
     def norm_back(e, gain, x):
         xhat, scale = standard(x)
@@ -825,17 +885,16 @@
     SG[0, 17:18, :] = jnp.sum(db, axis=0, keepdims=True)
     SG[0, 12:13, :] = jnp.sum(do, axis=0, keepdims=True)
 
+    back_tick(7)
     for i in range(2):
         IW[i, 3 * shard : 4 * shard, :] = dot_tn(MIX[shards[i]], GRL[...]).astype(LOW)
-    reduce_step(1, 2)
-    reduce_step(2, 5)
 
     def grad_mixture(s, carry):
         MIX[s] = dot_nt(GRL[...], W[0, s, pl.ds(3 * shard, shard), :]).astype(LOW)
         return carry
 
     lax.fori_loop(0, n_mp, grad_mixture, 0)
-    reduce_step(2, 6)
+    back_tick(8)
 
     def attention_back(b, carry):
         at = pl.ds(pl.multiple_of(b * BLOCK, 16), BLOCK)
@@ -875,14 +934,18 @@
     gt_copies = []
     cuts = (0, 4, n_blocks)
     for r in range(2):
-        lax.fori_loop(cuts[r], cuts[r + 1], attention_back, 0)
-        reduce_step(1, 3 + r)
+        middle = (cuts[r] + cuts[r + 1]) // 2
+        lax.fori_loop(cuts[r], middle, attention_back, 0)
+        back_tick(9 + 5 * r)
+        lax.fori_loop(middle, cuts[r + 1], attention_back, 0)
+        back_tick(10 + 5 * r)
         if r == 1:
             attend_gradient(2)
             reduce_start(0, 1)
             attend_gradient(0)
             attend_gradient(1)
             reduce_start(0, 0)
+            back_tick(20)
         first, last = cuts[r] * (BLOCK // LEN), cuts[r + 1] * (BLOCK // LEN)
         stripe = pl.ds(first * LEN, (last - first) * LEN)
 
@@ -900,9 +963,7 @@
             return carry
 
         lax.fori_loop(0, width // 256, grad_norm_one, 0)
-        if r == 1:
-            reduce_step(0, 1)
-
+        back_tick(11 + 5 * r)
         def back_one(t, carry):
             at = pl.ds(pl.multiple_of(t * LEN, LEN), LEN)
             dv, dg, db = norm_back(ACC[at, :], g1, TOK[t].astype(F32))
@@ -912,11 +973,12 @@
         small_gain, small_shift = lax.fori_loop(
             first, last, back_one, (small_gain, small_shift), unroll=7
         )
+        back_tick(12 + 5 * r)
         gt_copies.append(
             remote(GT.at[stripe], gt.at[half, stripe], gt_s.at[r], gt_r.at[r], pair_dev)
         )
+    back_tick(21)
     stores.append(local(GT, gt.at[half], out_sem.at[3]))
-    reduce_step(0, 2)
     SG[0, 14:15, :] = jnp.sum(small_gain, axis=0, keepdims=True)
     SG[0, 16:17, :] = jnp.sum(small_shift, axis=0, keepdims=True)
 
@@ -936,25 +998,23 @@
         small[i].wait_recv()
         SG[i + 1] = SG[i] + SGR[i]
 
+    back_tick(22)
     small_start(0)
-    reduce_step(1, 5)
+    back_tick(23)
     small_end(0)
     small_start(1)
-    reduce_step(0, 3)
+    back_tick(24)
     small_end(1)
     small_start(2)
-    reduce_step(1, 6)
+    back_tick(25)
     small_end(2)
     small_start(3)
-    reduce_step(2, 7)
-    reduce_step(0, 4)
+    back_tick(26)
     small_end(3)
     for i in range(4, 4 + extra):
         small_start(i)
         small_end(i)
-    reduce_step(0, 5)
-    reduce_step(1, 7)
-    reduce_step(0, 6)
+    back_tick(27)
     last = SG.shape[0] - 1
     sgo[...] = jnp.zeros_like(sgo)
     sgo[0:1, :] = SG[last, pl.ds(m, 1), :]
@@ -962,7 +1022,7 @@
     sgo[2:3, :] = SG[last, pl.ds(8 + m, 1), :]
     sgo[3:10, :] = SG[last, 12:19, :]
     sgo[10:11, :] = jnp.broadcast_to(loss, (1, width))
-    reduce_step(0, 7)
+    back_tick(28)
     for copy in gt_copies:
         copy.wait_recv()
     pltpu.make_async_copy(EMB.at[pl.ds(0, n_all - 1)], EMB.at[pl.ds(0, n_all - 1)], emb_s).wait()

time: 191 us -> 178 us (0.932)
  Pallas kernels: 189 us -> 175 us
    pallas_call x1, Pallas kernels: 181 us -> 167 us  [local_step(): pl.pallas_call(functools.partial(body, n_dp, n_mp), out_shape=(jax.ShapeD...]
where the time goes in v4:
time: 178 us; the launch traced here: 176 us
  Pallas kernels  175 us (98%)
    pallas_call x1, Pallas kernels, local_step(): pl.pallas_call(functools.partial(body, n_dp, n_mp), out_shape=(jax.ShapeD...  167 us
    pallas_call x1, Pallas kernels, local_step(): pl.pallas_call(finish, out_shape=tuple((jax.ShapeDtypeStruct(shape, F32)...  7.71 us

profile of v4, /device:TPU:0, one launch (start us, length us, event | category | flops | bytes accessed | tf_op | source)
XLA Modules:
  0.0 176.4 jit_solution(5824665892198090509)
XLA Ops:
  1.3 167.2 %step.1 = (bf16[3,768,768]{2,1,0:T(8,128)(2,1)}, bf16[2,784,768]{2,1,0:T(8,128)(2,1)}, f32[16,768]{1,0:T(8,128)}) custom-call(bf16[98,16,768]{2,1,0:T(8,128)(2,1)} %tok_in.1, bf16[7,50,768]{2,1,0:T(8,128)(2,1)} %imt.1, bf16[3,768,768]{2,1,0:T(8,128)(2,1)} %ia_in.1, bf16[768,768]{1,0:T(8,128)(2,1)} %io_in.1, bf16[768,3072]{1,0:T(8,128)(2,1)} %ie_in.1, ...), custom_call_target="tpu_custom_call" | custom-call | tf_op jit(solution)/shard_map/step/pallas_call | solution.py:1139
  168.5 7.7 %finish.1 = (f32[1]{0:T(128)}, f32[98,16,768]{2,1,0:T(8,128)}, f32[3,192,768]{2,1,0:T(8,128)}, f32[2,192]{1,0:T(2,128)}, f32[192,768]{1,0:T(8,128)}, /*index=5*/...) custom-call(bf16[3,768,768]{2,1,0:T(8,128)(2,1)} %get-tuple-element., ...), custom_call_target="tpu_custom_call" | custom-call | tf_op jit(solution)/shard_map/finish/pallas_call | solution.py:1191

commit v5 on v4

--- a/solution.py
+++ b/solution.py
@@ -19,32 +19,36 @@
     0: ((2, 0),),
     2: ((2, 1),),
     4: ((1, 0),),
-    6: ((2, 2), (1, 1)),
+    6: ((2, 2), (1, 1),),
     8: ((2, 3),),
-    10: ((1, 2), (2, 4)),
-    12: ((1, 3), (2, 5)),
-    15: ((1, 4), (2, 6)),
-    16: ((0, 1),),
-    22: ((0, 2),),
-    23: ((1, 5), (0, 3)),
-    24: ((1, 6),),
-    25: ((2, 7), (0, 4)),
-    26: ((1, 7), (0, 5)),
+    9: ((2, 4),),
+    12: ((1, 2),),
+    10: ((1, 3), (2, 5),),
+    11: ((2, 6),),
+    17: ((0, 1),),
+    21: ((0, 2),),
+    22: ((1, 4), (0, 3),),
+    23: ((1, 5),),
+    24: ((0, 4), (1, 6),),
+    25: ((0, 5), (2, 7),),
+    26: ((1, 7),),
     27: ((0, 6),),
     28: ((0, 7),),
 }
 PLAN = {
     1: ((0, 0, (1,)),),
-    2: ((0, 0, (2, 3)), (1, -1, ()),),
-    3: ((0, 1, (1, 2)),),
+    2: ((0, 0, (2, 3)), (1, -1, (1,)), (2, -1, (1,)),),
+    3: ((0, 1, (1, 2)), (1, -1, (2, 3)), (2, -1, (2, 3)),),
     5: ((0, 1, (3,)),),
     6: ((0, 2, (1, 2)),),
-    7: ((0, 2, (3,)), (1, 0, ALL_HOPS), (2, -1, ()),),
-    10: ((1, 1, ALL_HOPS),),
-    12: ((2, 0, ALL_HOPS),),
-    13: ((1, 2, ALL_HOPS),),
-    15: ((2, 1, ALL_HOPS),),
-    17: ((2, 2, ALL_HOPS),),
+    7: ((0, 2, (3,)), (1, 0, (1,)), (2, 0, (1,)),),
+    10: ((1, 1, (1,)), (2, 1, (1,)),),
+    12: ((1, 2, (1,)), (2, 2, (1,)),),
+    13: ((1, 0, (2, 3)),),
+    14: ((1, 1, (2, 3)), (2, 0, (2, 3)),),
+    16: ((1, 2, (2, 3)),),
+    17: ((2, 1, (2, 3)),),
+    19: ((2, 2, (2, 3)),),
 }
 GELU_A = 0.7978845608028654
 GELU_B = 0.044715
@@ -122,6 +126,7 @@
     N2,
     GP,
     PA,
+    PB,
     ACC,
     GRL,
     GT,
@@ -173,6 +178,8 @@
     gt_s,
     gt_r,
     out_sem,
+    pb_s,
+    pb_r,
 ):
     d = lax.axis_index("dp")
     m = lax.axis_index("mp")
@@ -228,17 +235,25 @@
 
     barrier = pltpu.get_barrier_semaphore()
 
+    low = lax.rem(d, 8)
+    slot = low * 2 + half
+
+    def near_device(k):
+        q = lax.rem(slot + k, 16)
+        return (d - low + q // 2, m - half + lax.rem(q, 2))
+
     def greet(k, carry):
-        q = lax.rem(me + k, n_all)
         pl.semaphore_signal(
-            barrier,
-            inc=1,
-            device_id=(q // n_mp, lax.rem(q, n_mp)),
-            device_id_type=pl.DeviceIdType.MESH,
-        )
-        return carry
-
-    lax.fori_loop(1, n_all, greet, 0)
+            barrier, inc=1, device_id=near_device(k), device_id_type=pl.DeviceIdType.MESH
+        )
+        return carry
+
+    far = flip(m, 1)
+    far_pair = flip(pair, 1)
+    others = [(d, far), (d, far_pair)] + [(flip(d, 3 + x), m) for x in range(extra)]
+    for dev in others:
+        pl.semaphore_signal(barrier, inc=1, device_id=dev, device_id_type=pl.DeviceIdType.MESH)
+    lax.fori_loop(1, 16, greet, 0)
 
     image_loads = {}
 
@@ -264,7 +279,7 @@
     SB[m] = SBL[...]
     for copy in ca_copies + own_loads[0:1]:
         copy.wait()
-    pl.semaphore_wait(barrier, n_all - 1)
+    pl.semaphore_wait(barrier, 15 + len(others))
 
     hops = (1, 2, 3)
 
@@ -278,8 +293,8 @@
     def span(p, n):
         return pl.ds(pl.multiple_of(p * PIECE, 16), n * PIECE)
 
-    def gather_z(g):
-        for k in hops:
+    def gather_z(g, ks=(1, 2, 3)):
+        for k in ks:
             dev = (d, partner(k))
             for ab, p in ((0, p_a), (1, p_b)):
                 zc[g, k, ab] = remote(
@@ -312,17 +327,17 @@
                     ga_r.at[g, k - 1],
                 )
 
-    def gather_end(g):
-        for k in hops:
+    def gather_end(g, ks=(1, 2, 3)):
+        for k in ks:
             for ab in range(2):
                 ac[g, 2, k, ab].wait_recv()
-        if g > 0:
+        if g > 0 and 1 in ks:
             own_loads[g].wait()
 
     def tick(place):
         for g, stage, ks in PLAN.get(place, ()):
             if stage < 0:
-                gather_z(g)
+                gather_z(g, ks)
             else:
                 gather_start(g, stage, ks)
 
@@ -345,13 +360,13 @@
         load_image(i)
     own_loads.append(local(we_in, W.at[1, m], loc_sem.at[1]))
     own_loads.append(local(wr_in, W.at[2, m], loc_sem.at[2]))
-    row_block = iota((BLOCK, BLOCK), 0) >> 4
-    near = jnp.where(row_block == (iota((BLOCK, BLOCK), 1) >> 4), 0.0, FAR)
+    query = iota((BLOCK, 3 * BLOCK), 1)
+    query = query - jnp.where(query >= 2 * BLOCK, 2 * BLOCK, jnp.where(query >= BLOCK, BLOCK, 0))
+    BM[...] = jnp.where((iota((BLOCK, 3 * BLOCK), 0) >> 4) == (query >> 4), 0.0, FAR)
     lane_shard = iota((BLOCK, shard), 1) >> 6
     for h in range(3):
         at = slice(h * BLOCK, (h + 1) * BLOCK)
         HM3[at, :] = jnp.where(lane_shard == h, 1.0, 0.0).astype(LOW)
-        BM[at, :] = near
     lane_four = iota((64, 256), 1) >> 6
     for h in range(4):
         HM4[64 * h : 64 * h + 64, :] = jnp.where(lane_four == h, 1.0, 0.0).astype(LOW)
@@ -471,19 +486,40 @@
         * lax.rsqrt(jnp.sum(pooled_image * pooled_image, axis=-1, keepdims=True) + 1e-6)
     ).astype(LOW)
 
-    def send_embed(k, carry):
-        q = lax.rem(me + k, n_all)
-        pltpu.make_async_remote_copy(
-            src_ref=EMB.at[me],
-            dst_ref=EMB.at[me],
-            send_sem=emb_s,
-            recv_sem=emb_r,
-            device_id=(q // n_mp, lax.rem(q, n_mp)),
-            device_id_type=pl.DeviceIdType.MESH,
-        ).start()
-        return carry
-
-    lax.fori_loop(1, n_all, send_embed, 0)
+    shown = {}
+
+    def show(stage, first, n, dev, at):
+        run = EMB.at[pl.ds(first * n_mp, n * n_mp)]
+        shown.setdefault(stage, []).append(
+            remote(run, run, emb_s.at[at], emb_r.at[at], dev)
+        )
+
+    def show_embeds(stage):
+        for copy in shown.get(stage - 1, ()):
+            copy.wait_recv()
+        if stage == 0:
+            for k in hops:
+                run = EMB.at[me]
+                shown.setdefault(0, []).append(
+                    remote(run, run, emb_s.at[k - 1], emb_r.at[k - 1], (d, partner(k)))
+                )
+        elif stage == 1:
+            show(1, d, 1, x_dev, 3)
+        elif stage == 2:
+            for x in range(2):
+                show(2, d + 2 * (x - xb), 1, y_dev, 4 + x)
+        elif stage == 3:
+            for q in range(4):
+                show(3, d - low + cb + 2 * q, 1, core_dev, 6 + q)
+        else:
+            for x in range(extra):
+                run = 8 << x
+                first = d - lax.rem(d, run)
+                show(4 + x, first, run, (flip(d, 3 + x), m), 10 + x)
+                for copy in shown[4 + x]:
+                    copy.wait_recv()
+
+    show_embeds(0)
 
     tok_copy.wait()
     g1, g2 = norm_gains[0:1, :], norm_gains[1:2, :]
@@ -526,10 +562,10 @@
         heads, mask = HM3[...], BM[...]
         every = []
         for q, k, v in loaded:
-            logits = dot_nt(jnp.concatenate([q] * 3, axis=0) * heads, k) * 0.125 + mask
-            expos = jnp.exp(logits - jnp.max(logits, axis=-1, keepdims=True))
-            probs = (expos * (1.0 / jnp.sum(expos, axis=-1, keepdims=True))).astype(LOW)
-            every.append((probs, join_heads(dot(probs, v)).astype(LOW)))
+            logits = dot_nt(k, jnp.concatenate([q] * 3, axis=0) * heads) * 0.125 + mask
+            expos = jnp.exp(logits - jnp.max(logits, axis=0, keepdims=True))
+            probs = (expos * (1.0 / jnp.sum(expos, axis=0, keepdims=True))).astype(LOW)
+            every.append((probs, join_heads(dot_tn(probs, v)).astype(LOW)))
         for s, (probs, mixed) in enumerate(every):
             PR[s, b] = probs
             MIX[s, at, :] = mixed
@@ -562,9 +598,10 @@
 
     lax.fori_loop(0, n_cap, norm_two, 0, unroll=7)
     tick(15)
-    gather_end(1)
-
-    def feed(s, carry):
+    show_embeds(1)
+    gather_end(1, (1,))
+
+    def feed_one(s):
         ACC[...] = dot(N2[...], W[1, s])
         bias = SB[s, 3:4, :]
 
@@ -577,17 +614,21 @@
 
         lax.fori_loop(0, n_cap, activate, 0, unroll=7)
         PA[s] = (dot(POOL[...], GT[...]) * (1.0 / LEN)).astype(LOW)
-        return carry
-
-    lax.fori_loop(0, 1, feed, 0)
+
+    def feed_near(i, carry):
+        feed_one(m + i * (pair - m))
+        return carry
+
+    def feed_far(i, carry):
+        feed_one(far + i * (far_pair - far))
+        return carry
+
+    lax.fori_loop(0, 1, feed_near, 0)
     tick(16)
-    lax.fori_loop(1, 2, feed, 0)
+    show_embeds(2)
+    lax.fori_loop(1, 2, feed_near, 0)
     tick(17)
-    lax.fori_loop(2, 3, feed, 0)
-    tick(18)
-    lax.fori_loop(3, n_mp, feed, 0)
-    tick(19)
-
+    show_embeds(3)
     def pool_residual(n, carry):
         lanes = pl.ds(pl.multiple_of(n * 128, 128), 128)
         res = RES[:, lanes]
@@ -598,14 +639,17 @@
 
     lax.fori_loop(0, width // 128, pool_residual, 0)
     pooled = EL[...] + reduce_bias[...].reshape(1, width)
-    gather_end(2)
-    for s in range(n_mp):
-        pooled += dot(PA[s], W[2, s])
+    gather_end(2, (1,))
+    PB[0] = (dot(PA[m], W[2, m]) + dot(PA[pair], W[2, pair])).astype(LOW)
+    pooled_copy = remote(PB.at[0], PB.at[1], pb_s, pb_r, (d, far))
+    tick(18)
+    pooled_copy.wait_recv()
+    pooled += PB[0].astype(F32) + PB[1].astype(F32)
     inverse = lax.rsqrt(jnp.sum(pooled * pooled, axis=-1, keepdims=True) + 1e-6)
     embed = pooled * inverse
     EL[...] = embed
 
-    pltpu.make_async_copy(EMB.at[pl.ds(0, n_all - 1)], EMB.at[pl.ds(0, n_all - 1)], emb_r).wait()
+    show_embeds(4)
     group = min(n_all, 32)
 
     def embeds(c):
@@ -641,23 +685,26 @@
     MSG[2:3, :] = jnp.sum(scores * matches, axis=0, keepdims=True)
     MSG[3:4, :] = jnp.sum(matches, axis=0, keepdims=True)
     MSG[4:5, :] = jnp.broadcast_to(row_part, (1, t_all))
-    low = lax.rem(d, 8)
-    slot = low * 2 + half
     STATS[slot] = MSG[...]
 
     def send_stats(k, carry):
-        q = lax.rem(slot + k, 16)
         pltpu.make_async_remote_copy(
             src_ref=MSG,
             dst_ref=STATS.at[slot],
             send_sem=st_s,
             recv_sem=st_r,
-            device_id=(d - low + q // 2, m - half + lax.rem(q, 2)),
+            device_id=near_device(k),
             device_id_type=pl.DeviceIdType.MESH,
         ).start()
         return carry
 
     lax.fori_loop(1, 16, send_stats, 0)
+    tick(19)
+    gather_end(1, (2, 3))
+    lax.fori_loop(0, 1, feed_far, 0)
+    tick(20)
+    lax.fori_loop(1, 2, feed_far, 0)
+    gather_end(2, (2, 3))
     pltpu.make_async_copy(STATS.at[pl.ds(0, 15)], STATS.at[pl.ds(0, 15)], st_r).wait()
     top = jnp.max(STATS[:, 0, :], axis=0, keepdims=True)
     total = jnp.sum(STATS[:, 1, :] * jnp.exp(STATS[:, 0, :] - top), axis=0, keepdims=True)
@@ -846,9 +893,10 @@
 
     def grad_norm_two(n, carry):
         p = pl.ds(pl.multiple_of(n * 384, 128), 384)
-        total = dot_nt(GP[0], W[1, 0, p, :])
-        for s in range(1, n_mp):
-            total += dot_nt(GP[s], W[1, s, p, :])
+        total = dot_nt(
+            jnp.concatenate([GP[s] for s in range(n_mp)], axis=1),
+            jnp.concatenate([W[1, s, p, :] for s in range(n_mp)], axis=1),
+        )
         ACC[:, pl.ds(pl.multiple_of(n * 384, 128), 384)] = total
         return carry
 
@@ -907,14 +955,14 @@
             q = jnp.concatenate([q] * 3, axis=0) * heads
             g = jnp.concatenate([g] * 3, axis=0) * heads
             probs = low_probs.astype(F32)
-            grad_probs = dot_nt(g, v)
-            inner = jnp.sum(grad_probs * probs, axis=-1, keepdims=True)
+            grad_probs = dot_nt(v, g)
+            inner = jnp.sum(grad_probs * probs, axis=0, keepdims=True)
             grad_logits = (probs * (grad_probs - inner)).astype(LOW)
             every.append(
                 (
-                    (join_heads(dot(grad_logits, k)) * 0.125).astype(LOW),
-                    (dot_tn(grad_logits, q) * 0.125).astype(LOW),
-                    dot_tn(low_probs, g).astype(LOW),
+                    (join_heads(dot_tn(grad_logits, k)) * 0.125).astype(LOW),
+                    (dot(grad_logits, q) * 0.125).astype(LOW),
+                    dot(low_probs, g).astype(LOW),
                 )
             )
         for s, grads in enumerate(every):
@@ -932,14 +980,11 @@
 
     small_gain, small_shift = zero8, zero8
     gt_copies = []
-    cuts = (0, 4, n_blocks)
-    for r in range(2):
-        middle = (cuts[r] + cuts[r + 1]) // 2
-        lax.fori_loop(cuts[r], middle, attention_back, 0)
-        back_tick(9 + 5 * r)
-        lax.fori_loop(middle, cuts[r + 1], attention_back, 0)
-        back_tick(10 + 5 * r)
-        if r == 1:
+    cuts = (0, 3, 5, n_blocks)
+    for r in range(3):
+        lax.fori_loop(cuts[r], cuts[r + 1], attention_back, 0)
+        back_tick(9 + r)
+        if r == 2:
             attend_gradient(2)
             reduce_start(0, 1)
             attend_gradient(0)
@@ -963,7 +1008,7 @@
             return carry
 
         lax.fori_loop(0, width // 256, grad_norm_one, 0)
-        back_tick(11 + 5 * r)
+        back_tick(12 + r)
         def back_one(t, carry):
             at = pl.ds(pl.multiple_of(t * LEN, LEN), LEN)
             dv, dg, db = norm_back(ACC[at, :], g1, TOK[t].astype(F32))
@@ -973,7 +1018,7 @@
         small_gain, small_shift = lax.fori_loop(
             first, last, back_one, (small_gain, small_shift), unroll=7
         )
-        back_tick(12 + 5 * r)
+        back_tick(15 + r)
         gt_copies.append(
             remote(GT.at[stripe], gt.at[half, stripe], gt_s.at[r], gt_r.at[r], pair_dev)
         )
@@ -1025,7 +1070,6 @@
     back_tick(28)
     for copy in gt_copies:
         copy.wait_recv()
-    pltpu.make_async_copy(EMB.at[pl.ds(0, n_all - 1)], EMB.at[pl.ds(0, n_all - 1)], emb_s).wait()
     pltpu.make_async_copy(STATS.at[pl.ds(0, 15)], STATS.at[pl.ds(0, 15)], st_s).wait()
     for copy in sends:
         copy.wait_send()
@@ -1078,12 +1122,13 @@
         pltpu.VMEM((n_cap, length, width), LOW),
         pltpu.VMEM((rows, width), LOW),
         pltpu.VMEM((3, n_mp, rows, shard), LOW),
-        pltpu.VMEM((n_mp, n_blocks, 3 * BLOCK, BLOCK), LOW),
+        pltpu.VMEM((n_mp, n_blocks, BLOCK, 3 * BLOCK), LOW),
         pltpu.VMEM((n_mp, rows, shard), LOW),
         pltpu.VMEM((rows, width), F32),
         pltpu.VMEM((rows, width), LOW),
         pltpu.VMEM((n_mp, rows, width), LOW),
         pltpu.VMEM((n_mp, 64, width), LOW),
+        pltpu.VMEM((2, 64, width), LOW),
         pltpu.VMEM((rows, width), F32),
         pltpu.VMEM((rows, width), LOW),
         pltpu.VMEM((rows, width), LOW),
@@ -1094,7 +1139,7 @@
         pltpu.VMEM((8, width), F32),
         pltpu.VMEM((n_mp, 8, width), F32),
         pltpu.VMEM((3 * BLOCK, shard), LOW),
-        pltpu.VMEM((3 * BLOCK, BLOCK), F32),
+        pltpu.VMEM((BLOCK, 3 * BLOCK), F32),
         pltpu.VMEM((256, 256), LOW),
         pltpu.VMEM((64, rows), LOW),
         pltpu.VMEM((64, width), F32),
@@ -1118,8 +1163,8 @@
         dma,
         dma((3,)),
         dma((3,)),
-        dma,
-        dma,
+        dma((10 + nx,)),
+        dma((10 + nx,)),
         dma,
         dma,
         dma((nx,)),
@@ -1132,9 +1177,11 @@
         dma((3, nx, 2)),
         dma((4 + extra,)),
         dma((4 + extra,)),
-        dma((2,)),
-        dma((2,)),
+        dma((3,)),
+        dma((3,)),
         dma((4,)),
+        dma,
+        dma,
     ]
     red, gt, sgo = pl.pallas_call(
         functools.partial(body, n_dp, n_mp),

time: 178 us -> 171 us (0.961)
  Pallas kernels: 175 us -> 168 us
    pallas_call x1, Pallas kernels: 167 us -> 160 us  [local_step(): pl.pallas_call(functools.partial(body, n_dp, n_mp), out_shape=(jax.ShapeD...]
where the time goes in v5:
time: 171 us; the launch traced here: 170 us
  Pallas kernels  168 us (98%)
    pallas_call x1, Pallas kernels, local_step(): pl.pallas_call(functools.partial(body, n_dp, n_mp), out_shape=(jax.ShapeD...  160 us
    pallas_call x1, Pallas kernels, local_step(): pl.pallas_call(finish, out_shape=tuple((jax.ShapeDtypeStruct(shape, F32)...  7.71 us

profile of v5, /device:TPU:0, one launch (start us, length us, event | category | flops | bytes accessed | tf_op | source)
XLA Modules:
  0.0 169.5 jit_solution(14730547759201687162)
XLA Ops:
  1.3 160.3 %step.1 = (bf16[3,768,768]{2,1,0:T(8,128)(2,1)}, bf16[2,784,768]{2,1,0:T(8,128)(2,1)}, f32[16,768]{1,0:T(8,128)}) custom-call(bf16[98,16,768]{2,1,0:T(8,128)(2,1)} %tok_in.1, bf16[7,50,768]{2,1,0:T(8,128)(2,1)} %imt.1, bf16[3,768,768]{2,1,0:T(8,128)(2,1)} %ia_in.1, bf16[768,768]{1,0:T(8,128)(2,1)} %io_in.1, bf16[768,3072]{1,0:T(8,128)(2,1)} %ie_in.1, ...), custom_call_target="tpu_custom_call" | custom-call | tf_op jit(solution)/shard_map/step/pallas_call | solution.py:1186
  161.6 7.7 %finish.1 = (f32[1]{0:T(128)}, f32[98,16,768]{2,1,0:T(8,128)}, f32[3,192,768]{2,1,0:T(8,128)}, f32[2,192]{1,0:T(2,128)}, f32[192,768]{1,0:T(8,128)}, /*index=5*/...) custom-call(bf16[3,768,768]{2,1,0:T(8,128)(2,1)} %get-tuple-element., ...), custom_call_target="tpu_custom_call" | custom-call | tf_op jit(solution)/shard_map/finish/pallas_call | solution.py:1238

commit v6 on v5

--- a/solution.py
+++ b/solution.py
@@ -19,36 +19,40 @@
     0: ((2, 0),),
     2: ((2, 1),),
     4: ((1, 0),),
-    6: ((2, 2), (1, 1),),
-    8: ((2, 3),),
-    9: ((2, 4),),
-    12: ((1, 2),),
-    10: ((1, 3), (2, 5),),
-    11: ((2, 6),),
-    17: ((0, 1),),
-    21: ((0, 2),),
-    22: ((1, 4), (0, 3),),
-    23: ((1, 5),),
-    24: ((0, 4), (1, 6),),
-    25: ((0, 5), (2, 7),),
-    26: ((1, 7),),
-    27: ((0, 6),),
+    5: ((2, 2), (1, 1),),
+    6: ((2, 3),),
+    8: ((2, 4),),
+    9: ((1, 2),),
+    20: ((1, 3),),
+    10: ((0, 1),),
+    15: ((1, 4),),
+    13: ((2, 5),),
+    11: ((0, 2),),
+    16: ((0, 3),),
+    17: ((2, 6),),
+    18: ((1, 5),),
+    21: ((0, 4),),
+    22: ((1, 6), (2, 7),),
+    23: ((0, 5),),
+    25: ((1, 7),),
+    26: ((0, 6),),
     28: ((0, 7),),
 }
 PLAN = {
     1: ((0, 0, (1,)),),
     2: ((0, 0, (2, 3)), (1, -1, (1,)), (2, -1, (1,)),),
     3: ((0, 1, (1, 2)), (1, -1, (2, 3)), (2, -1, (2, 3)),),
+    4: ((0, 2, (1,)),),
     5: ((0, 1, (3,)),),
-    6: ((0, 2, (1, 2)),),
-    7: ((0, 2, (3,)), (1, 0, (1,)), (2, 0, (1,)),),
+    7: ((0, 2, (2,)), (0, 2, (3,)), (1, 0, (1,)), (2, 0, (1,)),),
     10: ((1, 1, (1,)), (2, 1, (1,)),),
     12: ((1, 2, (1,)), (2, 2, (1,)),),
     13: ((1, 0, (2, 3)),),
-    14: ((1, 1, (2, 3)), (2, 0, (2, 3)),),
+    14: ((1, 1, (2, 3)),),
     16: ((1, 2, (2, 3)),),
-    17: ((2, 1, (2, 3)),),
-    19: ((2, 2, (2, 3)),),
+    17: ((2, 0, (2, 3)),),
+    20: ((2, 1, (2, 3)),),
+    22: ((2, 2, (2, 3)),),
 }
 GELU_A = 0.7978845608028654
 GELU_B = 0.044715
@@ -94,7 +98,7 @@
     n_dp,
     n_mp,
     tok_in,
-    imt,
+    imt_in,
     ia_in,
     io_in,
     ie_in,
@@ -118,6 +122,7 @@
     W,
     IW,
     TOK,
+    imt,
     N1,
     QKV,
     PR,
@@ -158,6 +163,7 @@
     loc_sem,
     ca_sem,
     iw_sem,
+    imt_sem,
     tok_sem,
     sb_s,
     sb_r,
@@ -353,6 +359,7 @@
                 (d, partner(k)),
             )
         )
+    imt_copy = local(imt_in, imt, imt_sem)
     for i in range(3):
         load_image(i)
     tok_copy = local(tok_in.at[pl.ds(half * n_cap, n_cap)], TOK, tok_sem)
@@ -383,6 +390,7 @@
         GP[3, pl.ds(at, image_len), :] = (standard(x)[0] * gain_one).astype(LOW)
         return carry
 
+    imt_copy.wait()
     lax.fori_loop(0, images, image_norm, 0)
     for i in range(3):
         image_loads[i].wait()
@@ -534,18 +542,22 @@
     tick(8)
     for copy in sb_copies:
         copy.wait_recv()
-    gather_end(0)
-
-    def project(t, carry):
-        s, j = t // 3, lax.rem(t, 3)
-        weight = W[0, s, pl.ds(pl.multiple_of(shard * j, 16), shard), :]
-        QKV[j, s] = (dot_nt(N1[...], weight) + SB[s, pl.ds(j, 1), 0:shard]).astype(LOW)
-        return carry
+    gather_end(0, (1,))
+
+    def project(near, distant):
+        def one(t, carry):
+            s, j = near + (t // 3) * (distant - near), lax.rem(t, 3)
+            weight = W[0, s, pl.ds(pl.multiple_of(shard * j, 16), shard), :]
+            QKV[j, s] = (dot_nt(N1[...], weight) + SB[s, pl.ds(j, 1), 0:shard]).astype(LOW)
+            return carry
+
+        lax.fori_loop(0, 6, one, 0)
 
     tick(9)
-    lax.fori_loop(0, 6, project, 0)
+    project(m, pair)
     tick(10)
-    lax.fori_loop(6, 3 * n_mp, project, 0)
+    gather_end(0, (2, 3))
+    project(far, far_pair)
     tick(11)
     lane_three = iota((BLOCK, shard), 1) >> 6
 
@@ -629,6 +641,11 @@
     lax.fori_loop(1, 2, feed_near, 0)
     tick(17)
     show_embeds(3)
+    gather_end(2, (1,))
+    PB[0] = (dot(PA[m], W[2, m]) + dot(PA[pair], W[2, pair])).astype(LOW)
+    pooled_copy = remote(PB.at[0], PB.at[1], pb_s, pb_r, (d, far))
+    tick(18)
+
     def pool_residual(n, carry):
         lanes = pl.ds(pl.multiple_of(n * 128, 128), 128)
         res = RES[:, lanes]
@@ -639,10 +656,6 @@
 
     lax.fori_loop(0, width // 128, pool_residual, 0)
     pooled = EL[...] + reduce_bias[...].reshape(1, width)
-    gather_end(2, (1,))
-    PB[0] = (dot(PA[m], W[2, m]) + dot(PA[pair], W[2, pair])).astype(LOW)
-    pooled_copy = remote(PB.at[0], PB.at[1], pb_s, pb_r, (d, far))
-    tick(18)
     pooled_copy.wait_recv()
     pooled += PB[0].astype(F32) + PB[1].astype(F32)
     inverse = lax.rsqrt(jnp.sum(pooled * pooled, axis=-1, keepdims=True) + 1e-6)
@@ -704,7 +717,6 @@
     lax.fori_loop(0, 1, feed_far, 0)
     tick(20)
     lax.fori_loop(1, 2, feed_far, 0)
-    gather_end(2, (2, 3))
     pltpu.make_async_copy(STATS.at[pl.ds(0, 15)], STATS.at[pl.ds(0, 15)], st_r).wait()
     top = jnp.max(STATS[:, 0, :], axis=0, keepdims=True)
     total = jnp.sum(STATS[:, 1, :] * jnp.exp(STATS[:, 0, :] - top), axis=0, keepdims=True)
@@ -803,10 +815,30 @@
             at, got = span(own[ab], 1), RB2[g % 2, i, ab]
         IW[2 * g + i, at, :] = IW[2 * g + i, at, :] + got
 
+    def pass_on(g, ab, k, across_one, across_two, dev):
+        bit_one = axis_one[ab][0] + across_one * (1 - 2 * axis_one[ab][0])
+        bit_two = axis_two[ab][0] + across_two * (1 - 2 * axis_two[ab][0])
+        run = whole(g).at[span(8 * ab + 4 * cb + 2 * bit_one + bit_two, 1)]
+        state[g, "back", k, ab] = remote(run, run, ag_s.at[g, k, ab], ag_r.at[g, k, ab], dev)
+
     def gather_back(g, stage, ab):
-        state[g, "gather", stage, ab] = spread(
-            lambda p, n: whole(g).at[span(p, n)], stage, ab, ag_s.at[g], ag_r.at[g]
-        )
+        dev_one, dev_two = axis_one[ab][1], axis_two[ab][1]
+        if stage == 0:
+            pass_on(g, ab, 0, 0, 0, dev_two)
+            pass_on(g, ab, 1, 0, 0, dev_one)
+            pass_on(g, ab, 2, 0, 0, core_dev)
+        elif stage == 1:
+            state[g, "back", 0, ab].wait_recv()
+            pass_on(g, ab, 3, 0, 1, dev_one)
+            pass_on(g, ab, 4, 0, 1, core_dev)
+        elif stage == 2:
+            state[g, "back", 1, ab].wait_recv()
+            pass_on(g, ab, 5, 1, 0, core_dev)
+            state[g, "back", 3, ab].wait_recv()
+            pass_on(g, ab, 6, 1, 1, core_dev)
+        else:
+            for k in (2, 4, 5, 6):
+                state[g, "back", k, ab].wait_recv()
 
     def reduce_start(g, ab):
         if g == 0:
@@ -814,13 +846,14 @@
         for i in (1, 0):
             scatter(g, 0, i, ab)
 
-    def reduce_step(g, step):
+    def reduce_step(g, step, half_of=None):
         if step == 0:
             for ab in range(2):
                 reduce_start(g, ab)
         elif step < 4:
+            halves = (half_of,) if half_of is not None else (0, 1)
             for i in (1, 0):
-                for ab in range(2):
+                for ab in halves:
                     add_in(g, step - 1, i, ab)
                     if step < 3 or i == 1:
                         scatter(g, step, i, ab)
@@ -843,16 +876,15 @@
                 gather_back(g, 0, ab)
         elif step < 7:
             for ab in range(2):
-                state[g, "gather", step - 5, ab].wait_recv()
                 gather_back(g, step - 4, ab)
         else:
             for ab in range(2):
-                state[g, "gather", 2, ab].wait_recv()
+                gather_back(g, 3, ab)
             stores.append(local(whole(g), red.at[g], out_sem.at[g]))
 
     def back_tick(place):
-        for g, step in RPLAN.get(place, ()):
-            reduce_step(g, step)
+        for entry in RPLAN.get(place, ()):
+            reduce_step(*entry)
 
     shards = (m, pair)
     for i in range(2):
@@ -860,28 +892,33 @@
 
     back_tick(0)
 
-    def grad_activation(s, carry):
-        GA[s] = dot_nt(GPL[1], W[2, s])
-        return carry
-
-    lax.fori_loop(0, n_mp, grad_activation, 0)
+    def grad_activation(near, distant):
+        for s in (near, distant):
+            GA[s] = dot_nt(GPL[1], W[2, s])
+
+    ones = jnp.ones((16, rows), LOW)
+
+    def grad_hidden(near, distant):
+        def one(k, carry):
+            s = near + k * (distant - near)
+
+            def scale(t, inner):
+                at = pl.ds(pl.multiple_of(t * LEN, LEN), LEN)
+                GP[s, at, :] = (GP[s, at, :].astype(F32) * GA[s, pl.ds(t, 1), :]).astype(LOW)
+                return inner
+
+            lax.fori_loop(0, n_cap, scale, 0, unroll=7)
+            SG[0, pl.ds(8 + s, 1), :] = dot(ones, GP[s])[0:1]
+            return carry
+
+        lax.fori_loop(0, 2, one, 0)
+
+    grad_activation(m, pair)
     back_tick(1)
-    ones = jnp.ones((16, rows), LOW)
-
-    def grad_hidden(s, carry):
-        def scale(t, inner):
-            at = pl.ds(pl.multiple_of(t * LEN, LEN), LEN)
-            GP[s, at, :] = (GP[s, at, :].astype(F32) * GA[s, pl.ds(t, 1), :]).astype(LOW)
-            return inner
-
-        lax.fori_loop(0, n_cap, scale, 0, unroll=7)
-        SG[0, pl.ds(8 + s, 1), :] = dot(ones, GP[s])[0:1]
-        return carry
-
-    lax.fori_loop(0, 2, grad_hidden, 0)
+    tick(21)
+    grad_hidden(m, pair)
     back_tick(2)
-    lax.fori_loop(2, n_mp, grad_hidden, 0)
-    back_tick(3)
+    tick(22)
 
     def expand_gradient(i, carry):
         s = m + i * (pair - m)
@@ -890,6 +927,12 @@
 
     lax.fori_loop(0, 2, expand_gradient, 0)
     back_tick(4)
+    tick(23)
+    gather_end(2, (2, 3))
+    grad_activation(far, far_pair)
+    back_tick(3)
+    grad_hidden(far, far_pair)
+    back_tick(5)
 
     def grad_norm_two(n, carry):
         p = pl.ds(pl.multiple_of(n * 384, 128), 384)
@@ -900,9 +943,7 @@
         ACC[:, pl.ds(pl.multiple_of(n * 384, 128), 384)] = total
         return carry
 
-    lax.fori_loop(0, 1, grad_norm_two, 0)
-    back_tick(5)
-    lax.fori_loop(1, 2, grad_norm_two, 0)
+    lax.fori_loop(0, 2, grad_norm_two, 0)
     back_tick(6)
 
     def norm_back(e, gain, x):
@@ -944,11 +985,11 @@
     lax.fori_loop(0, n_mp, grad_mixture, 0)
     back_tick(8)
 
-    def attention_back(b, carry):
-        at = pl.ds(pl.multiple_of(b * BLOCK, 16), BLOCK)
-        loaded = [
-            [QKV[j, s, at, :] for j in range(3)] + [MIX[s, at, :], PR[s, b]] for s in range(n_mp)
-        ]
+    def attention_back(places):
+        loaded = []
+        for b, s in places:
+            at = pl.ds(pl.multiple_of(b * BLOCK, 16), BLOCK)
+            loaded.append([QKV[j, s, at, :] for j in range(3)] + [MIX[s, at, :], PR[s, b]])
         heads = HM3[...]
         every = []
         for q, k, v, g, low_probs in loaded:
@@ -965,10 +1006,20 @@
                     dot(low_probs, g).astype(LOW),
                 )
             )
-        for s, grads in enumerate(every):
+        for (b, s), grads in zip(places, every):
+            at = pl.ds(pl.multiple_of(b * BLOCK, 16), BLOCK)
             for j in range(3):
                 QKV[j, s, at, :] = grads[j]
-        return carry
+
+    def attention_back_run(first, count, shards):
+        def two(t, carry):
+            b = first + 2 * t
+            attention_back([(b + x, s) for x in range(2) for s in shards])
+            return carry
+
+        lax.fori_loop(0, count // 2, two, 0)
+        if count % 2:
+            attention_back([(first + count - 1, s) for s in shards])
 
     def attend_gradient(j):
         def one(i, carry):
@@ -978,19 +1029,30 @@
 
         lax.fori_loop(0, 2, one, 0)
 
+    small_devs = [core_dev, y_dev, x_dev, pair_dev] + [(flip(d, 3 + x), m) for x in range(extra)]
+    small = {}
+
+    def small_start(i):
+        small[i] = remote(SG.at[i], SGR.at[i], sg_s.at[i], sg_r.at[i], small_devs[i])
+
+    def small_end(i):
+        small[i].wait_recv()
+        SG[i + 1] = SG[i] + SGR[i]
+
     small_gain, small_shift = zero8, zero8
     gt_copies = []
-    cuts = (0, 3, 5, n_blocks)
-    for r in range(3):
-        lax.fori_loop(cuts[r], cuts[r + 1], attention_back, 0)
-        back_tick(9 + r)
-        if r == 2:
-            attend_gradient(2)
-            reduce_start(0, 1)
-            attend_gradient(0)
-            attend_gradient(1)
-            reduce_start(0, 0)
-            back_tick(20)
+    cuts = (0, 4, n_blocks)
+    attention_back_run(0, n_blocks, (m, pair))
+    back_tick(9)
+    attend_gradient(2)
+    reduce_start(0, 1)
+    attend_gradient(0)
+    attend_gradient(1)
+    reduce_start(0, 0)
+    back_tick(20)
+    for r in range(2):
+        attention_back_run(cuts[r], cuts[r + 1] - cuts[r], (far, far_pair))
+        back_tick(10 + r)
         first, last = cuts[r] * (BLOCK // LEN), cuts[r + 1] * (BLOCK // LEN)
         stripe = pl.ds(first * LEN, (last - first) * LEN)
 
@@ -1018,48 +1080,39 @@
         small_gain, small_shift = lax.fori_loop(
             first, last, back_one, (small_gain, small_shift), unroll=7
         )
-        back_tick(15 + r)
+        if r == 1:
+            SG[0, 14:15, :] = jnp.sum(small_gain, axis=0, keepdims=True)
+            SG[0, 16:17, :] = jnp.sum(small_shift, axis=0, keepdims=True)
+
+            def bias_gradient(s, carry):
+                SG[0, pl.ds(s, 1), 0:shard] = dot(ones, QKV[0, s])[0:1]
+                SG[0, pl.ds(4 + s, 1), 0:shard] = dot(ones, QKV[2, s])[0:1]
+                return carry
+
+            lax.fori_loop(0, n_mp, bias_gradient, 0)
+            small_start(0)
+            back_tick(16)
+            small_end(0)
+            small_start(1)
+            back_tick(17)
+            small_end(1)
+            small_start(2)
+            back_tick(18)
+            small_end(2)
+            small_start(3)
+        else:
+            back_tick(15)
         gt_copies.append(
             remote(GT.at[stripe], gt.at[half, stripe], gt_s.at[r], gt_r.at[r], pair_dev)
         )
+    stores.append(local(GT, gt.at[half], out_sem.at[3]))
     back_tick(21)
-    stores.append(local(GT, gt.at[half], out_sem.at[3]))
-    SG[0, 14:15, :] = jnp.sum(small_gain, axis=0, keepdims=True)
-    SG[0, 16:17, :] = jnp.sum(small_shift, axis=0, keepdims=True)
-
-    def bias_gradient(s, carry):
-        SG[0, pl.ds(s, 1), 0:shard] = dot(ones, QKV[0, s])[0:1]
-        SG[0, pl.ds(4 + s, 1), 0:shard] = dot(ones, QKV[2, s])[0:1]
-        return carry
-
-    lax.fori_loop(0, n_mp, bias_gradient, 0)
-    small_devs = [core_dev, y_dev, x_dev, pair_dev] + [(flip(d, 3 + x), m) for x in range(extra)]
-    small = {}
-
-    def small_start(i):
-        small[i] = remote(SG.at[i], SGR.at[i], sg_s.at[i], sg_r.at[i], small_devs[i])
-
-    def small_end(i):
-        small[i].wait_recv()
-        SG[i + 1] = SG[i] + SGR[i]
-
-    back_tick(22)
-    small_start(0)
-    back_tick(23)
-    small_end(0)
-    small_start(1)
-    back_tick(24)
-    small_end(1)
-    small_start(2)
-    back_tick(25)
-    small_end(2)
-    small_start(3)
-    back_tick(26)
     small_end(3)
     for i in range(4, 4 + extra):
         small_start(i)
         small_end(i)
-    back_tick(27)
+    for place in range(22, 28):
+        back_tick(place)
     last = SG.shape[0] - 1
     sgo[...] = jnp.zeros_like(sgo)
     sgo[0:1, :] = SG[last, pl.ds(m, 1), :]
@@ -1120,6 +1173,7 @@
         pltpu.VMEM((3, n_mp, width, width), LOW),
         pltpu.VMEM((8, width, width), LOW),
         pltpu.VMEM((n_cap, length, width), LOW),
+        pltpu.VMEM((images, image_len, width), LOW),
         pltpu.VMEM((rows, width), LOW),
         pltpu.VMEM((3, n_mp, rows, shard), LOW),
         pltpu.VMEM((n_mp, n_blocks, BLOCK, 3 * BLOCK), LOW),
@@ -1161,6 +1215,7 @@
         dma((3,)),
         dma((12,)),
         dma,
+        dma,
         dma((3,)),
         dma((3,)),
         dma((10 + nx,)),
@@ -1171,8 +1226,8 @@
         dma((nx,)),
         dma((3, 4, 4)),
         dma((3, 4, 4)),
-        dma((3, 3, 2)),
-        dma((3, 3, 2)),
+        dma((3, 7, 2)),
+        dma((3, 7, 2)),
         dma((3, nx, 2)),
         dma((3, nx, 2)),
         dma((4 + extra,)),
@@ -1190,7 +1245,7 @@
             jax.ShapeDtypeStruct((2, rows, width), LOW),
             jax.ShapeDtypeStruct((16, width), F32),
         ),
-        in_specs=[any_space, vmem] + [any_space] * 8 + [vmem] * 9,
+        in_specs=[any_space] * 10 + [vmem] * 9,
         out_specs=(any_space, any_space, vmem),
         scratch_shapes=scratch,
         compiler_params=pltpu.CompilerParams(

time: 171 us -> 165 us (0.965)
  Pallas kernels: 168 us -> 163 us
    pallas_call x1, Pallas kernels: 160 us -> 155 us  [local_step(): pl.pallas_call(functools.partial(body, n_dp, n_mp), out_shape=(jax.ShapeD...]
where the time goes in v6:
time: 165 us; the launch traced here: 164 us
  Pallas kernels  163 us (99%)
    pallas_call x1, Pallas kernels, local_step(): pl.pallas_call(functools.partial(body, n_dp, n_mp), out_shape=(jax.ShapeD...  155 us
    pallas_call x1, Pallas kernels, local_step(): pl.pallas_call(finish, out_shape=tuple((jax.ShapeDtypeStruct(shape, F32)...  7.71 us

profile of v6, /device:TPU:0, one launch (start us, length us, event | category | flops | bytes accessed | tf_op | source)
XLA Modules:
  0.0 164.4 jit_solution(14767712347984810694)
XLA Ops:
  1.3 155.2 %step.1 = (bf16[3,768,768]{2,1,0:T(8,128)(2,1)}, bf16[2,784,768]{2,1,0:T(8,128)(2,1)}, f32[16,768]{1,0:T(8,128)}) custom-call(bf16[98,16,768]{2,1,0:T(8,128)(2,1)} %tok_in.1, bf16[7,50,768]{2,1,0:T(8,128)(2,1)} %imt_in.1, bf16[3,768,768]{2,1,0:T(8,128)(2,1)} %ia_in.1, bf16[768,768]{1,0:T(8,128)(2,1)} %io_in.1, bf16[768,3072]{1,0:T(8,128)(2,1)} %ie_in.1, ...), custom_call_target="tpu_custom_call" | custom-call | tf_op jit(solution)/shard_map/step/pallas_call | solution.py:1241
  156.5 7.7 %finish.1 = (f32[1]{0:T(128)}, f32[98,16,768]{2,1,0:T(8,128)}, f32[3,192,768]{2,1,0:T(8,128)}, f32[2,192]{1,0:T(2,128)}, f32[192,768]{1,0:T(8,128)}, /*index=5*/...) custom-call(bf16[3,768,768]{2,1,0:T(8,128)(2,1)} %get-tuple-element., ...), custom_call_target="tpu_custom_call" | custom-call | tf_op jit(solution)/shard_map/finish/pallas_call | solution.py:1293

commit v7 on v6

--- a/solution.py
+++ b/solution.py
@@ -15,6 +15,7 @@
 LOW = jnp.bfloat16
 FAR = -1e30
 ALL_HOPS = (1, 2, 3)
+TILES = 7
 RPLAN = {
     0: ((2, 0),),
     2: ((2, 1),),
@@ -84,10 +85,9 @@
 
 def gelu_parts(h):
     square = h * h
-    t = jnp.tanh(GELU_A * h * (1.0 + GELU_B * square))
-    half = 0.5 * (1.0 + t)
-    slope = half + 0.5 * h * (1.0 - t * t) * (GELU_A * (1.0 + 3.0 * GELU_B * square))
-    return h * half, slope
+    p = 0.5 + 0.5 * jnp.tanh(h * (GELU_A + GELU_A * GELU_B * square))
+    inner = h * (2.0 * GELU_A + 6.0 * GELU_A * GELU_B * square)
+    return h * p, p * (1.0 + inner * (1.0 - p))
 
 
 def sum8(x):
@@ -470,7 +470,7 @@
         def activate(t, inner):
             at = pl.ds(pl.multiple_of(t * 16, 16), 16)
             h = ACC[at, :]
-            act = 0.5 * h * (1.0 + jnp.tanh(GELU_A * h * (1.0 + GELU_B * h * h)))
+            act = h * (0.5 + 0.5 * jnp.tanh(h * (GELU_A + GELU_A * GELU_B * (h * h))))
             N2[at, :] = act.astype(LOW)
             return inner
 
@@ -614,17 +614,20 @@
     gather_end(1, (1,))
 
     def feed_one(s):
-        ACC[...] = dot(N2[...], W[1, s])
         bias = SB[s, 3:4, :]
 
-        def activate(t, inner):
-            at = pl.ds(pl.multiple_of(t * LEN, LEN), LEN)
-            act, slope = gelu_parts(ACC[at, :] + bias)
-            GT[at, :] = act.astype(LOW)
-            GP[s, at, :] = slope.astype(LOW)
-            return inner
-
-        lax.fori_loop(0, n_cap, activate, 0, unroll=7)
+        def tiles(t, carry):
+            for x in range(TILES):
+                first = pl.multiple_of((TILES * t + x) * BLOCK, 16)
+                h = dot(N2[pl.ds(first, BLOCK), :], W[1, s])
+                for u in range(BLOCK // LEN):
+                    at = pl.ds(first + u * LEN, LEN)
+                    act, slope = gelu_parts(h[u * LEN : (u + 1) * LEN] + bias)
+                    GT[at, :] = act.astype(LOW)
+                    GP[s, at, :] = slope.astype(LOW)
+            return carry
+
+        lax.fori_loop(0, n_blocks // TILES, tiles, 0)
         PA[s] = (dot(POOL[...], GT[...]) * (1.0 / LEN)).astype(LOW)
 
     def feed_near(i, carry):

time: 165 us -> 161 us (0.976)
  Pallas kernels: 163 us -> 159 us
    pallas_call x1, Pallas kernels: 155 us -> 151 us  [local_step(): pl.pallas_call(functools.partial(body, n_dp, n_mp), out_shape=(jax.ShapeD...]
where the time goes in v7:
time: 161 us; the launch traced here: 160 us
  Pallas kernels  159 us (99%)
    pallas_call x1, Pallas kernels, local_step(): pl.pallas_call(functools.partial(body, n_dp, n_mp), out_shape=(jax.ShapeD...  151 us
    pallas_call x1, Pallas kernels, local_step(): pl.pallas_call(finish, out_shape=tuple((jax.ShapeDtypeStruct(shape, F32)...  7.71 us

profile of v7, /device:TPU:0, one launch (start us, length us, event | category | flops | bytes accessed | tf_op | source)
XLA Modules:
  0.0 160.3 jit_solution(8358085361038295983)
XLA Ops:
  1.3 151.1 %step.1 = (bf16[3,768,768]{2,1,0:T(8,128)(2,1)}, bf16[2,784,768]{2,1,0:T(8,128)(2,1)}, f32[16,768]{1,0:T(8,128)}) custom-call(bf16[98,16,768]{2,1,0:T(8,128)(2,1)} %tok_in.1, bf16[7,50,768]{2,1,0:T(8,128)(2,1)} %imt_in.1, bf16[3,768,768]{2,1,0:T(8,128)(2,1)} %ia_in.1, bf16[768,768]{1,0:T(8,128)(2,1)} %io_in.1, bf16[768,3072]{1,0:T(8,128)(2,1)} %ie_in.1, ...), custom_call_target="tpu_custom_call" | custom-call | tf_op jit(solution)/shard_map/step/pallas_call | solution.py:1244
  152.4 7.7 %finish.1 = (f32[1]{0:T(128)}, f32[98,16,768]{2,1,0:T(8,128)}, f32[3,192,768]{2,1,0:T(8,128)}, f32[2,192]{1,0:T(2,128)}, f32[192,768]{1,0:T(8,128)}, /*index=5*/...) custom-call(bf16[3,768,768]{2,1,0:T(8,128)(2,1)} %get-tuple-element., ...), custom_call_target="tpu_custom_call" | custom-call | tf_op jit(solution)/shard_map/finish/pallas_call | solution.py:1296

commit v8 on v7

--- a/solution.py
+++ b/solution.py
@@ -590,25 +590,22 @@
     lax.fori_loop(4, n_blocks, attention, 0)
     tick(14)
 
-    def attend_out(n, carry):
-        lanes = pl.ds(pl.multiple_of(n * 256, 256), 256)
-        total = dot(MIX[0], W[0, 0, pl.ds(3 * shard, shard), lanes])
+    out_bias = output_bias[...].reshape(1, width)
+
+    def attend_out(t, carry):
+        start = pl.multiple_of(t * BLOCK, 16)
+        rows_here = pl.ds(start, BLOCK)
+        total = dot(MIX[0, rows_here, :], W[0, 0, pl.ds(3 * shard, shard), :])
         for s in range(1, n_mp):
-            total += dot(MIX[s], W[0, s, pl.ds(3 * shard, shard), lanes])
-        ACC[:, lanes] = total
-        return carry
-
-    lax.fori_loop(0, width // 256, attend_out, 0)
-    out_bias = output_bias[...].reshape(1, width)
-
-    def norm_two(t, carry):
-        at = pl.ds(pl.multiple_of(t * LEN, LEN), LEN)
-        x = TOK[t].astype(F32) + (ACC[at, :] + out_bias)
-        RES[at, :] = x
-        N2[at, :] = (standard(x)[0] * g2 + b2).astype(LOW)
-        return carry
-
-    lax.fori_loop(0, n_cap, norm_two, 0, unroll=7)
+            total += dot(MIX[s, rows_here, :], W[0, s, pl.ds(3 * shard, shard), :])
+        for u in range(BLOCK // LEN):
+            at = pl.ds(start + u * LEN, LEN)
+            x = TOK[7 * t + u].astype(F32) + (total[u * LEN : (u + 1) * LEN] + out_bias)
+            RES[at, :] = x
+            N2[at, :] = (standard(x)[0] * g2 + b2).astype(LOW)
+        return carry
+
+    lax.fori_loop(0, n_blocks, attend_out, 0, unroll=True)
     tick(15)
     show_embeds(1)
     gather_end(1, (1,))
@@ -1059,30 +1056,28 @@
         first, last = cuts[r] * (BLOCK // LEN), cuts[r + 1] * (BLOCK // LEN)
         stripe = pl.ds(first * LEN, (last - first) * LEN)
 
-        def grad_norm_one(n, carry):
-            lanes = pl.ds(pl.multiple_of(n * 256, 256), 256)
-            total = None
+        def last_norm(t, carry):
+            dg, db = carry
+            start = pl.multiple_of((first + 7 * t) * LEN, 16)
+            rows_here = pl.ds(start, BLOCK)
+            e = None
             for s in range(n_mp):
                 for j in range(3):
-                    term = dot(
-                        QKV[j, s, stripe, :],
-                        W[0, s, pl.ds(shard * j, shard), lanes],
-                    )
-                    total = term if total is None else total + term
-            ACC[stripe, lanes] = total
-            return carry
-
-        lax.fori_loop(0, width // 256, grad_norm_one, 0)
+                    term = dot(QKV[j, s, rows_here, :], W[0, s, pl.ds(shard * j, shard), :])
+                    e = term if e is None else e + term
+            for u in range(BLOCK // LEN):
+                at = pl.ds(start + u * LEN, LEN)
+                dv, one, two = norm_back(
+                    e[u * LEN : (u + 1) * LEN], g1, TOK[first + 7 * t + u].astype(F32)
+                )
+                GT[at, :] = (RES[at, :] + dv).astype(LOW)
+                dg, db = dg + one, db + two
+            return dg, db
+
+        small_gain, small_shift = lax.fori_loop(
+            0, (last - first) // 7, last_norm, (small_gain, small_shift)
+        )
         back_tick(12 + r)
-        def back_one(t, carry):
-            at = pl.ds(pl.multiple_of(t * LEN, LEN), LEN)
-            dv, dg, db = norm_back(ACC[at, :], g1, TOK[t].astype(F32))
-            GT[at, :] = (RES[at, :] + dv).astype(LOW)
-            return carry[0] + dg, carry[1] + db
-
-        small_gain, small_shift = lax.fori_loop(
-            first, last, back_one, (small_gain, small_shift), unroll=7
-        )
         if r == 1:
             SG[0, 14:15, :] = jnp.sum(small_gain, axis=0, keepdims=True)
             SG[0, 16:17, :] = jnp.sum(small_shift, axis=0, keepdims=True)

time: 161 us -> 160 us (level)
  no operation moved by 1% of the time
where the time goes in v8:
time: 160 us; the launch traced here: 159 us
  Pallas kernels  158 us (99%)
    pallas_call x1, Pallas kernels, local_step(): pl.pallas_call(functools.partial(body, n_dp, n_mp), out_shape=(jax.ShapeD...  150 us
    pallas_call x1, Pallas kernels, local_step(): pl.pallas_call(finish, out_shape=tuple((jax.ShapeDtypeStruct(shape, F32)...  7.71 us

profile of v8, /device:TPU:0, one launch (start us, length us, event | category | flops | bytes accessed | tf_op | source)
XLA Modules:
  0.0 159.5 jit_solution(15942105174324158598)
XLA Ops:
  1.3 150.3 %step.1 = (bf16[3,768,768]{2,1,0:T(8,128)(2,1)}, bf16[2,784,768]{2,1,0:T(8,128)(2,1)}, f32[16,768]{1,0:T(8,128)}) custom-call(bf16[98,16,768]{2,1,0:T(8,128)(2,1)} %tok_in.1, bf16[7,50,768]{2,1,0:T(8,128)(2,1)} %imt_in.1, bf16[3,768,768]{2,1,0:T(8,128)(2,1)} %ia_in.1, bf16[768,768]{1,0:T(8,128)(2,1)} %io_in.1, bf16[768,3072]{1,0:T(8,128)(2,1)} %ie_in.1, ...), custom_call_target="tpu_custom_call" | custom-call | tf_op jit(solution)/shard_map/step/pallas_call | solution.py:1239
  151.6 7.7 %finish.1 = (f32[1]{0:T(128)}, f32[98,16,768]{2,1,0:T(8,128)}, f32[3,192,768]{2,1,0:T(8,128)}, f32[2,192]{1,0:T(2,128)}, f32[192,768]{1,0:T(8,128)}, /*index=5*/...) custom-call(bf16[3,768,768]{2,1,0:T(8,128)(2,1)} %get-tuple-element., ...), custom_call_target="tpu_custom_call" | custom-call | tf_op jit(solution)/shard_map/finish/pallas_call | solution.py:1291

commit v9 on v8

--- a/solution.py
+++ b/solution.py
@@ -902,13 +902,16 @@
         def one(k, carry):
             s = near + k * (distant - near)
 
-            def scale(t, inner):
-                at = pl.ds(pl.multiple_of(t * LEN, LEN), LEN)
-                GP[s, at, :] = (GP[s, at, :].astype(F32) * GA[s, pl.ds(t, 1), :]).astype(LOW)
-                return inner
-
-            lax.fori_loop(0, n_cap, scale, 0, unroll=7)
-            SG[0, pl.ds(8 + s, 1), :] = dot(ones, GP[s])[0:1]
+            def scale(t, total):
+                for u in range(7):
+                    at = pl.ds(pl.multiple_of((7 * t + u) * LEN, LEN), LEN)
+                    low_grad = (GP[s, at, :].astype(F32) * GA[s, pl.ds(7 * t + u, 1), :]).astype(LOW)
+                    GP[s, at, :] = low_grad
+                    total = total + sum8(low_grad.astype(F32))
+                return total
+
+            total = lax.fori_loop(0, n_cap // 7, scale, jnp.zeros((8, width), F32))
+            SG[0, pl.ds(8 + s, 1), :] = jnp.sum(total, axis=0, keepdims=True)
             return carry
 
         lax.fori_loop(0, 2, one, 0)

time: 160 us -> 161 us (level)
  no operation moved by 1% of the time
where the time goes in v9:
time: 161 us; the launch traced here: 160 us
  Pallas kernels  159 us (99%)
    pallas_call x1, Pallas kernels, local_step(): pl.pallas_call(functools.partial(body, n_dp, n_mp), out_shape=(jax.ShapeD...  151 us
    pallas_call x1, Pallas kernels, local_step(): pl.pallas_call(finish, out_shape=tuple((jax.ShapeDtypeStruct(shape, F32)...  7.71 us

profile of v9, /device:TPU:0, one launch (start us, length us, event | category | flops | bytes accessed | tf_op | source)
XLA Modules:
  0.0 160.4 jit_solution(17930369999267684334)
XLA Ops:
  1.3 151.2 %step.1 = (bf16[3,768,768]{2,1,0:T(8,128)(2,1)}, bf16[2,784,768]{2,1,0:T(8,128)(2,1)}, f32[16,768]{1,0:T(8,128)}) custom-call(bf16[98,16,768]{2,1,0:T(8,128)(2,1)} %tok_in.1, bf16[7,50,768]{2,1,0:T(8,128)(2,1)} %imt_in.1, bf16[3,768,768]{2,1,0:T(8,128)(2,1)} %ia_in.1, bf16[768,768]{1,0:T(8,128)(2,1)} %io_in.1, bf16[768,3072]{1,0:T(8,128)(2,1)} %ie_in.1, ...), custom_call_target="tpu_custom_call" | custom-call | tf_op jit(solution)/shard_map/step/pallas_call | solution.py:1242
  152.5 7.7 %finish.1 = (f32[1]{0:T(128)}, f32[98,16,768]{2,1,0:T(8,128)}, f32[3,192,768]{2,1,0:T(8,128)}, f32[2,192]{1,0:T(2,128)}, f32[192,768]{1,0:T(8,128)}, /*index=5*/...) custom-call(bf16[3,768,768]{2,1,0:T(8,128)(2,1)} %get-tuple-element., ...), custom_call_target="tpu_custom_call" | custom-call | tf_op jit(solution)/shard_map/finish/pallas_call | solution.py:1294
